TPU v7x, 128 devices: a whole 4x4x4 slice. The times are simulated.
128 devices in a mesh: lo: 16 (over z, y), hi: 8 (over x, core).
Axes of the slice: x: 4, y: 4, z: 4, core: 2. Of those that a mesh axis runs over, the one named last changes fastest.
Arguments:
- contribution: float32 [8, 16, 1024, 1024], P('hi', 'lo'), as said below
- pivot_one: float32 [8, 16, 384, 768], P('hi', 'lo'), as said below
- rows_one: float32 [8, 16, 768, 2304], P('hi', 'lo'), as said below
- pivot_two: float32 [8, 16, 192, 768], P('hi', 'lo'), as said below
- rows_two: float32 [8, 16, 384, 2304], P('hi', 'lo'), as said below
- map_one: int32 [8, 16, 8], replicated, may hold values from 0 to 17, as said below
- map_two: int32 [8, 8, 12], replicated, may hold values from 0 to 17, as said below
- fill_one: int32 [8, 8, 12, 6], replicated, may hold values 0 or 1
- fill_two: int32 [4, 8, 12, 6], replicated, may hold values 0 or 1
- live_one: int32 [8, 8], replicated, may hold values from 3 to 6, as said below
- live_two: int32 [4, 8], replicated, may hold values from 3 to 6, as said below
Outputs:
- lower_one: float32 [8, 16, 384, 768], P('hi', 'lo')
- panel_one: float32 [8, 16, 768, 768], P('hi', 'lo')
- lower_two: float32 [8, 16, 192, 768], P('hi', 'lo')
- panel_two: float32 [8, 16, 384, 768], P('hi', 'lo')
- schur_two: float32 [8, 16, 384, 1536], P('hi', 'lo')
Inputs may be any that keep to these rules, and one draw needn't show every extreme that they name: `contribution`: symmetric and negative semidefinite: minus a Gram matrix, divided by 1024. `pivot_one`: with rows_one, the rows of a symmetric matrix of each front with a dominant diagonal. `rows_one`: with pivot_one, the rows of a symmetric matrix of each front with a dominant diagonal. `pivot_two`: with rows_two, the rows of a symmetric matrix of each front with a dominant diagonal. `rows_two`: with pivot_two, the rows of a symmetric matrix of each front with a dominant diagonal. `map_one`: each device's list names 8 distinct tiles. `map_two`: each front's list names 12 distinct tiles. `live_one`: both ends reached in every draw. `live_two`: both ends reached in every draw.
All inputs are finite; a program needn't handle non-finite values.
Results may differ from a plain program's by a relative error of at most 0.0003.
Values sent between devices are 32-bit elements; how exact they have to be, the bound alone decides.
A program may use at most 192 MiB of HBM per device.

v0:
```python
import jax
import jax.numpy as jnp
from jax import lax
from jax.sharding import PartitionSpec as P

TILE = 128
P1T = 6
U1T = 12
P2T = 6
U2T = 12


HIGHEST_MODE = lax.Precision.HIGHEST


def partner(array, axis, apart):
    return lax.ppermute(array, axis, [(i, i ^ 1 << apart) for i in range(lax.axis_size(axis))])


def spread(source_block, row_map, col_map, row_first, row_tiles, col_tiles):
    row_count = row_map.shape[0]
    col_count = col_map.shape[0]
    tile_size = source_block.shape[1] // col_count
    targets = row_first + jnp.arange(row_tiles, dtype=jnp.int32)
    row_onehot = (row_map[:, None] == targets[None, :]).astype(jnp.float32)
    col_onehot = (col_map[:, None] == jnp.arange(col_tiles, dtype=jnp.int32)[None, :]).astype(
        jnp.float32
    )
    blocks = source_block.reshape(row_count, tile_size, col_count, tile_size)
    placed = jnp.einsum("ia,ixky->axky", row_onehot, blocks, precision=HIGHEST_MODE)
    placed = jnp.einsum("axky,kb->axby", placed, col_onehot, precision=HIGHEST_MODE)
    return placed.reshape(row_tiles * tile_size, col_tiles * tile_size)


def factor(pivot_block, coupling, live_tiles):
    kept = (jnp.arange(pivot_block.shape[0]) // TILE < live_tiles).astype(pivot_block.dtype)
    pivot_block = pivot_block * kept[:, None] * kept[None, :] + jnp.diag(1.0 - kept)
    coupling = coupling * kept[None, :]
    factor_lower = jnp.linalg.cholesky(pivot_block)
    panel_part = lax.linalg.triangular_solve(
        factor_lower, coupling, left_side=False, lower=True, transpose_a=True
    )
    return (factor_lower, panel_part)


def expand_fill(fill_tiles):
    return jnp.repeat(jnp.repeat(fill_tiles, TILE, axis=0), TILE, axis=1).astype(jnp.float32)


def across_lo(values_in):
    return partner(values_in, "lo", lax.axis_size("lo").bit_length() - 2)


def across_hi(values_in):
    return partner(values_in, "hi", lax.axis_size("hi").bit_length() - 2)


def ordered(mine, theirs, which_side):
    first_half = jnp.where(which_side == 0, mine, theirs)
    second_half = jnp.where(which_side == 0, theirs, mine)
    return jnp.concatenate([first_half, second_half], axis=0)


def body(
    contribution,
    pivot_one,
    rows_one,
    pivot_two,
    rows_two,
    map_one,
    map_two,
    fill_one,
    fill_two,
    live_one,
    live_two,
):
    size_lo = lax.axis_size("lo")
    size_hi = lax.axis_size("hi")
    half_lo = size_lo // 2
    half_hi = size_hi // 2
    index_lo = lax.axis_index("lo")
    index_hi = lax.axis_index("hi")
    side_lo = index_lo // half_lo
    side_hi = index_hi // half_hi
    front_lo = index_lo % half_lo
    front_hi = index_hi % half_hi
    pivot_size = P1T * TILE
    half_tiles = U1T // 2
    own_block = contribution[0, 0]
    own_map = map_one[index_hi, index_lo]
    own_pivot = pivot_one[0, 0]
    fill_tiles = lax.dynamic_slice_in_dim(
        fill_one[index_hi, front_lo], side_lo * half_tiles, half_tiles, 0
    )
    own_rows = rows_one[0, 0]
    own_rows = jnp.concatenate(
        [own_rows[:, :pivot_size] * expand_fill(fill_tiles), own_rows[:, pivot_size:]], axis=1
    )
    own_start = P1T + side_lo * half_tiles
    placed_pivot = lax.dynamic_update_slice(
        jnp.zeros((pivot_size, pivot_size), jnp.float32),
        own_pivot,
        (side_lo * (pivot_size // 2), 0),
    )
    other_block, other_pivot = partner((own_block, own_pivot), "lo", size_lo.bit_length() - 2)
    other_map = map_one[index_hi, (index_lo + half_lo) % size_lo]
    placed_pivot = lax.dynamic_update_slice(
        placed_pivot, other_pivot, ((1 - side_lo) * (pivot_size // 2), 0)
    )
    pivot_block = (
        placed_pivot
        + spread(own_block, own_map, own_map, 0, P1T, P1T)
        + spread(other_block, other_map, other_map, 0, P1T, P1T)
    )
    front_rows = (
        own_rows
        + spread(own_block, own_map, own_map, own_start, half_tiles, P1T + U1T)
        + spread(other_block, other_map, other_map, own_start, half_tiles, P1T + U1T)
    )
    factor_lower, panel_part = factor(
        pivot_block, front_rows[:, :pivot_size], live_one[index_hi, front_lo]
    )
    full_panel = ordered(panel_part, across_lo(panel_part), side_lo)
    schur_rows = front_rows[:, pivot_size:] - jnp.dot(
        panel_part, full_panel.T, precision=HIGHEST_MODE
    )
    lower_one = lax.dynamic_slice_in_dim(
        factor_lower, side_lo * (pivot_size // 2), pivot_size // 2, 0
    )
    second_size = P2T * TILE
    quarter_tiles = U2T // 4
    quarter_rows = quarter_tiles * TILE
    quarter_pivot = second_size // 4
    second_width = (P2T + U2T) * TILE
    quarter = 2 * side_hi + side_lo
    second_map = map_two[index_hi, front_lo]
    row_map = lax.dynamic_slice_in_dim(second_map, side_lo * half_tiles, half_tiles, 0)
    pivot_part = lax.dynamic_update_slice(
        jnp.zeros((second_size, second_size), jnp.float32),
        pivot_two[0, 0],
        (quarter * quarter_pivot, 0),
    )
    pivot_part = pivot_part + spread(schur_rows, row_map, second_map, 0, P2T, P2T)
    part_rows = spread(schur_rows, row_map, second_map, P2T, U2T, P2T + U2T)
    grouped = part_rows.reshape(2, 2 * quarter_rows, second_width)
    got_pivot, got_rows = across_hi((pivot_part, grouped[1 - side_hi]))
    pivot_part = pivot_part + got_pivot
    kept_rows = (grouped[side_hi] + got_rows).reshape(2, quarter_rows, second_width)
    got_pivot, got_rows = across_lo((pivot_part, kept_rows[1 - side_lo]))
    second_pivot = pivot_part + got_pivot
    quarter_part = kept_rows[side_lo] + got_rows
    fill_second = lax.dynamic_slice_in_dim(
        fill_two[front_hi, front_lo], quarter * quarter_tiles, quarter_tiles, 0
    )
    own_second = rows_two[0, 0]
    quarter_part = quarter_part + jnp.concatenate(
        [own_second[:, :second_size] * expand_fill(fill_second), own_second[:, second_size:]],
        axis=1,
    )
    lower_full, panel_two = factor(
        second_pivot, quarter_part[:, :second_size], live_two[front_hi, front_lo]
    )
    pair_panel = ordered(panel_two, across_lo(panel_two), side_lo)
    all_panel = ordered(pair_panel, across_hi(pair_panel), side_hi)
    schur_two = quarter_part[:, second_size:] - jnp.dot(
        panel_two, all_panel.T, precision=HIGHEST_MODE
    )
    lower_two = lax.dynamic_slice_in_dim(lower_full, quarter * quarter_pivot, quarter_pivot, 0)
    return (
        lower_one[None, None],
        panel_part[None, None],
        lower_two[None, None],
        panel_two[None, None],
        schur_two[None, None],
    )


def solution(mesh):
    placed = (
        P("hi", "lo", None, None),
        P("hi", "lo", None, None),
        P("hi", "lo", None, None),
        P("hi", "lo", None, None),
        P("hi", "lo", None, None),
        P(),
        P(),
        P(),
        P(),
        P(),
        P(),
    )
    return jax.shard_map(
        body,
        mesh=mesh,
        in_specs=placed,
        out_specs=(
            P("hi", "lo", None, None),
            P("hi", "lo", None, None),
            P("hi", "lo", None, None),
            P("hi", "lo", None, None),
            P("hi", "lo", None, None),
        ),
        check_vma=False,
    )
```

profile of v0, /device:TPU:0, one launch (start us, length us, event | category | flops | bytes accessed | tf_op | source)
XLA Modules:
  0.0 991.3 jit_solution(8089663317388518020)
XLA Ops:
  70.4 50.5 %collective-permute-done = f32[384,768]{0,1:T(8,128)} collective-permute-done((f32[384,768]{0,1:T(8,128)}, f32[384,768]{0,1:T(8,128)}, u32[]{:S(2)}, u32[]{:S(2)}) %collective-permute-start) | collective-permute-done | bytes 1179680 | tf_op jit(solution)/shard_map/ppermute | solution.py:17
  181.0 11.7 %cholesky.453 = f32[128,128]{1,0:T(8,128)S(1)} custom-call(f32[128,128]{1,0:T(8,128)S(1)} %cholesky.669), custom_call_target="Cholesky" | custom-call | tf_op jit(solution)/shard_map/jit(cholesky)/cholesky | solution.py:39
  205.7 11.7 %cholesky.472 = f32[128,128]{1,0:T(8,128)S(1)} custom-call(f32[128,128]{1,0:T(8,128)S(1)} %cholesky.673), custom_call_target="Cholesky" | custom-call | tf_op jit(solution)/shard_map/jit(cholesky)/cholesky | solution.py:39
  230.3 11.7 %cholesky.493 = f32[128,128]{1,0:T(8,128)S(1)} custom-call(f32[128,128]{1,0:T(8,128)S(1)} %cholesky.678), custom_call_target="Cholesky" | custom-call | tf_op jit(solution)/shard_map/jit(cholesky)/cholesky | solution.py:39
  254.5 11.9 %cholesky.512 = f32[128,128]{1,0:T(8,128)S(1)} custom-call(f32[128,128]{1,0:T(8,128)S(1)} %cholesky.683), custom_call_target="Cholesky" | custom-call | tf_op jit(solution)/shard_map/jit(cholesky)/cholesky | solution.py:39
  278.6 11.7 %cholesky.531 = f32[128,128]{1,0:T(8,128)S(1)} custom-call(f32[128,128]{1,0:T(8,128)S(1)} %cholesky.688), custom_call_target="Cholesky" | custom-call | tf_op jit(solution)/shard_map/jit(cholesky)/cholesky | solution.py:39
  302.3 11.7 %cholesky.548 = f32[128,128]{1,0:T(8,128)S(1)} custom-call(f32[128,128]{1,0:T(8,128)S(1)} %slice_subtract_fusion.21), custom_call_target="Cholesky" | custom-call | tf_op jit(solution)/shard_map/jit(cholesky)/cholesky | solution.py:39
  323.8 18.1 %while.2 = (s32[]{:T(128)}, f32[768,768]{0,1:T(8,128)}, s32[6,2]{0,1:T(2,128)S(1)}, f32[6,128,128]{2,1,0:T(8,128)S(1)}, s32[]{:T(128)}) while((s32[]{:T(128)}, f32[768,768]{0,1:T(8,128)}, s32[6,2]{0,1:T(2,128)S(1)}, f32[6,128,128]{2,1,0:T(8,128)S(1)}, s32[]{:T(128)}) %tuple.86), condition=%wide.while_cond, body=%wide.while_body.sunk | while | flops 2 | bytes 393329 | solution.py:40
  341.9 59.4 %custom-call.38 = f32[6,128,128]{1,2,0:T(8,128)S(1)} custom-call(f32[6,128,128]{2,1,0:T(8,128)S(1)} %get-tuple-element.13), custom_call_target="InvertDiagBlocksLowerTriangular" | custom-call | tf_op jit(solution)/shard_map/triangular_solve | solution.py:40
  426.4 47.3 %collective-permute-done.2 = f32[768,768]{0,1:T(8,128)} collective-permute-done((f32[768,768]{0,1:T(8,128)}, f32[768,768]{0,1:T(8,128)}, u32[]{:S(2)}, u32[]{:S(2)}) %collective-permute-start.2) | collective-permute-done | bytes 2359328 | tf_op jit(solution)/shard_map/ppermute | solution.py:17
  476.4 25.2 %slice_subtract_fusion = f32[768,1536]{0,1:T(8,128)} fusion(f32[768,2304]{0,1:T(8,128)S(1)} %bitcast.301, f32[768,768]{0,1:T(8,128)} %convolution_dynamic-update-slice_fusion, f32[768,768]{0,1:T(8,128)S(1)} %get-tuple-element.103, f32[768,768]{0,1:T(8,128)S(1)} %get-tuple-element.102), kind=kOutput, calls=%fused_computation.15 | convolution fusion | flops 10873995264 | bytes 16515072 | tf_op jit(solution)/shard_map/dot_general | solution.py:124
  545.3 14.6 %fusion.2 = f32[12,128,18,128]{3,2,1,0:T(8,128)} fusion(f32[12,128,12,128]{3,0,2,1:T(8,128)S(1)} %fusion.185, s32[12]{0:T(128)S(1)} %fusion.206), kind=kOutput, calls=%fused_computation.6 | convolution fusion | flops 509608160 | bytes 23593008 | tf_op jit(solution)/shard_map/axky,kb->axby/dot_general | solution.py:31
  559.9 17.8 %reshape_reshape.3 = f32[2,768,2304]{2,1,0:T(8,128)} reshape(f32[12,128,18,128]{3,2,1,0:T(8,128)} %fusion.2) | data formatting | bytes 28311552 | tf_op jit(solution)/shard_map/reshape;reshape | solution.py:145
  612.9 30.8 %collective-permute-done.4 = f32[768,768]{0,1:T(8,128)} collective-permute-done((f32[768,768]{0,1:T(8,128)}, f32[768,768]{0,1:T(8,128)}, u32[]{:S(2)}, u32[]{:S(2)}) %collective-permute-start.4) | collective-permute-done | bytes 2359328 | tf_op jit(solution)/shard_map/ppermute | solution.py:17
  651.9 11.7 %cholesky.563 = f32[128,128]{1,0:T(8,128)S(1)} custom-call(f32[128,128]{1,0:T(8,128)S(1)} %cholesky.692), custom_call_target="Cholesky" | custom-call | tf_op jit(solution)/shard_map/jit(cholesky)/cholesky | solution.py:39
  676.6 11.7 %cholesky.582 = f32[128,128]{1,0:T(8,128)S(1)} custom-call(f32[128,128]{1,0:T(8,128)S(1)} %cholesky.696), custom_call_target="Cholesky" | custom-call | tf_op jit(solution)/shard_map/jit(cholesky)/cholesky | solution.py:39
  701.0 11.7 %cholesky.603 = f32[128,128]{1,0:T(8,128)S(1)} custom-call(f32[128,128]{1,0:T(8,128)S(1)} %cholesky.701), custom_call_target="Cholesky" | custom-call | tf_op jit(solution)/shard_map/jit(cholesky)/cholesky | solution.py:39
  725.2 12.2 %cholesky.622 = f32[128,128]{1,0:T(8,128)S(1)} custom-call(f32[128,128]{1,0:T(8,128)S(1)} %cholesky.706), custom_call_target="Cholesky" | custom-call | tf_op jit(solution)/shard_map/jit(cholesky)/cholesky | solution.py:39
  749.6 11.7 %cholesky.641 = f32[128,128]{1,0:T(8,128)S(1)} custom-call(f32[128,128]{1,0:T(8,128)S(1)} %cholesky.711), custom_call_target="Cholesky" | custom-call | tf_op jit(solution)/shard_map/jit(cholesky)/cholesky | solution.py:39
  773.3 11.7 %cholesky.658 = f32[128,128]{1,0:T(8,128)S(1)} custom-call(f32[128,128]{1,0:T(8,128)S(1)} %slice_subtract_fusion.20), custom_call_target="Cholesky" | custom-call | tf_op jit(solution)/shard_map/jit(cholesky)/cholesky | solution.py:39
  808.5 18.1 %while.3 = (s32[]{:T(128)}, f32[768,768]{0,1:T(8,128)}, s32[6,2]{0,1:T(2,128)S(1)}, f32[6,128,128]{2,1,0:T(8,128)S(1)}, s32[]{:T(128)}) while((s32[]{:T(128)}, f32[768,768]{0,1:T(8,128)}, s32[6,2]{0,1:T(2,128)S(1)}, f32[6,128,128]{2,1,0:T(8,128)S(1)}, s32[]{:T(128)}) %tuple.92), condition=%wide.while_cond.1, body=%wide.while_body.1.sunk | while | flops 2 | bytes 393329 | solution.py:40
  826.6 59.0 %custom-call.39 = f32[6,128,128]{1,2,0:T(8,128)S(1)} custom-call(f32[6,128,128]{2,1,0:T(8,128)S(1)} %get-tuple-element.21), custom_call_target="InvertDiagBlocksLowerTriangular" | custom-call | tf_op jit(solution)/shard_map/triangular_solve | solution.py:40
  903.5 25.2 %collective-permute-done.7 = f32[384,768]{0,1:T(8,128)S(1)} collective-permute-done((f32[384,768]{0,1:T(8,128)S(1)}, f32[384,768]{0,1:T(8,128)S(1)}, u32[]{:S(2)}, u32[]{:S(2)}) %collective-permute-start.7) | collective-permute-done | bytes 1179680 | tf_op jit(solution)/shard_map/ppermute | solution.py:17
  945.1 36.0 %collective-permute-done.8 = f32[768,768]{0,1:T(8,128)} collective-permute-done((f32[768,768]{0,1:T(8,128)}, f32[768,768]{0,1:T(8,128)}, u32[]{:S(2)}, u32[]{:S(2)}) %collective-permute-start.8) | collective-permute-done | bytes 2359328 | tf_op jit(solution)/shard_map/ppermute | solution.py:17
  (313 shorter events, 474.1 us)
Async XLA Ops:
  0.6 49.3 %copy-start = (s32[8,8,12,6]{2,1,3,0:T(8,128)S(1)}, s32[8,8,12,6]{2,1,3,0:T(8,128)}, u32[]{:S(2)}) copy-start(s32[8,8,12,6]{2,1,3,0:T(8,128)} %param.19) | copy-start | bytes 55300
  0.6 121.6 %collective-permute-start.1 = (f32[1024,1024]{1,0:T(8,128)}, f32[1024,1024]{1,0:T(8,128)}, u32[]{:S(2)}, u32[]{:S(2)}) collective-permute-start(f32[1024,1024]{1,0:T(8,128)} %bitcast.316), channel_id=1, source_target_pairs={{0,64},{8,72},{16,80},{24,88},{32,96},{40,104},{48,112},{56,120},{... | collective-permute-start | bytes 12582920 | tf_op jit(solution)/shard_map/ppermute | solution.py:17
  7.4 113.5 %collective-permute-start = (f32[384,768]{0,1:T(8,128)}, f32[384,768]{0,1:T(8,128)}, u32[]{:S(2)}, u32[]{:S(2)}) collective-permute-start(f32[384,768]{0,1:T(8,128)} %bitcast), channel_id=1, source_target_pairs={{0,64},{8,72},{16,80},{24,88},{32,96},{40,104},{48,112},{56,120},{... | collective-permute-start | bytes 3538952 | tf_op jit(solution)/shard_map/ppermute | solution.py:17
  163.3 7.2 copy-start.7
  163.3 7.8 copy-start.8
  163.3 8.5 copy-start.10
  171.9 3.7 copy-start.2
  179.6 1.4 copy-start.12
  323.7 79.8 %copy-start.11 = (f32[768,768]{0,1:T(8,128)S(1)}, f32[768,768]{0,1:T(8,128)}, u32[]{:S(2)}) copy-start(f32[768,768]{0,1:T(8,128)} %get-tuple-element.146) | copy-start | bytes 7077892
  415.5 60.9 %slice-start = ((s8[7077888]{0:T(1024)(128)(4,1)}), s8[2883584]{0:T(1024)(128)(4,1)S(1)}, s32[]{:S(2)}) async-start(s8[7077888]{0:T(1024)(128)(4,1)} %bitcast.300), calls=%async_computation | async-start | bytes 5767168
  419.5 54.2 %collective-permute-start.2 = (f32[768,768]{0,1:T(8,128)}, f32[768,768]{0,1:T(8,128)}, u32[]{:S(2)}, u32[]{:S(2)}) collective-permute-start(f32[768,768]{0,1:T(8,128)} %convolution_dynamic-update-slice_fusion), channel_id=1, source_target_pairs={{0,64},{8,72},{16,80},{24,88},{32,96},{40,104},{48,112},{56,120},{... | collective-permute-start | bytes 7077896 | tf_op jit(solution)/shard_map/ppermute | solution.py:17
  426.4 50.0 %slice-start.1 = ((s8[7077888]{0:T(1024)(128)(4,1)}), s8[4194304]{0:T(1024)(128)(4,1)S(1)}, s32[]{:S(2)}) async-start(s8[7077888]{0:T(1024)(128)(4,1)} %bitcast.300), calls=%async_computation.1 | async-start | bytes 8388608
  524.7 2.1 copy-start.14
  534.6 53.2 %collective-permute-start.3 = (f32[768,768]{0,1:T(8,128)S(1)}, f32[768,768]{0,1:T(8,128)}, u32[]{:S(2)}, u32[]{:S(2)}) collective-permute-start(f32[768,768]{0,1:T(8,128)S(1)} %add.233), channel_id=1, source_target_pairs={{0,4},{1,5},{2,6},{3,7},{4,0},{5,1},{6,2},{7,3},{8,12},{9,13},{10,... | collective-permute-start | bytes 7077896 | tf_op jit(solution)/shard_map/ppermute | solution.py:17
  591.2 52.5 %collective-permute-start.4 = (f32[768,768]{0,1:T(8,128)}, f32[768,768]{0,1:T(8,128)}, u32[]{:S(2)}, u32[]{:S(2)}) collective-permute-start(f32[768,768]{0,1:T(8,128)} %add.234), channel_id=1, source_target_pairs={{0,64},{8,72},{16,80},{24,88},{32,96},{40,104},{48,112},{56,120},{... | collective-permute-start | bytes 7077896 | tf_op jit(solution)/shard_map/ppermute | solution.py:17
  601.1 189.1 %collective-permute-start.5 = (f32[768,2304]{1,0:T(8,128)}, f32[768,2304]{1,0:T(8,128)}, u32[]{:S(2)}, u32[]{:S(2)}) collective-permute-start(f32[768,2304]{1,0:T(8,128)} %dynamic-slice_bitcast_fusion), channel_id=1, source_target_pairs={{0,4},{1,5},{2,6},{3,7},{4,0},{5,1},{6,2},{7,3},{8,12},{9,13},{10,... | collective-permute-start | bytes 21233672 | tf_op jit(solution)/shard_map/ppermute | solution.py:17
  796.1 4.0 copy-start.3
  800.1 85.5 %collective-permute-start.6 = (f32[384,2304]{1,0:T(8,128)}, f32[384,2304]{1,0:T(8,128)}, u32[]{:S(2)}, u32[]{:S(2)}) collective-permute-start(f32[384,2304]{1,0:T(8,128)} %dynamic-slice_bitcast_fusion.1), channel_id=1, source_target_pairs={{0,64},{8,72},{16,80},{24,88},{32,96},{40,104},{48,112},{56,120},{... | collective-permute-start | bytes 10616840 | tf_op jit(solution)/shard_map/ppermute | solution.py:17
  890.3 2.4 copy-start.4
  903.2 25.6 %collective-permute-start.7 = (f32[384,768]{0,1:T(8,128)S(1)}, f32[384,768]{0,1:T(8,128)S(1)}, u32[]{:S(2)}, u32[]{:S(2)}) collective-permute-start(f32[384,768]{0,1:T(8,128)S(1)} %convolution_dynamic-update-slice_fusion.3), channel_id=1, source_target_pairs={{0,64},{8,72},{16,80},{24,88},{32,96},{40,104},{48,112},{56,120},{... | collective-permute-start | bytes 3538952 | tf_op jit(solution)/shard_map/ppermute | solution.py:17
  929.0 1.8 copy-start.6
  930.8 50.2 %collective-permute-start.8 = (f32[768,768]{0,1:T(8,128)}, f32[768,768]{0,1:T(8,128)}, u32[]{:S(2)}, u32[]{:S(2)}) collective-permute-start(f32[768,768]{0,1:T(8,128)} %pad_maximum_fusion), channel_id=1, source_target_pairs={{0,4},{1,5},{2,6},{3,7},{4,0},{5,1},{6,2},{7,3},{8,12},{9,13},{10,... | collective-permute-start | bytes 7077896 | tf_op jit(solution)/shard_map/ppermute | solution.py:17
  945.1 38.3 %copy-start.5 = (f32[384,2304]{1,0:T(8,128)S(1)}, f32[384,2304]{1,0:T(8,128)}, u32[]{:S(2)}) copy-start(f32[384,2304]{1,0:T(8,128)} %copy-done.4) | copy-start | bytes 10616836
  983.4 7.5 copy-start.1
  (2 other events, 2.8 us)
where the time goes:
time: 1000 us; the launch traced here: 991 us
  other arithmetic  416 us (42%)
  waiting for transfers between devices  200 us (20%)
  local copies, waits for them, and re-layouts  188 us (19%)
  matrix products  156 us (16%)
  starting transfers between devices  20.9 us (2%)
    another operation x45, other arithmetic, factor(): factor_lower = jnp.linalg.cholesky(pivot_block)  247 us
    ppermute x9, waiting for transfers between devices, partner(): lax.ppermute(array, axis, [(i, i ^ 1 << apart) for i in range(lax.axis_si...  200 us
    another operation x5, other arithmetic, factor(): lax.linalg.triangular_solve(factor_lower, coupling, left_side=False, lowe...  123 us
    unnamed x54, local copies, waits for them, and re-layouts  49.8 us
    dot_general x6, matrix products, spread(): jnp.einsum('ia,ixky->axky', row_onehot, blocks, precision=HIGHEST_MODE)  37.1 us
    another operation x61, local copies, waits for them, and re-layouts  35.9 us
    dot_general x6, matrix products, spread(): jnp.einsum('axky,kb->axby', placed, col_onehot, precision=HIGHEST_MODE)  32.1 us
    another operation x22, matrix products, factor(): lax.linalg.triangular_solve(factor_lower, coupling, left_side=False, lowe...  30.9 us
  transfers between devices with their start and end apart: 9, of which 6 were waited for; matrix products, arithmetic and copies ran while one was open for 37% of the time, Pallas kernels for 0%

commit v1 on v0

v1 whole, which is shorter than its diff:
```python
import functools
import jax
import jax.numpy as jnp
from jax import lax
from jax.experimental import pallas as pl
from jax.experimental.pallas import tpu as pltpu
from jax.sharding import PartitionSpec as P

T = 128
NP = 6
NU = 12
NC = 8
f32 = jnp.float32
bf16 = jnp.bfloat16
NN = ((1,), (0,))
NT = ((1,), (1,))
OWN, OTH, MAP2, SLO, SHI, LIVE1, LIVE2, FILL1, FILL2 = 0, 8, 16, 28, 29, 30, 31, 32, 68


def tl(i):
    return pl.ds(pl.multiple_of(i * T, T), T)


def split(x):
    hi = x.astype(bf16)
    return hi, (x - hi.astype(f32)).astype(bf16)


def dot3(a, b, dims):
    (ah, al), (bh, bl) = a, b
    dn = (dims, ((), ()))
    f = lambda x, y: lax.dot_general(x, y, dn, preferred_element_type=f32)
    return f(ah, bh) + (f(ah, bl) + f(al, bh))


def call(kernel, args, specs, outs, scratch, name, flops=0, grid=(1,)):
    whole = pl.BlockSpec(memory_space=pltpu.VMEM)
    in_specs = [whole if s is None else s for s in specs]
    nbytes = sum(4 * a.size for a in args[1:]) + sum(4 * o.size for o in outs)
    return pl.pallas_call(
        kernel,
        grid_spec=pltpu.PrefetchScalarGridSpec(
            num_scalar_prefetch=1,
            grid=grid,
            in_specs=in_specs,
            out_specs=[whole] * len(outs),
            scratch_shapes=scratch,
        ),
        out_shape=outs,
        compiler_params=pltpu.CompilerParams(vmem_limit_bytes=60 * 1024 * 1024),
        cost_estimate=pl.CostEstimate(flops=flops, bytes_accessed=nbytes, transcendentals=0),
        name=name,
    )(*args)


def shape(*dims, dtype=f32):
    return jax.ShapeDtypeStruct(dims, dtype)


def block(rows, cols, j):
    return pl.BlockSpec((rows, cols), lambda i, s: (0, j))


def invert(s_ref, first, count, inv_ref, size):
    for r in range(size):
        inv_ref[r] = -1
    for i in range(count):
        inv_ref[s_ref[first + i]] = i


def gather_one_kernel(s_ref, c_ref, p_ref, piv_ref, coup_ref, inv):
    side = s_ref[SLO]
    invert(s_ref, OWN, NC, inv, 18)

    def piv_row(r, _):
        local = r - 3 * side

        def piv_col(c, _):
            at = r * (r + 1) // 2 + c

            @pl.when((local >= 0) & (local < 3))
            def _():
                piv_ref[at] = p_ref[tl(local), tl(c)]

            @pl.when((local < 0) | (local >= 3))
            def _():
                piv_ref[at] = jnp.zeros((T, T), f32)

            @pl.when((inv[r] >= 0) & (inv[c] >= 0))
            def _():
                piv_ref[at] += c_ref[tl(inv[r]), tl(inv[c])]

            return 0

        return lax.fori_loop(0, r + 1, piv_col, 0)

    lax.fori_loop(0, NP, piv_row, 0)

    def coup_tile(t, count):
        row = inv[NP + (1 - side) * 6 + t // NP]
        col = inv[t % NP]
        hit = (row >= 0) & (col >= 0)

        @pl.when(hit)
        def _():
            coup_ref[count] = c_ref[tl(row), tl(col)]

        return count + hit.astype(jnp.int32)

    lax.fori_loop(0, 36, coup_tile, 0)


def factor_tile(d_ref, w_ref, u_ref):
    lane = lax.broadcasted_iota(jnp.int32, (8, T), 1)
    row = lax.broadcasted_iota(jnp.int32, (8, T), 0)
    for g in range(16):
        r0 = 8 * g
        w_ref[r0 : r0 + 8, :] = jnp.where(lane == row + r0, 1.0, 0.0).astype(f32)
    for g in range(16):
        r0 = 8 * g
        rows = [jnp.broadcast_to(d_ref[r0 + i : r0 + i + 1, :], (8, T)) for i in range(8)]
        wrows = [jnp.broadcast_to(w_ref[r0 + i : r0 + i + 1, :], (8, T)) for i in range(8)]
        e = [
            [jnp.broadcast_to(rows[i][:, r0 + k : r0 + k + 1], (8, T)) for k in range(i + 1)]
            for i in range(8)
        ]
        l = [[None] * 8 for _ in range(8)]
        rinv = [None] * 8
        for j in range(8):
            rinv[j] = lax.rsqrt(e[j][j])
            for i in range(j + 1, 8):
                l[i][j] = e[i][j] * rinv[j]
            for i in range(j + 1, 8):
                for k in range(j + 1, i + 1):
                    e[i][k] = e[i][k] - l[i][j] * l[k][j]
        u = [None] * 8
        w = [None] * 8
        for j in range(8):
            a = rows[j]
            b = wrows[j]
            for k in range(j):
                a = a - l[j][k] * u[k]
                b = b - l[j][k] * w[k]
            u[j] = a * rinv[j]
            w[j] = b * rinv[j]
            u_ref[r0 + j : r0 + j + 1, :] = jnp.where(lane[:1] >= r0 + j, u[j][:1], 0.0)
            w_ref[r0 + j : r0 + j + 1, :] = w[j][:1]
        for r in range(g + 1, 16):
            q = 8 * r
            dr = d_ref[q : q + 8, :]
            wr = w_ref[q : q + 8, :]
            c = [jnp.broadcast_to(dr[:, r0 + k : r0 + k + 1], (8, T)) for k in range(8)]
            for j in range(8):
                a = c[j]
                for k in range(j):
                    a = a - l[j][k] * c[k]
                c[j] = a * rinv[j]
            for j in range(8):
                dr = dr - c[j] * u[j]
                wr = wr - c[j] * w[j]
            d_ref[q : q + 8, :] = dr
            w_ref[q : q + 8, :] = wr


def factor_kernel(counts, live_at, take, s_ref, *refs):
    n_in = 2 * len(counts)
    ins = refs[:n_in]
    low_ref, lh_ref, ll_ref, wh_ref, wl_ref, a_s, l_s, d_s, w_s, u_s = refs[n_in:]
    live = s_ref[live_at]
    first = 0
    spots = [(r, c) for r in range(NP) for c in range(r + 1)]
    for n, count in enumerate(counts):
        for t in range(count):
            r, c = spots[first + t]
            a_s[r * T : r * T + T, c * T : c * T + T] = ins[2 * n][t] + ins[2 * n + 1][t]
        first += count
    l_s[...] = jnp.zeros_like(l_s)
    ii = lax.broadcasted_iota(jnp.int32, (T, T), 0)
    jj = lax.broadcasted_iota(jnp.int32, (T, T), 1)
    eye = jnp.where(ii == jj, 1.0, 0.0).astype(f32)

    def dead(k, _):
        l_s[tl(k), tl(k)] = eye
        return 0

    lax.fori_loop(live, NP, dead, 0)

    def step(k, _):
        s = tl(k)
        d_s[...] = a_s[s, s]
        factor_tile(d_s, w_s, u_s)
        l_s[s, s] = u_s[...].T
        w = split(w_s[...])
        wh_ref[s, :] = w[0]
        wl_ref[s, :] = w[1]

        def panel(i, _):
            x = dot3(split(a_s[tl(i), s]), w, NT)
            l_s[tl(i), s] = x
            xh, xl = split(x)
            lh_ref[tl(i), s] = xh
            ll_ref[tl(i), s] = xl
            return 0

        lax.fori_loop(k + 1, live, panel, 0)

        def col(j, _):
            xj = (lh_ref[tl(j), s], ll_ref[tl(j), s])

            def tile(i, _):
                xi = (lh_ref[tl(i), s], ll_ref[tl(i), s])
                a_s[tl(i), tl(j)] = a_s[tl(i), tl(j)] - dot3(xi, xj, NT)
                return 0

            return lax.fori_loop(j, live, tile, 0)

        return lax.fori_loop(k + 1, live, col, 0)

    lax.fori_loop(0, live, step, 0)
    low_ref[...] = l_s[pl.ds(pl.multiple_of(take(s_ref), 64), low_ref.shape[0]), :]


def factor(scalars, pairs, live_at, take, rows, name):
    counts = tuple(x.shape[0] for x, _ in pairs)
    n = NP * T
    return call(
        functools.partial(factor_kernel, counts, live_at, take),
        [scalars] + [x for pair in pairs for x in pair],
        [None] * (2 * len(pairs)),
        [shape(rows, n), shape(n, n, dtype=bf16), shape(n, n, dtype=bf16)]
        + [shape(n, T, dtype=bf16)] * 2,
        [pltpu.VMEM((n, n), f32)] * 2 + [pltpu.VMEM((T, T), f32)] * 3,
        name,
        flops=20_000_000_000,
    )


def solve(x_ref, live, lh_ref, ll_ref, wh_ref, wl_ref, ph, plo):
    for k in range(NP):
        s = slice(k * T, k * T + T)

        @pl.when(k < live)
        def _():
            x = x_ref[:, s]
            if k:
                b = slice(0, k * T)
                x = x - dot3((ph[:, b], plo[:, b]), (lh_ref[s, b], ll_ref[s, b]), NT)
            x = dot3(split(x), (wh_ref[s, :], wl_ref[s, :]), NT)
            x_ref[:, s] = x
            xh, xl = split(x)
            ph[:, s] = xh
            plo[:, s] = xl

        @pl.when(k >= live)
        def _():
            x_ref[:, s] = jnp.zeros_like(x_ref[:, s])
            ph[:, s] = jnp.zeros_like(ph[:, s])
            plo[:, s] = jnp.zeros_like(plo[:, s])


def panel_one_kernel(
    s_ref, r_ref, c_ref, got_ref, lh, ll, wh, wl, p_ref, send_ref, ph, plo, inv, inv2
):
    side = s_ref[SLO]
    invert(s_ref, OWN, NC, inv, 18)
    invert(s_ref, OTH, NC, inv2, 18)

    def tile(t, count):
        r = t // NP
        c = t % NP
        dst = (tl(r), tl(c))
        row = NP + side * 6 + r
        p_ref[dst] = r_ref[dst] * s_ref[FILL1 + t].astype(f32)

        @pl.when((inv[row] >= 0) & (inv[c] >= 0))
        def _():
            p_ref[dst] += c_ref[tl(inv[row]), tl(inv[c])]

        hit = (inv2[row] >= 0) & (inv2[c] >= 0)

        @pl.when(hit)
        def _():
            p_ref[dst] += got_ref[count]

        return count + hit.astype(jnp.int32)

    lax.fori_loop(0, 36, tile, 0)
    solve(p_ref, s_ref[LIVE1], lh, ll, wh, wl, ph, plo)
    send_ref[...] = p_ref[:, pl.ds(pl.multiple_of((1 - side) * 384, T), 384)]


def product_kernel(s_ref, p_ref, q_ref, t0_ref, t1_ref, own_ref, cross_ref, ph, plo):
    side = s_ref[SLO]
    ph[...], plo[...] = split(p_ref[...])
    qh, ql = split(q_ref[...])
    mine = pl.ds(pl.multiple_of(side * 384, T), 384)
    pc = (ph[:, mine], plo[:, mine])
    for n in range(3):
        s = slice(n * 256, n * 256 + 256)
        base = jnp.where(side == 0, t0_ref[:, s], t1_ref[:, s])
        own_ref[:, s] = base - dot3((ph[...], plo[...]), (ph[s, :], plo[s, :]), NT)
        base = jnp.where(side == 0, t1_ref[:, s], 0.0)
        cross_ref[:, s] = base - dot3(pc, (qh[s, :], ql[s, :]), NT)


def source_tile(side, inv, inv2, own_ref, cross_ref, c_ref, out_ref, at, r, c):
    i = inv2[r]
    j = inv2[c]
    used = (i >= 0) & (j >= 0)
    i = jnp.maximum(i, 0)
    j = jnp.maximum(j, 0)
    mi = (i // 6) == side
    mj = (j // 6) == side
    li = i % 6
    lj = j % 6

    @pl.when(used & mi & mj)
    def _():
        out_ref[at] = own_ref[tl(li), tl(lj)]

    @pl.when(used & mi & jnp.logical_not(mj))
    def _():
        out_ref[at] = cross_ref[tl(li), tl(lj)]

    @pl.when(used & jnp.logical_not(mi) & mj)
    def _():
        out_ref[at] = cross_ref[tl(lj), tl(li)].T

    @pl.when(jnp.logical_not(used) | (jnp.logical_not(mi) & jnp.logical_not(mj)))
    def _():
        out_ref[at] = jnp.zeros((T, T), f32)

    ci = inv[i + NP]
    cj = inv[j + NP]

    @pl.when(used & (ci >= 0) & (cj >= 0))
    def _():
        out_ref[at] += c_ref[tl(ci), tl(cj)]


def pivot_two_kernel(s_ref, own_ref, cross_ref, c_ref, p_ref, a_ref, b_ref, wide, inv, inv2):
    side = s_ref[SLO]
    quarter = 2 * s_ref[SHI] + side
    invert(s_ref, OWN, NC, inv, 18)
    invert(s_ref, MAP2, NU, inv2, 18)
    wide[...] = jnp.zeros_like(wide)
    wide[pl.ds(pl.multiple_of((quarter % 2) * 64, 64), 192), :] = p_ref[...]
    base = (3 * quarter) // 2

    def emit(out_ref, first, row):
        def col(c, _):
            at = row * (row + 1) // 2 + c - first
            source_tile(side, inv, inv2, own_ref, cross_ref, c_ref, out_ref, at, row, c)

            @pl.when((row >= base) & (row < base + 2))
            def _():
                out_ref[at] += wide[tl(row - base), tl(c)]

            return 0

        lax.fori_loop(0, row + 1, col, 0)

    lax.fori_loop(0, 4, lambda r, _: (emit(a_ref, 0, r), 0)[1], 0)
    lax.fori_loop(4, 6, lambda r, _: (emit(b_ref, 10, r), 0)[1], 0)


def rows_two_kernel(first, width, s_ref, own_ref, cross_ref, c_ref, *refs):
    outs = refs[:4]
    inv, inv2 = refs[4:]
    lo = s_ref[SLO]
    hi = s_ref[SHI]
    invert(s_ref, OWN, NC, inv, 18)
    invert(s_ref, MAP2, NU, inv2, 18)
    half = width // 2
    orders = (
        (0, (1 - hi, 1 - lo), (1 - hi, lo)),
        (0, (hi, 1 - lo), (hi, lo)),
        (half, (1 - hi, 1 - lo), (hi, 1 - lo)),
        (half, (1 - hi, lo), (hi, lo)),
    )
    for out_ref, (skip, one, two) in zip(outs, orders):

        def tile(t, _):
            r = t // half
            later = (r >= 3).astype(jnp.int32)
            a = one[0] + (two[0] - one[0]) * later
            b = one[1] + (two[1] - one[1]) * later
            row = NP + 6 * a + 3 * b + r % 3
            col = first + skip + t % half
            source_tile(lo, inv, inv2, own_ref, cross_ref, c_ref, out_ref, t, row, col)
            return 0

        lax.fori_loop(0, 6 * half, tile, 0)


def rows_two(scalars, own, cross, block_c, first, width, name):
    count = 3 * width
    return call(
        functools.partial(rows_two_kernel, first, width),
        [scalars, own, cross, block_c],
        [None] * 3,
        [shape(count, T, T)] * 4,
        [pltpu.SMEM((18,), jnp.int32)] * 2,
        name,
    )


def panel_two_kernel(
    s_ref, r_ref, xk, x1, x2, zk, z1, z2, lh, ll, wh, wl, p_ref, ph, plo
):
    for r in range(3):
        for c in range(3):
            t = 3 * r + c
            dst = (slice(r * T, r * T + T), slice(c * T, c * T + T))
            fill = s_ref[FILL2 + 6 * r + c].astype(f32)
            p_ref[dst] = r_ref[dst] * fill + ((xk[9 + t] + x1[9 + t]) + x2[t])
            dst = (dst[0], slice((c + 3) * T, (c + 4) * T))
            fill = s_ref[FILL2 + 6 * r + c + 3].astype(f32)
            p_ref[dst] = r_ref[dst] * fill + ((zk[9 + t] + z1[9 + t]) + z2[t])
    solve(p_ref, s_ref[LIVE2], lh, ll, wh, wl, ph, plo)


def schur_kernel(
    s_ref, t0_ref, t1_ref, xk, x1, x2, zk, z1, z2, p_ref, px, pz, pd0, pd1, out_ref
):
    hi = s_ref[SHI]
    lo = s_ref[SLO]
    for r in range(3):
        for c in range(6):
            t = 6 * r + c
            rows = slice(r * T, r * T + T)
            cols = slice(c * T, c * T + T)
            out_ref[rows, cols] = t0_ref[rows, cols] + ((xk[18 + t] + x1[18 + t]) + x2[t])
            right = slice(768 + c * T, 768 + c * T + T)
            out_ref[rows, right] = t1_ref[rows, cols] + ((zk[18 + t] + z1[18 + t]) + z2[t])
    mine = split(p_ref[...])

    def minus(a, b, skip, size, ref):
        cols = pl.ds(pl.multiple_of((2 * a + b) * 384 + skip, 64), size)
        return cols, dot3(mine, split(ref[...]), NT)

    for a, b, ref in ((hi, lo, p_ref), (1 - hi, lo, px), (hi, 1 - lo, pz)):
        cols = pl.ds(pl.multiple_of((2 * a + b) * 384, T), 384)
        out_ref[:, cols] = out_ref[:, cols] - dot3(mine, split(ref[...]), NT)
    diag = jnp.concatenate([pd0[...], pd1[...]], axis=0)
    cols = pl.ds(pl.multiple_of((2 * (1 - hi) + 1 - lo) * 384, T), 384)
    out_ref[:, cols] = out_ref[:, cols] - dot3(mine, split(diag), NT)


def across(axis, values):
    size = lax.axis_size(axis)
    return lax.ppermute(values, axis, [(i, i ^ (size // 2)) for i in range(size)])


def body(
    contribution,
    pivot_one,
    rows_one,
    pivot_two,
    rows_two_in,
    map_one,
    map_two,
    fill_one,
    fill_two,
    live_one,
    live_two,
):
    size_lo = lax.axis_size("lo")
    size_hi = lax.axis_size("hi")
    half_lo = size_lo // 2
    half_hi = size_hi // 2
    lo = lax.axis_index("lo")
    hi = lax.axis_index("hi")
    side_lo = lo // half_lo
    side_hi = hi // half_hi
    front_lo = lo % half_lo
    front_hi = hi % half_hi
    quarter = 2 * side_hi + side_lo
    i32 = jnp.int32
    scalars = jnp.concatenate(
        [
            map_one[hi, lo],
            map_one[hi, (lo + half_lo) % size_lo],
            map_two[hi, front_lo],
            jnp.stack([side_lo, side_hi]).astype(i32),
            live_one[hi, front_lo][None],
            live_two[front_hi, front_lo][None],
            lax.dynamic_slice_in_dim(fill_one[hi, front_lo], side_lo * 6, 6, 0).reshape(36),
            lax.dynamic_slice_in_dim(fill_two[front_hi, front_lo], quarter * 3, 3, 0).reshape(18),
        ]
    )
    c = contribution[0, 0]
    rows1 = rows_one[0, 0]
    rows2 = rows_two_in[0, 0]
    smem = pltpu.SMEM((18,), i32)
    n = NP * T

    piv, coup = call(
        gather_one_kernel,
        [scalars, c, pivot_one[0, 0]],
        [None, None],
        [shape(21, T, T), shape(16, T, T)],
        [smem],
        "gather_one",
    )
    piv_got = across("lo", piv)
    coup, piv_got = lax.optimization_barrier((coup, piv_got))
    coup_got = across("lo", coup)
    lower_one, *fac1 = factor(
        scalars, [(piv, piv_got)], LIVE1, lambda s: s[SLO] * 384, 384, "factor_one"
    )
    panel_one, send = call(
        panel_one_kernel,
        [scalars, rows1, c, coup_got, *fac1],
        [block(n, n, 0)] + [None] * 6,
        [shape(n, n), shape(n, n // 2)],
        [pltpu.VMEM((n, n), bf16)] * 2 + [smem] * 2,
        "panel_one",
        flops=3_000_000_000,
    )
    got = across("lo", send)
    own, cross = call(
        product_kernel,
        [scalars, panel_one, got, rows1, rows1],
        [None, None, block(n, n, 1), block(n, n, 2)],
        [shape(n, n), shape(n, n)],
        [pltpu.VMEM((n, n), bf16)] * 2,
        "product_one",
        flops=4_000_000_000,
    )
    pa, pb = call(
        pivot_two_kernel,
        [scalars, own, cross, c, pivot_two[0, 0]],
        [None] * 4,
        [shape(10, T, T), shape(11, T, T)],
        [pltpu.VMEM((2 * T, n), f32), smem, smem],
        "pivot_two",
    )
    pa1 = across("hi", pa)
    pb1 = across("lo", pb)
    cxs, cxk, czs, czk = rows_two(scalars, own, cross, c, 0, NP, "coupling_two")
    cx1 = across("hi", cxs)
    cz1 = across("lo", czs)
    pa = pa + pa1
    pb = pb + pb1
    pa2 = across("lo", pa)
    pb2 = across("hi", pb)
    txs, txk, tzs, tzk = rows_two(scalars, own, cross, c, NP, NU, "trailing_two")
    tx1 = across("hi", txs)
    tz1 = across("lo", tzs)
    cx2 = across("lo", cxk[:9] + cx1[:9])
    cz2 = across("hi", czk[:9] + cz1[:9])
    lower_two, *fac2 = factor(
        scalars,
        [(pa, pa2), (pb, pb2)],
        LIVE2,
        lambda s: (2 * s[SHI] + s[SLO]) * 192,
        192,
        "factor_two",
    )
    (panel_two,) = call(
        panel_two_kernel,
        [scalars, rows2, cxk, cx1, cx2, czk, cz1, cz2, *fac2],
        [block(384, n, 0)] + [None] * 10,
        [shape(384, n)],
        [pltpu.VMEM((384, n), bf16)] * 2,
        "panel_two",
        flops=2_000_000_000,
    )
    tx2 = across("lo", txk[:18] + tx1[:18])
    tz2 = across("hi", tzk[:18] + tz1[:18])
    px = across("hi", panel_two)
    pz = across("lo", panel_two)
    pd0 = across("hi", pz[:192])
    pd1 = across("lo", px[192:])
    (schur_two,) = call(
        schur_kernel,
        [scalars, rows2, rows2, txk, tx1, tx2, tzk, tz1, tz2, panel_two, px, pz, pd0, pd1],
        [block(384, n, 1), block(384, n, 2)] + [None] * 11,
        [shape(384, NU * T)],
        [],
        "schur_two",
        flops=3_000_000_000,
    )
    return tuple(
        out[None, None] for out in (lower_one, panel_one, lower_two, panel_two, schur_two)
    )


def solution(mesh):
    split_spec = P("hi", "lo", None, None)
    return jax.shard_map(
        body,
        mesh=mesh,
        in_specs=(split_spec,) * 5 + (P(),) * 6,
        out_specs=(split_spec,) * 5,
        check_vma=False,
    )
```

time: 1000 us -> 386 us (0.39)
  other arithmetic: 416 us -> 6.9 us
  local copies, waits for them, and re-layouts: 188 us -> 10.6 us
  Pallas kernels: 0 us -> 176 us
  matrix products: 156 us -> 0 us
  waiting for transfers between devices: 200 us -> 155 us
  starting transfers between devices: 20.9 us -> 36.4 us
    another operation x50 -> x0, other arithmetic: 371 us -> none  [the longest x45 247 us: factor(): factor_lower = jnp.linalg.cholesky(pivot_block)]
    pallas_call x0 -> x10, Pallas kernels: none -> 176 us  [call(): pl.pallas_call(kernel, grid_spec=pltpu.PrefetchScalarGridSpec(num_scalar_...]
    dot_general x14 -> x0, matrix products: 102 us -> none  [the longest x6 37.1 us: spread(): jnp.einsum('ia,ixky->axky', row_onehot, blocks, precision=HIGHEST_MODE)]
    another operation x101 -> x0, local copies, waits for them, and re-layouts: 55.7 us -> none
    another operation x42 -> x0, matrix products: 54.6 us -> none  [the longest x22 30.9 us: factor(): lax.linalg.triangular_solve(factor_lower, coupling, left_side=False, lowe...]
    unnamed x54 -> x36, local copies, waits for them, and re-layouts: 49.8 us -> 3.15 us
    ppermute x9 -> x19, waiting for transfers between devices: 200 us -> 155 us  [across(): return lax.ppermute(values, axis, [(i, i ^ size // 2) for i in range(size)])]
    reshape x7 -> x2, local copies, waits for them, and re-layouts: 38 us -> 0.17 us  [the longest x1 0.08 us: body(): lax.dynamic_slice_in_dim(fill_two[front_hi, front_lo], quarter * 3, 3, 0)]
  transfers between devices with their start and end apart: 9 -> 19, of which waited for: 6 -> 8; matrix products, arithmetic and copies ran while one was open for 37% -> 2% of each run, Pallas kernels for 0% -> 31%
where the time goes in v1:
time: 386 us
  Pallas kernels  176 us (46%)
  waiting for transfers between devices  155 us (40%)
  starting transfers between devices  36.4 us (9%)
  local copies, waits for them, and re-layouts  10.6 us (3%)
  other arithmetic  6.9 us (2%)
    pallas_call x10, Pallas kernels, call(): pl.pallas_call(kernel, grid_spec=pltpu.PrefetchScalarGridSpec(num_scalar_...  176 us
    ppermute x19, waiting for transfers between devices, across(): return lax.ppermute(values, axis, [(i, i ^ size // 2) for i in range(size)])  155 us
    ppermute x19, starting transfers between devices, across(): return lax.ppermute(values, axis, [(i, i ^ size // 2) for i in range(size)])  36.4 us
  transfers between devices with their start and end apart: 19, of which 8 were waited for; matrix products, arithmetic and copies ran while one was open for 2% of the time, Pallas kernels for 31%

profile of v1, /device:TPU:0, one launch (start us, length us, event | category | flops | bytes accessed | tf_op | source)
XLA Modules:
  0.0 386.0 jit_solution(16354361448274942425)
XLA Ops:
  8.1 6.3 %gather_one.1 = (f32[21,128,128]{2,1,0:T(8,128)}, f32[16,128,128]{2,1,0:T(8,128)}) custom-call(s32[86]{0:T(128)} %concatenate.3.s_ref, f32[1024,1024]{1,0:T(8,128)} %bitcast.16, f32[384,768]{1,0:T(8,128)} %bitcast.30), custom_call_target="tpu_custom_call" | custom-call | bytes 7798784 | tf_op jit(solution)/shard_map/gather_one/pallas_call | solution.py:40
  14.4 4.2 %collective-permute-start = (f32[21,128,128]{2,1,0:T(8,128)}, f32[21,128,128]{2,1,0:T(8,128)S(1)}, u32[]{:S(2)}, u32[]{:S(2)}) collective-permute-start(f32[21,128,128]{2,1,0:T(8,128)} %get-tuple-element.33.refs_0_), channel_id=1, source_target_pairs={{0,64},{8,72},{16,80},{24,88},{32,96},{40,104},{48,112},{56,120},{... | collective-permute-start | bytes 4128776 | tf_op jit(solution)/shard_map/ppermute | solution.py:452
  18.6 30.4 %collective-permute-done.refs_1_ = f32[21,128,128]{2,1,0:T(8,128)S(1)} collective-permute-done((f32[21,128,128]{2,1,0:T(8,128)}, f32[21,128,128]{2,1,0:T(8,128)S(1)}, u32[]{:S(2)}, u32[]{:S(2)}) %collective-permute-start) | collective-permute-done | bytes 1376288 | tf_op jit(solution)/shard_map/ppermute | solution.py:452
  49.0 3.2 collective-permute-start.1
  52.2 40.7 %factor_one.1 = (f32[384,768]{1,0:T(8,128)}, bf16[768,768]{1,0:T(8,128)(2,1)}, bf16[768,768]{1,0:T(8,128)(2,1)}, bf16[768,128]{1,0:T(8,128)(2,1)}, bf16[768,128]{1,0:T(8,128)(2,1)}) custom-call(s32[86]{0:T(128)} %concatenate.3.s_ref, f32[21,128,128]{2,1,0:T(8,128)} %get-tuple-element.33.refs_0_, f32[21,128,128]{2,1,0:T(8,128)} %copy-done.17), custom_call_target="tpu_custom_call" | custom-call | flops 20000000000 | bytes 9437184 | tf_op jit(solution)/shard_map/factor_one/pallas_call | solution.py:40
  93.9 13.6 %panel_one.1 = (f32[768,768]{1,0:T(8,128)}, f32[768,384]{1,0:T(8,128)}) custom-call(s32[86]{0:T(128)} %concatenate.3.s_ref, f32[768,2304]{1,0:T(8,128)} %bitcast.21, f32[1024,1024]{1,0:T(8,128)} %bitcast.17, f32[16,128,128]{2,1,0:T(8,128)} %copy-done.13, bf16[768,768]{1,0:T(8,128)(2,1)} %get-tuple-element.38.lh, bf16[768,768]{1,0:T(8,128)(2,1)} %get-tuple-element.39.ll, ...), custom_call_target="tpu_custom_call" | custom-call | flops 3000000000 | bytes 21364736 | tf_op jit(solution)/shard_map/panel_one/pallas_call | solution.py:40
  108.6 27.2 %collective-permute-done.2.q_ref = f32[768,384]{1,0:T(8,128)S(1)} collective-permute-done((f32[768,384]{1,0:T(8,128)}, f32[768,384]{1,0:T(8,128)S(1)}, u32[]{:S(2)}, u32[]{:S(2)}) %collective-permute-start.2) | collective-permute-done | bytes 1179680 | tf_op jit(solution)/shard_map/ppermute | solution.py:452
  136.9 11.1 %product_one.1 = (f32[768,768]{1,0:T(8,128)}, f32[768,768]{1,0:T(8,128)}) custom-call(s32[86]{0:T(128)} %concatenate.3.s_ref, f32[768,768]{1,0:T(8,128)} %get-tuple-element.42.p_ref, f32[768,384]{1,0:T(8,128)} %copy-done.12, f32[768,2304]{1,0:T(8,128)} %bitcast.22, f32[768,2304]{1,0:T(8,128)} %bitcast.23), custom_call_target="tpu_custom_call" | custom-call | flops 4000000000 | bytes 22413312 | tf_op jit(solution)/shard_map/product_one/pallas_call | solution.py:40
  148.0 13.8 %coupling_two.1 = (f32[18,128,128]{2,1,0:T(8,128)}, f32[18,128,128]{2,1,0:T(8,128)}, f32[18,128,128]{2,1,0:T(8,128)}, f32[18,128,128]{2,1,0:T(8,128)}) custom-call(s32[86]{0:T(128)} %concatenate.3.s_ref, f32[768,768]{1,0:T(8,128)} %get-tuple-element.44.own_ref, f32[768,768]{1,0:T(8,128)} %get-tuple-element.45.cross_ref, f32[1024,1024]{1,0:T(8,128)} %bitcast.18), custom_call_target="tpu_custom_call" | custom-call | bytes 13631488 | tf_op jit(solution)/shard_map/coupling_two/pallas_call | solution.py:40
  161.8 7.3 %pivot_two.1 = (f32[10,128,128]{2,1,0:T(8,128)}, f32[11,128,128]{2,1,0:T(8,128)}) custom-call(s32[86]{0:T(128)} %concatenate.3.s_ref, f32[768,768]{1,0:T(8,128)} %get-tuple-element.44.own_ref, f32[768,768]{1,0:T(8,128)} %get-tuple-element.45.cross_ref, f32[1024,1024]{1,0:T(8,128)} %bitcast.19, f32[192,768]{1,0:T(8,128)} %bitcast.31), custom_call_target="tpu_custom_call" | custom-call | bytes 10878976 | tf_op jit(solution)/shard_map/pivot_two/pallas_call | solution.py:40
  169.1 3.4 collective-permute-start.5
  172.5 3.6 collective-permute-start.3
  176.1 27.8 %collective-permute-done.5 = f32[11,128,128]{2,1,0:T(8,128)S(1)} collective-permute-done((f32[11,128,128]{2,1,0:T(8,128)}, f32[11,128,128]{2,1,0:T(8,128)S(1)}, u32[]{:S(2)}, u32[]{:S(2)}) %collective-permute-start.5) | collective-permute-done | bytes 720928 | tf_op jit(solution)/shard_map/ppermute | solution.py:452
  205.9 3.2 collective-permute-start.6
  211.5 19.9 %trailing_two.1 = (f32[36,128,128]{2,1,0:T(8,128)}, f32[36,128,128]{2,1,0:T(8,128)}, f32[36,128,128]{2,1,0:T(8,128)}, f32[36,128,128]{2,1,0:T(8,128)}) custom-call(s32[86]{0:T(128)} %concatenate.3.s_ref, f32[768,768]{1,0:T(8,128)} %get-tuple-element.44.own_ref, f32[768,768]{1,0:T(8,128)} %get-tuple-element.45.cross_ref, f32[1024,1024]{1,0:T(8,128)} %bitcast.20), custom_call_target="tpu_custom_call" | custom-call | bytes 18350080 | tf_op jit(solution)/shard_map/trailing_two/pallas_call | solution.py:40
  236.7 2.8 collective-permute-start.10
  239.4 40.7 %factor_two.1 = (f32[192,768]{1,0:T(8,128)}, bf16[768,768]{1,0:T(8,128)(2,1)}, bf16[768,768]{1,0:T(8,128)(2,1)}, bf16[768,128]{1,0:T(8,128)(2,1)}, bf16[768,128]{1,0:T(8,128)(2,1)}) custom-call(s32[86]{0:T(128)} %concatenate.3.s_ref, f32[10,128,128]{2,1,0:T(8,128)} %add.86.refs_0_, f32[10,128,128]{2,1,0:T(8,128)} %collective-permute-done.4.refs_1_, ...), custom_call_target="tpu_custom_call" | custom-call | flops 20000000000 | bytes 8847360 | tf_op jit(solution)/shard_map/factor_two/pallas_call | solution.py:40
  280.1 16.4 %collective-permute-done.8.x2 = f32[9,128,128]{2,1,0:T(8,128)S(1)} collective-permute-done((f32[9,128,128]{2,1,0:T(8,128)}, f32[9,128,128]{2,1,0:T(8,128)S(1)}, u32[]{:S(2)}, u32[]{:S(2)}) %collective-permute-start.8) | collective-permute-done | bytes 589856 | tf_op jit(solution)/shard_map/ppermute | solution.py:452
  297.6 9.6 %panel_two.1.p_ref = f32[384,768]{1,0:T(8,128)} custom-call(s32[86]{0:T(128)} %concatenate.3.s_ref, f32[384,2304]{1,0:T(8,128)} %bitcast.24, f32[18,128,128]{2,1,0:T(8,128)} %get-tuple-element.49.xk, f32[18,128,128]{2,1,0:T(8,128)} %copy-done.8, f32[9,128,128]{2,1,0:T(8,128)} %copy-done.15, f32[18,128,128]{2,1,0:T(8,128)} %get-tuple-element.51.zk, ...), custom_call_target="tpu_custom_call" | custom-call | flops 2000000000 | bytes 16121856 | tf_op jit(solution)/shard_map/panel_two/pallas_call | solution.py:40
  312.1 2.9 collective-permute-start.12
  317.4 23.0 %collective-permute-done.16.pz = f32[384,768]{1,0:T(8,128)S(1)} collective-permute-done((f32[384,768]{1,0:T(8,128)}, f32[384,768]{1,0:T(8,128)S(1)}, u32[]{:S(2)}, u32[]{:S(2)}) %collective-permute-start.16) | collective-permute-done | bytes 1179680 | tf_op jit(solution)/shard_map/ppermute | solution.py:452
  342.4 23.2 %collective-permute-done.12.x2 = f32[18,128,128]{2,1,0:T(8,128)S(1)} collective-permute-done((f32[18,128,128]{2,1,0:T(8,128)S(1)}, f32[18,128,128]{2,1,0:T(8,128)S(1)}, u32[]{:S(2)}, u32[]{:S(2)}) %collective-permute-start.12) | collective-permute-done | bytes 1179680 | tf_op jit(solution)/shard_map/ppermute | solution.py:452
  365.7 5.1 %collective-permute-done.17.pd0 = f32[192,768]{1,0:T(8,128)} collective-permute-done((f32[192,768]{1,0:T(8,128)S(1)}, f32[192,768]{1,0:T(8,128)}, u32[]{:S(2)}, u32[]{:S(2)}) %collective-permute-start.17) | collective-permute-done | bytes 589856 | tf_op jit(solution)/shard_map/ppermute | solution.py:452
  373.1 12.9 %schur_two.1 = f32[384,1536]{1,0:T(8,128)} custom-call(s32[86]{0:T(128)} %concatenate.3.s_ref, f32[384,2304]{1,0:T(8,128)} %bitcast.25, f32[384,2304]{1,0:T(8,128)} %bitcast.26, f32[36,128,128]{2,1,0:T(8,128)} %get-tuple-element.57.xk, f32[36,128,128]{2,1,0:T(8,128)} %collective-permute-done.11.x1, f32[18,128,128]{2,1,0:T(8,128)} %copy-done.10, ...), custom_call_target="tpu_custom_call" | custom-call | flops 3000000000 | bytes 25952256 | tf_op jit(solution)/shard_map/schur_two/pallas_call | solution.py:40
  (79 shorter events, 32.9 us)
Async XLA Ops:
  14.4 34.6 %collective-permute-start = (f32[21,128,128]{2,1,0:T(8,128)}, f32[21,128,128]{2,1,0:T(8,128)S(1)}, u32[]{:S(2)}, u32[]{:S(2)}) collective-permute-start(f32[21,128,128]{2,1,0:T(8,128)} %get-tuple-element.33.refs_0_), channel_id=1, source_target_pairs={{0,64},{8,72},{16,80},{24,88},{32,96},{40,104},{48,112},{56,120},{... | collective-permute-start | bytes 4128776 | tf_op jit(solution)/shard_map/ppermute | solution.py:452
  49.0 43.9 %collective-permute-start.1 = (f32[16,128,128]{2,1,0:T(8,128)}, f32[16,128,128]{2,1,0:T(8,128)S(1)}, u32[]{:S(2)}, u32[]{:S(2)}) collective-permute-start(f32[16,128,128]{2,1,0:T(8,128)} %get-tuple-element.37), channel_id=1, source_target_pairs={{0,64},{8,72},{16,80},{24,88},{32,96},{40,104},{48,112},{56,120},{... | collective-permute-start | bytes 3145736 | tf_op jit(solution)/shard_map/ppermute | solution.py:452
  107.5 28.3 %collective-permute-start.2 = (f32[768,384]{1,0:T(8,128)}, f32[768,384]{1,0:T(8,128)S(1)}, u32[]{:S(2)}, u32[]{:S(2)}) collective-permute-start(f32[768,384]{1,0:T(8,128)} %get-tuple-element.43), channel_id=1, source_target_pairs={{0,64},{8,72},{16,80},{24,88},{32,96},{40,104},{48,112},{56,120},{... | collective-permute-start | bytes 3538952 | tf_op jit(solution)/shard_map/ppermute | solution.py:452
  161.7 70.4 %collective-permute-start.7 = (f32[18,128,128]{2,1,0:T(8,128)}, f32[18,128,128]{2,1,0:T(8,128)S(1)}, u32[]{:S(2)}, u32[]{:S(2)}) collective-permute-start(f32[18,128,128]{2,1,0:T(8,128)} %get-tuple-element.50), channel_id=1, source_target_pairs={{0,4},{1,5},{2,6},{3,7},{4,0},{5,1},{6,2},{7,3},{8,12},{9,13},{10,... | collective-permute-start | bytes 3538952 | tf_op jit(solution)/shard_map/ppermute | solution.py:452
  161.8 73.6 %collective-permute-start.9 = (f32[18,128,128]{2,1,0:T(8,128)}, f32[18,128,128]{2,1,0:T(8,128)S(1)}, u32[]{:S(2)}, u32[]{:S(2)}) collective-permute-start(f32[18,128,128]{2,1,0:T(8,128)} %get-tuple-element.52), channel_id=1, source_target_pairs={{0,64},{8,72},{16,80},{24,88},{32,96},{40,104},{48,112},{56,120},{... | collective-permute-start | bytes 3538952 | tf_op jit(solution)/shard_map/ppermute | solution.py:452
  169.1 40.1 %copy-start.14 = (f32[10,128,128]{2,1,0:T(8,128)S(1)}, f32[10,128,128]{2,1,0:T(8,128)}, u32[]{:S(2)}) copy-start(f32[10,128,128]{2,1,0:T(8,128)} %get-tuple-element.46) | copy-start | bytes 1966084
  169.1 34.8 %collective-permute-start.5 = (f32[11,128,128]{2,1,0:T(8,128)}, f32[11,128,128]{2,1,0:T(8,128)S(1)}, u32[]{:S(2)}, u32[]{:S(2)}) collective-permute-start(f32[11,128,128]{2,1,0:T(8,128)} %get-tuple-element.47), channel_id=1, source_target_pairs={{0,64},{8,72},{16,80},{24,88},{32,96},{40,104},{48,112},{56,120},{... | collective-permute-start | bytes 2162696 | tf_op jit(solution)/shard_map/ppermute | solution.py:452
  172.5 36.7 %collective-permute-start.3 = (f32[10,128,128]{2,1,0:T(8,128)}, f32[10,128,128]{2,1,0:T(8,128)S(1)}, u32[]{:S(2)}, u32[]{:S(2)}) collective-permute-start(f32[10,128,128]{2,1,0:T(8,128)} %get-tuple-element.46), channel_id=1, source_target_pairs={{0,4},{1,5},{2,6},{3,7},{4,0},{5,1},{6,2},{7,3},{8,12},{9,13},{10,... | collective-permute-start | bytes 1966088 | tf_op jit(solution)/shard_map/ppermute | solution.py:452
  205.9 33.5 %collective-permute-start.6 = (f32[11,128,128]{2,1,0:T(8,128)}, f32[11,128,128]{2,1,0:T(8,128)}, u32[]{:S(2)}, u32[]{:S(2)}) collective-permute-start(f32[11,128,128]{2,1,0:T(8,128)} %add.87.refs_2_), channel_id=1, source_target_pairs={{0,4},{1,5},{2,6},{3,7},{4,0},{5,1},{6,2},{7,3},{8,12},{9,13},{10,... | collective-permute-start | bytes 2162696 | tf_op jit(solution)/shard_map/ppermute | solution.py:452
  210.1 24.4 %copy-start.6 = (f32[18,128,128]{2,1,0:T(8,128)S(1)}, f32[18,128,128]{2,1,0:T(8,128)}, u32[]{:S(2)}) copy-start(f32[18,128,128]{2,1,0:T(8,128)} %get-tuple-element.49.xk) | copy-start | bytes 3538948
  210.1 26.5 %collective-permute-start.4 = (f32[10,128,128]{2,1,0:T(8,128)}, f32[10,128,128]{2,1,0:T(8,128)}, u32[]{:S(2)}, u32[]{:S(2)}) collective-permute-start(f32[10,128,128]{2,1,0:T(8,128)} %add.86.refs_0_), channel_id=1, source_target_pairs={{0,64},{8,72},{16,80},{24,88},{32,96},{40,104},{48,112},{56,120},{... | collective-permute-start | bytes 1966088 | tf_op jit(solution)/shard_map/ppermute | solution.py:452
  231.3 79.2 %collective-permute-start.11 = (f32[36,128,128]{2,1,0:T(8,128)}, f32[36,128,128]{2,1,0:T(8,128)}, u32[]{:S(2)}, u32[]{:S(2)}) collective-permute-start(f32[36,128,128]{2,1,0:T(8,128)} %get-tuple-element.58), channel_id=1, source_target_pairs={{0,4},{1,5},{2,6},{3,7},{4,0},{5,1},{6,2},{7,3},{8,12},{9,13},{10,... | collective-permute-start | bytes 7077896 | tf_op jit(solution)/shard_map/ppermute | solution.py:452
  232.1 82.8 %collective-permute-start.13 = (f32[36,128,128]{2,1,0:T(8,128)}, f32[36,128,128]{2,1,0:T(8,128)}, u32[]{:S(2)}, u32[]{:S(2)}) collective-permute-start(f32[36,128,128]{2,1,0:T(8,128)} %get-tuple-element.60), channel_id=1, source_target_pairs={{0,64},{8,72},{16,80},{24,88},{32,96},{40,104},{48,112},{56,120},{... | collective-permute-start | bytes 7077896 | tf_op jit(solution)/shard_map/ppermute | solution.py:452
  235.4 44.8 %copy-start.9 = (f32[18,128,128]{2,1,0:T(8,128)}, f32[18,128,128]{2,1,0:T(8,128)S(1)}, u32[]{:S(2)}) copy-start(f32[18,128,128]{2,1,0:T(8,128)S(1)} %collective-permute-done.9.z1) | copy-start | bytes 3538948
  235.4 61.1 %collective-permute-start.8 = (f32[9,128,128]{2,1,0:T(8,128)}, f32[9,128,128]{2,1,0:T(8,128)S(1)}, u32[]{:S(2)}, u32[]{:S(2)}) collective-permute-start(f32[9,128,128]{2,1,0:T(8,128)} %slice_add_fusion.3), channel_id=1, source_target_pairs={{0,64},{8,72},{16,80},{24,88},{32,96},{40,104},{48,112},{56,120},{... | collective-permute-start | bytes 1769480 | tf_op jit(solution)/shard_map/ppermute | solution.py:452
  236.7 59.9 %collective-permute-start.10 = (f32[9,128,128]{2,1,0:T(8,128)S(1)}, f32[9,128,128]{2,1,0:T(8,128)S(1)}, u32[]{:S(2)}, u32[]{:S(2)}) collective-permute-start(f32[9,128,128]{2,1,0:T(8,128)S(1)} %slice_add_fusion.2), channel_id=1, source_target_pairs={{0,4},{1,5},{2,6},{3,7},{4,0},{5,1},{6,2},{7,3},{8,12},{9,13},{10,... | collective-permute-start | bytes 1769480 | tf_op jit(solution)/shard_map/ppermute | solution.py:452
  297.6 13.0 %copy-start.2 = (f32[36,128,128]{2,1,0:T(8,128)S(1)}, f32[36,128,128]{2,1,0:T(8,128)}, u32[]{:S(2)}) copy-start(f32[36,128,128]{2,1,0:T(8,128)} %get-tuple-element.57.xk) | copy-start | bytes 7077892
  307.1 34.2 %collective-permute-start.15 = (f32[384,768]{1,0:T(8,128)}, f32[384,768]{1,0:T(8,128)S(1)}, u32[]{:S(2)}, u32[]{:S(2)}) collective-permute-start(f32[384,768]{1,0:T(8,128)} %panel_two.1.p_ref), channel_id=1, source_target_pairs={{0,4},{1,5},{2,6},{3,7},{4,0},{5,1},{6,2},{7,3},{8,12},{9,13},{10,... | collective-permute-start | bytes 3538952 | tf_op jit(solution)/shard_map/ppermute | solution.py:452
  309.8 30.6 %collective-permute-start.16 = (f32[384,768]{1,0:T(8,128)}, f32[384,768]{1,0:T(8,128)S(1)}, u32[]{:S(2)}, u32[]{:S(2)}) collective-permute-start(f32[384,768]{1,0:T(8,128)} %panel_two.1.p_ref), channel_id=1, source_target_pairs={{0,64},{8,72},{16,80},{24,88},{32,96},{40,104},{48,112},{56,120},{... | collective-permute-start | bytes 3538952 | tf_op jit(solution)/shard_map/ppermute | solution.py:452
  312.1 53.5 %collective-permute-start.12 = (f32[18,128,128]{2,1,0:T(8,128)S(1)}, f32[18,128,128]{2,1,0:T(8,128)S(1)}, u32[]{:S(2)}, u32[]{:S(2)}) collective-permute-start(f32[18,128,128]{2,1,0:T(8,128)S(1)} %slice_add_fusion.1), channel_id=1, source_target_pairs={{0,64},{8,72},{16,80},{24,88},{32,96},{40,104},{48,112},{56,120},{... | collective-permute-start | bytes 3538952 | tf_op jit(solution)/shard_map/ppermute | solution.py:452
  316.4 49.2 %collective-permute-start.14 = (f32[18,128,128]{2,1,0:T(8,128)S(1)}, f32[18,128,128]{2,1,0:T(8,128)S(1)}, u32[]{:S(2)}, u32[]{:S(2)}) collective-permute-start(f32[18,128,128]{2,1,0:T(8,128)S(1)} %slice_add_fusion), channel_id=1, source_target_pairs={{0,4},{1,5},{2,6},{3,7},{4,0},{5,1},{6,2},{7,3},{8,12},{9,13},{10,... | collective-permute-start | bytes 3538952 | tf_op jit(solution)/shard_map/ppermute | solution.py:452
  340.4 30.3 %collective-permute-start.17 = (f32[192,768]{1,0:T(8,128)S(1)}, f32[192,768]{1,0:T(8,128)}, u32[]{:S(2)}, u32[]{:S(2)}) collective-permute-start(f32[192,768]{1,0:T(8,128)S(1)} %slice.44), channel_id=1, source_target_pairs={{0,4},{1,5},{2,6},{3,7},{4,0},{5,1},{6,2},{7,3},{8,12},{9,13},{10,... | collective-permute-start | bytes 1769480 | tf_op jit(solution)/shard_map/ppermute | solution.py:452
  341.4 31.7 %copy-start.4 = (f32[384,768]{1,0:T(8,128)}, f32[384,768]{1,0:T(8,128)S(1)}, u32[]{:S(2)}) copy-start(f32[384,768]{1,0:T(8,128)S(1)} %collective-permute-done.15.px) | copy-start | bytes 3538948
  341.4 31.7 %collective-permute-start.18 = (f32[192,768]{1,0:T(8,128)S(1)}, f32[192,768]{1,0:T(8,128)}, u32[]{:S(2)}, u32[]{:S(2)}) collective-permute-start(f32[192,768]{1,0:T(8,128)S(1)} %slice.45), channel_id=1, source_target_pairs={{0,64},{8,72},{16,80},{24,88},{32,96},{40,104},{48,112},{56,120},{... | collective-permute-start | bytes 1769480 | tf_op jit(solution)/shard_map/ppermute | solution.py:452
  (13 other events, 53.5 us)

commit v2 on v1

--- a/solution.py
+++ b/solution.py
@@ -68,8 +68,8 @@
         inv_ref[s_ref[first + i]] = i
 
 
-def gather_one_kernel(s_ref, c_ref, p_ref, piv_ref, coup_ref, inv):
-    side = s_ref[SLO]
+def gather_one_kernel(half_lo, s_ref, c_ref, p_ref, piv_ref, coup_ref, inv):
+    side = lax.axis_index("lo") // half_lo
     invert(s_ref, OWN, NC, inv, 18)
 
     def piv_row(r, _):
@@ -184,35 +184,25 @@
         return 0
 
     lax.fori_loop(live, NP, dead, 0)
+    tile_row = lax.broadcasted_iota(jnp.int32, (NP * T, T), 0) // T
 
     def step(k, _):
         s = tl(k)
         d_s[...] = a_s[s, s]
         factor_tile(d_s, w_s, u_s)
-        l_s[s, s] = u_s[...].T
         w = split(w_s[...])
         wh_ref[s, :] = w[0]
         wl_ref[s, :] = w[1]
 
-        def panel(i, _):
-            x = dot3(split(a_s[tl(i), s]), w, NT)
-            l_s[tl(i), s] = x
-            xh, xl = split(x)
-            lh_ref[tl(i), s] = xh
-            ll_ref[tl(i), s] = xl
-            return 0
-
-        lax.fori_loop(k + 1, live, panel, 0)
+        x = dot3(split(a_s[:, s]), w, NT)
+        lh_ref[:, s], ll_ref[:, s] = split(x)
+        l_s[:, s] = jnp.where((tile_row > k) & (tile_row < live), x, 0.0)
+        l_s[s, s] = u_s[...].T
 
         def col(j, _):
             xj = (lh_ref[tl(j), s], ll_ref[tl(j), s])
-
-            def tile(i, _):
-                xi = (lh_ref[tl(i), s], ll_ref[tl(i), s])
-                a_s[tl(i), tl(j)] = a_s[tl(i), tl(j)] - dot3(xi, xj, NT)
-                return 0
-
-            return lax.fori_loop(j, live, tile, 0)
+            a_s[:, tl(j)] = a_s[:, tl(j)] - dot3((lh_ref[:, s], ll_ref[:, s]), xj, NT)
+            return 0
 
         return lax.fori_loop(k + 1, live, col, 0)
 
@@ -258,29 +248,40 @@
             plo[:, s] = jnp.zeros_like(plo[:, s])
 
 
-def panel_one_kernel(
-    s_ref, r_ref, c_ref, got_ref, lh, ll, wh, wl, p_ref, send_ref, ph, plo, inv, inv2
-):
+def couple_one_kernel(s_ref, r_ref, c_ref, x_ref, inv):
     side = s_ref[SLO]
     invert(s_ref, OWN, NC, inv, 18)
-    invert(s_ref, OTH, NC, inv2, 18)
-
-    def tile(t, count):
+
+    def tile(t, _):
         r = t // NP
         c = t % NP
         dst = (tl(r), tl(c))
         row = NP + side * 6 + r
-        p_ref[dst] = r_ref[dst] * s_ref[FILL1 + t].astype(f32)
+        x_ref[dst] = r_ref[dst] * s_ref[FILL1 + t].astype(f32)
 
         @pl.when((inv[row] >= 0) & (inv[c] >= 0))
         def _():
-            p_ref[dst] += c_ref[tl(inv[row]), tl(inv[c])]
-
+            x_ref[dst] += c_ref[tl(inv[row]), tl(inv[c])]
+
+        return 0
+
+    lax.fori_loop(0, 36, tile, 0)
+
+
+def panel_one_kernel(s_ref, x_ref, got_ref, lh, ll, wh, wl, p_ref, send_ref, ph, plo, inv2):
+    side = s_ref[SLO]
+    invert(s_ref, OTH, NC, inv2, 18)
+    p_ref[...] = x_ref[...]
+
+    def tile(t, count):
+        r = t // NP
+        c = t % NP
+        row = NP + side * 6 + r
         hit = (inv2[row] >= 0) & (inv2[c] >= 0)
 
         @pl.when(hit)
         def _():
-            p_ref[dst] += got_ref[count]
+            p_ref[tl(r), tl(c)] += got_ref[count]
 
         return count + hit.astype(jnp.int32)
 
@@ -289,18 +290,13 @@
     send_ref[...] = p_ref[:, pl.ds(pl.multiple_of((1 - side) * 384, T), 384)]
 
 
-def product_kernel(s_ref, p_ref, q_ref, t0_ref, t1_ref, own_ref, cross_ref, ph, plo):
+def own_kernel(s_ref, p_ref, t0_ref, t1_ref, own_ref, ph, plo):
     side = s_ref[SLO]
     ph[...], plo[...] = split(p_ref[...])
-    qh, ql = split(q_ref[...])
-    mine = pl.ds(pl.multiple_of(side * 384, T), 384)
-    pc = (ph[:, mine], plo[:, mine])
     for n in range(3):
         s = slice(n * 256, n * 256 + 256)
         base = jnp.where(side == 0, t0_ref[:, s], t1_ref[:, s])
         own_ref[:, s] = base - dot3((ph[...], plo[...]), (ph[s, :], plo[s, :]), NT)
-        base = jnp.where(side == 0, t1_ref[:, s], 0.0)
-        cross_ref[:, s] = base - dot3(pc, (qh[s, :], ql[s, :]), NT)
 
 
 def source_tile(side, inv, inv2, own_ref, cross_ref, c_ref, out_ref, at, r, c):
@@ -338,13 +334,22 @@
         out_ref[at] += c_ref[tl(ci), tl(cj)]
 
 
-def pivot_two_kernel(s_ref, own_ref, cross_ref, c_ref, p_ref, a_ref, b_ref, wide, inv, inv2):
+def cross_kernel(
+    s_ref, p_ref, q_ref, t1_ref, own_ref, c_ref, pv_ref, cross_ref, a_ref, b_ref, wide, inv, inv2
+):
     side = s_ref[SLO]
     quarter = 2 * s_ref[SHI] + side
+    mine = pl.ds(pl.multiple_of(side * 384, T), 384)
+    pc = split(p_ref[:, mine])
+    qh, ql = split(q_ref[...])
+    for n in range(3):
+        s = slice(n * 256, n * 256 + 256)
+        base = jnp.where(side == 0, t1_ref[:, s], 0.0)
+        cross_ref[:, s] = base - dot3(pc, (qh[s, :], ql[s, :]), NT)
     invert(s_ref, OWN, NC, inv, 18)
     invert(s_ref, MAP2, NU, inv2, 18)
     wide[...] = jnp.zeros_like(wide)
-    wide[pl.ds(pl.multiple_of((quarter % 2) * 64, 64), 192), :] = p_ref[...]
+    wide[pl.ds(pl.multiple_of((quarter % 2) * 64, 64), 192), :] = pv_ref[...]
     base = (3 * quarter) // 2
 
     def emit(out_ref, first, row):
@@ -405,6 +410,58 @@
     )
 
 
+NINE = [(r, c) for r in range(3) for c in range(3)]
+DX, DZ = [(0, 0), (1, 0), (1, 1)], [(2, 0), (2, 1), (2, 2)]
+GX, GZ = NINE[:4], NINE[4:]
+
+
+def chain_x(m, x, z, d):
+    return (
+        [(z, z, t) for t in DX]
+        + [(z, x, t) for t in GX]
+        + [(m, z, t) for t in NINE]
+        + [(m, m, t) for t in DX]
+        + [(m, d, t) for t in GX]
+    )
+
+
+def chain_z(m, x, z, d):
+    return (
+        [(x, x, t) for t in DZ]
+        + [(x, z, t) for t in GZ]
+        + [(m, x, t) for t in NINE]
+        + [(m, m, t) for t in DZ]
+        + [(m, d, t) for t in GZ]
+    )
+
+
+def trailing_two_kernel(
+    s_ref, own_ref, cross_ref, c_ref, xs, xk, zs, zk, inv, inv2, rtab, ctab
+):
+    lo = s_ref[SLO]
+    hi = s_ref[SHI]
+    invert(s_ref, OWN, NC, inv, 18)
+    invert(s_ref, MAP2, NU, inv2, 18)
+    m, x, z, d = (
+        NP + 3 * (2 * a + b) for a, b in ((hi, lo), (1 - hi, lo), (hi, 1 - lo), (1 - hi, 1 - lo))
+    )
+    for out_ref, tiles in (
+        (xs, chain_x(x, m, d, z)),
+        (xk, chain_x(m, x, z, d)),
+        (zs, chain_z(z, d, m, x)),
+        (zk, chain_z(m, x, z, d)),
+    ):
+        for n, (rq, cq, (r, c)) in enumerate(tiles):
+            rtab[n] = rq + r
+            ctab[n] = cq + c
+
+        def tile(t, _):
+            source_tile(lo, inv, inv2, own_ref, cross_ref, c_ref, out_ref, t, rtab[t], ctab[t])
+            return 0
+
+        lax.fori_loop(0, len(tiles), tile, 0)
+
+
 def panel_two_kernel(
     s_ref, r_ref, xk, x1, x2, zk, z1, z2, lh, ll, wh, wl, p_ref, ph, plo
 ):
@@ -420,31 +477,51 @@
     solve(p_ref, s_ref[LIVE2], lh, ll, wh, wl, ph, plo)
 
 
-def schur_kernel(
-    s_ref, t0_ref, t1_ref, xk, x1, x2, zk, z1, z2, p_ref, px, pz, pd0, pd1, out_ref
-):
+def schur_base_kernel(s_ref, r_ref, p_ref, xk, x1, x2, zk, z1, z2, out_ref):
     hi = s_ref[SHI]
     lo = s_ref[SLO]
-    for r in range(3):
-        for c in range(6):
-            t = 6 * r + c
-            rows = slice(r * T, r * T + T)
-            cols = slice(c * T, c * T + T)
-            out_ref[rows, cols] = t0_ref[rows, cols] + ((xk[18 + t] + x1[18 + t]) + x2[t])
-            right = slice(768 + c * T, 768 + c * T + T)
-            out_ref[rows, right] = t1_ref[rows, cols] + ((zk[18 + t] + z1[18 + t]) + z2[t])
+    out_ref[...] = r_ref[:, NP * T :]
+    m, x, z, d = (
+        3 * (2 * a + b) for a, b in ((hi, lo), (1 - hi, lo), (hi, 1 - lo), (1 - hi, 1 - lo))
+    )
     mine = split(p_ref[...])
-
-    def minus(a, b, skip, size, ref):
-        cols = pl.ds(pl.multiple_of((2 * a + b) * 384 + skip, 64), size)
-        return cols, dot3(mine, split(ref[...]), NT)
-
-    for a, b, ref in ((hi, lo, p_ref), (1 - hi, lo, px), (hi, 1 - lo, pz)):
+    cols = pl.ds(pl.multiple_of(m * T, T), 384)
+    out_ref[:, cols] = out_ref[:, cols] - dot3(mine, mine, NT)
+
+    def add(quarter, r, c, value):
+        out_ref[r * T : r * T + T, tl(quarter + c)] += value
+
+    for k, r1, r2, diag, cross, pair in ((xk, x1, x2, DX, GX, z), (zk, z1, z2, DZ, GZ, x)):
+        nd = len(diag)
+        ng = len(cross)
+        base = nd + ng + 9
+        for n, (r, c) in enumerate(diag):
+            v = (k[base + n] + r1[base + n]) + r2[n]
+            add(m, r, c, v)
+            if r != c:
+                add(m, c, r, v.T)
+        for n, (r, c) in enumerate(cross):
+            v = (k[base + nd + n] + r1[base + nd + n]) + r2[nd + n]
+            add(d, r, c, v)
+        for n, (r, c) in enumerate(NINE):
+            v = (k[nd + ng + n] + r1[nd + ng + n]) + r2[nd + ng + 3 * c + r].T
+            add(pair, r, c, v)
+
+
+def schur_kernel(s_ref, b_ref, p_ref, px, pz, pd0, pd1, out_ref):
+    hi = s_ref[SHI]
+    lo = s_ref[SLO]
+    mine = split(p_ref[...])
+
+    def minus(a, b, other):
         cols = pl.ds(pl.multiple_of((2 * a + b) * 384, T), 384)
-        out_ref[:, cols] = out_ref[:, cols] - dot3(mine, split(ref[...]), NT)
-    diag = jnp.concatenate([pd0[...], pd1[...]], axis=0)
-    cols = pl.ds(pl.multiple_of((2 * (1 - hi) + 1 - lo) * 384, T), 384)
-    out_ref[:, cols] = out_ref[:, cols] - dot3(mine, split(diag), NT)
+        out_ref[:, cols] = b_ref[:, cols] - dot3(mine, split(other), NT)
+
+    minus(1 - hi, lo, px[...])
+    minus(hi, 1 - lo, pz[...])
+    minus(1 - hi, 1 - lo, jnp.concatenate([pd0[...], pd1[...]], axis=0))
+    cols = pl.ds(pl.multiple_of((2 * hi + lo) * 384, T), 384)
+    out_ref[:, cols] = b_ref[:, cols]
 
 
 def across(axis, values):
@@ -477,6 +554,24 @@
     front_hi = hi % half_hi
     quarter = 2 * side_hi + side_lo
     i32 = jnp.int32
+    c = contribution[0, 0]
+    rows1 = rows_one[0, 0]
+    rows2 = rows_two_in[0, 0]
+    smem = pltpu.SMEM((18,), i32)
+    n = NP * T
+
+    piv, coup = call(
+        functools.partial(gather_one_kernel, half_lo),
+        [map_one[hi, lo], c, pivot_one[0, 0]],
+        [None, None],
+        [shape(21, T, T), shape(16, T, T)],
+        [smem],
+        "gather_one",
+    )
+    piv, map_one, map_two, fill_one, fill_two, live_one, live_two = lax.optimization_barrier(
+        (piv, map_one, map_two, fill_one, fill_two, live_one, live_two)
+    )
+    piv_got = across("lo", piv)
     scalars = jnp.concatenate(
         [
             map_one[hi, lo],
@@ -489,21 +584,14 @@
             lax.dynamic_slice_in_dim(fill_two[front_hi, front_lo], quarter * 3, 3, 0).reshape(18),
         ]
     )
-    c = contribution[0, 0]
-    rows1 = rows_one[0, 0]
-    rows2 = rows_two_in[0, 0]
-    smem = pltpu.SMEM((18,), i32)
-    n = NP * T
-
-    piv, coup = call(
-        gather_one_kernel,
-        [scalars, c, pivot_one[0, 0]],
-        [None, None],
-        [shape(21, T, T), shape(16, T, T)],
+    (x_one,) = call(
+        couple_one_kernel,
+        [scalars, rows1, c],
+        [block(n, n, 0), None],
+        [shape(n, n)],
         [smem],
-        "gather_one",
-    )
-    piv_got = across("lo", piv)
+        "couple_one",
+    )
     coup, piv_got = lax.optimization_barrier((coup, piv_got))
     coup_got = across("lo", coup)
     lower_one, *fac1 = factor(
@@ -511,45 +599,53 @@
     )
     panel_one, send = call(
         panel_one_kernel,
-        [scalars, rows1, c, coup_got, *fac1],
-        [block(n, n, 0)] + [None] * 6,
+        [scalars, x_one, coup_got, *fac1],
+        [None] * 6,
         [shape(n, n), shape(n, n // 2)],
-        [pltpu.VMEM((n, n), bf16)] * 2 + [smem] * 2,
+        [pltpu.VMEM((n, n), bf16)] * 2 + [smem],
         "panel_one",
         flops=3_000_000_000,
     )
     got = across("lo", send)
-    own, cross = call(
-        product_kernel,
-        [scalars, panel_one, got, rows1, rows1],
-        [None, None, block(n, n, 1), block(n, n, 2)],
-        [shape(n, n), shape(n, n)],
+    (own,) = call(
+        own_kernel,
+        [scalars, panel_one, rows1, rows1],
+        [None, block(n, n, 1), block(n, n, 2)],
+        [shape(n, n)],
         [pltpu.VMEM((n, n), bf16)] * 2,
-        "product_one",
+        "own_one",
         flops=4_000_000_000,
     )
-    pa, pb = call(
-        pivot_two_kernel,
-        [scalars, own, cross, c, pivot_two[0, 0]],
-        [None] * 4,
-        [shape(10, T, T), shape(11, T, T)],
+    cross, pa, pb = call(
+        cross_kernel,
+        [scalars, panel_one, got, rows1, own, c, pivot_two[0, 0]],
+        [None, None, block(n, n, 2), None, None, None],
+        [shape(n, n), shape(10, T, T), shape(11, T, T)],
         [pltpu.VMEM((2 * T, n), f32), smem, smem],
-        "pivot_two",
+        "cross_one",
+        flops=2_000_000_000,
     )
     pa1 = across("hi", pa)
     pb1 = across("lo", pb)
+    pa, pb, cross = lax.optimization_barrier((pa, pb, cross))
     cxs, cxk, czs, czk = rows_two(scalars, own, cross, c, 0, NP, "coupling_two")
+    pa = pa + pa1
+    pb = pb + pb1
+    pa, pb, cxs, czs = lax.optimization_barrier((pa, pb, cxs, czs))
+    pa2 = across("lo", pa)
+    pb2 = across("hi", pb)
     cx1 = across("hi", cxs)
     cz1 = across("lo", czs)
-    pa = pa + pa1
-    pb = pb + pb1
-    pa2 = across("lo", pa)
-    pb2 = across("hi", pb)
-    txs, txk, tzs, tzk = rows_two(scalars, own, cross, c, NP, NU, "trailing_two")
+    txs, txk, tzs, tzk = call(
+        trailing_two_kernel,
+        [scalars, own, cross, c],
+        [None] * 3,
+        [shape(23, T, T)] * 2 + [shape(25, T, T)] * 2,
+        [smem, smem] + [pltpu.SMEM((32,), i32)] * 2,
+        "trailing_two",
+    )
     tx1 = across("hi", txs)
     tz1 = across("lo", tzs)
-    cx2 = across("lo", cxk[:9] + cx1[:9])
-    cz2 = across("hi", czk[:9] + cz1[:9])
     lower_two, *fac2 = factor(
         scalars,
         [(pa, pa2), (pb, pb2)],
@@ -558,6 +654,8 @@
         192,
         "factor_two",
     )
+    cx2 = across("lo", cxk[:9] + cx1[:9])
+    cz2 = across("hi", czk[:9] + cz1[:9])
     (panel_two,) = call(
         panel_two_kernel,
         [scalars, rows2, cxk, cx1, cx2, czk, cz1, cz2, *fac2],
@@ -567,16 +665,25 @@
         "panel_two",
         flops=2_000_000_000,
     )
-    tx2 = across("lo", txk[:18] + tx1[:18])
-    tz2 = across("hi", tzk[:18] + tz1[:18])
+    tx2 = across("lo", txk[:16] + tx1[:16])
+    tz2 = across("hi", tzk[:17] + tz1[:17])
     px = across("hi", panel_two)
     pz = across("lo", panel_two)
     pd0 = across("hi", pz[:192])
     pd1 = across("lo", px[192:])
+    (base_two,) = call(
+        schur_base_kernel,
+        [scalars, rows2, panel_two, txk, tx1, tx2, tzk, tz1, tz2],
+        [None] * 8,
+        [shape(384, NU * T)],
+        [],
+        "schur_base",
+        flops=1_000_000_000,
+    )
     (schur_two,) = call(
         schur_kernel,
-        [scalars, rows2, rows2, txk, tx1, tx2, tzk, tz1, tz2, panel_two, px, pz, pd0, pd1],
-        [block(384, n, 1), block(384, n, 2)] + [None] * 11,
+        [scalars, base_two, panel_two, px, pz, pd0, pd1],
+        [None] * 6,
         [shape(384, NU * T)],
         [],
         "schur_two",

time: 386 us -> 330 us (0.85)
  the two profiles are of different devices: /device:TPU:0 before, /device:TPU:34 now
where the time goes in v2:
time: 330 us; the launch traced here: 328 us
  Pallas kernels  157 us (48%)
  waiting for transfers between devices  97.1 us (29%)
  starting transfers between devices  53.6 us (16%)
  local copies, waits for them, and re-layouts  14.6 us (4%)
  other arithmetic  5.57 us (2%)
    pallas_call x12, Pallas kernels, call(): pl.pallas_call(kernel, grid_spec=pltpu.PrefetchScalarGridSpec(num_scalar_...  157 us
    ppermute x19, waiting for transfers between devices, across(): return lax.ppermute(values, axis, [(i, i ^ size // 2) for i in range(size)])  97.1 us
    ppermute x19, starting transfers between devices, across(): return lax.ppermute(values, axis, [(i, i ^ size // 2) for i in range(size)])  53.6 us
  transfers between devices with their start and end apart: 19, of which 10 were waited for; matrix products, arithmetic and copies ran while one was open for 4% of the time, Pallas kernels for 37%

profile of v2, /device:TPU:34, one launch (start us, length us, event | category | flops | bytes accessed | tf_op | source)
XLA Modules:
  0.0 328.4 jit_solution(17695627472670747157)
XLA Ops:
  2.1 6.4 %gather_one.1 = (f32[21,128,128]{2,1,0:T(8,128)}, f32[16,128,128]{2,1,0:T(8,128)}) custom-call(s32[8]{0:T(128)} %dynamic-slice_reduce_fusion.2.s_ref, f32[1024,1024]{1,0:T(8,128)} %bitcast.20, f32[384,768]{1,0:T(8,128)} %bitcast.29), custom_call_target="tpu_custom_call" | custom-call | bytes 7798784 | tf_op jit(solution)/shard_map/gather_one/pallas_call | solution.py:40
  8.5 3.1 collective-permute-start
  18.9 6.1 %couple_one.1.x_ref = f32[768,768]{1,0:T(8,128)} custom-call(s32[86]{0:T(128)} %concatenate.3.s_ref, f32[768,2304]{1,0:T(8,128)} %bitcast.16, f32[1024,1024]{1,0:T(8,128)} %bitcast.21), custom_call_target="tpu_custom_call" | custom-call | bytes 13631488 | tf_op jit(solution)/shard_map/couple_one/pallas_call | solution.py:40
  24.9 17.2 %collective-permute-done.refs_1_ = f32[21,128,128]{2,1,0:T(8,128)S(1)} collective-permute-done((f32[21,128,128]{2,1,0:T(8,128)}, f32[21,128,128]{2,1,0:T(8,128)S(1)}, u32[]{:S(2)}, u32[]{:S(2)}) %collective-permute-start) | collective-permute-done | bytes 1376288 | tf_op jit(solution)/shard_map/ppermute | solution.py:529
  42.1 3.0 collective-permute-start.1
  45.1 25.0 %factor_one.1 = (f32[384,768]{1,0:T(8,128)}, bf16[768,768]{1,0:T(8,128)(2,1)}, bf16[768,768]{1,0:T(8,128)(2,1)}, bf16[768,128]{1,0:T(8,128)(2,1)}, bf16[768,128]{1,0:T(8,128)(2,1)}) custom-call(s32[86]{0:T(128)} %concatenate.3.s_ref, f32[21,128,128]{2,1,0:T(8,128)} %get-tuple-element.53.refs_0_, f32[21,128,128]{2,1,0:T(8,128)} %copy-done.17), custom_call_target="tpu_custom_call" | custom-call | flops 20000000000 | bytes 9437184 | tf_op jit(solution)/shard_map/factor_one/pallas_call | solution.py:40
  70.1 9.7 %panel_one.1 = (f32[768,768]{1,0:T(8,128)}, f32[768,384]{1,0:T(8,128)}) custom-call(s32[86]{0:T(128)} %concatenate.3.s_ref, f32[768,768]{1,0:T(8,128)} %couple_one.1.x_ref, f32[16,128,128]{2,1,0:T(8,128)} %collective-permute-done.1.got_ref, bf16[768,768]{1,0:T(8,128)(2,1)} %get-tuple-element.58.lh, bf16[768,768]{1,0:T(8,128)(2,1)} %get-tuple-element.59.ll, ...), custom_call_target="tpu_custom_call" | custom-call | flops 3000000000 | bytes 12451840 | tf_op jit(solution)/shard_map/panel_one/pallas_call | solution.py:40
  80.9 8.1 %own_one.1.own_ref = f32[768,768]{1,0:T(8,128)} custom-call(s32[86]{0:T(128)} %concatenate.3.s_ref, f32[768,768]{1,0:T(8,128)} %get-tuple-element.62.p_ref, f32[768,2304]{1,0:T(8,128)} %bitcast.17, f32[768,2304]{1,0:T(8,128)} %bitcast.18), custom_call_target="tpu_custom_call" | custom-call | flops 4000000000 | bytes 18874368 | tf_op jit(solution)/shard_map/own_one/pallas_call | solution.py:40
  89.0 16.6 %collective-permute-done.2.q_ref = f32[768,384]{1,0:T(8,128)S(1)} collective-permute-done((f32[768,384]{1,0:T(8,128)}, f32[768,384]{1,0:T(8,128)S(1)}, u32[]{:S(2)}, u32[]{:S(2)}) %collective-permute-start.2) | collective-permute-done | bytes 1179680 | tf_op jit(solution)/shard_map/ppermute | solution.py:529
  106.7 10.8 %cross_one.1 = (f32[768,768]{1,0:T(8,128)}, f32[10,128,128]{2,1,0:T(8,128)}, f32[11,128,128]{2,1,0:T(8,128)}) custom-call(s32[86]{0:T(128)} %concatenate.3.s_ref, f32[768,768]{1,0:T(8,128)} %get-tuple-element.62.p_ref, f32[768,384]{1,0:T(8,128)} %copy-done.8, f32[768,2304]{1,0:T(8,128)} %bitcast.19, f32[768,768]{1,0:T(8,128)} %own_one.1.own_ref, ...), custom_call_target="tpu_custom_call" | custom-call | flops 2000000000 | bytes 21495808 | tf_op jit(solution)/shard_map/cross_one/pallas_call | solution.py:40
  118.4 19.9 %collective-permute-start.3 = (f32[10,128,128]{2,1,0:T(8,128)}, f32[10,128,128]{2,1,0:T(8,128)S(1)}, u32[]{:S(2)}, u32[]{:S(2)}) collective-permute-start(f32[10,128,128]{2,1,0:T(8,128)} %get-tuple-element.67), channel_id=1, source_target_pairs={{0,4},{1,5},{2,6},{3,7},{4,0},{5,1},{6,2},{7,3},{8,12},{9,13},{10,... | collective-permute-start | bytes 1966088 | tf_op jit(solution)/shard_map/ppermute | solution.py:529
  138.2 13.0 %coupling_two.1 = (f32[18,128,128]{2,1,0:T(8,128)}, f32[18,128,128]{2,1,0:T(8,128)}, f32[18,128,128]{2,1,0:T(8,128)}, f32[18,128,128]{2,1,0:T(8,128)}) custom-call(s32[86]{0:T(128)} %concatenate.3.s_ref, f32[768,768]{1,0:T(8,128)} %own_one.1.own_ref, f32[768,768]{1,0:T(8,128)} %get-tuple-element.69.cross_ref, f32[1024,1024]{1,0:T(8,128)} %bitcast.23), custom_call_target="tpu_custom_call" | custom-call | bytes 13631488 | tf_op jit(solution)/shard_map/coupling_two/pallas_call | solution.py:40
  152.5 3.3 %collective-permute-start.7 = (f32[18,128,128]{2,1,0:T(8,128)}, f32[18,128,128]{2,1,0:T(8,128)S(1)}, u32[]{:S(2)}, u32[]{:S(2)}) collective-permute-start(f32[18,128,128]{2,1,0:T(8,128)} %get-tuple-element.76), channel_id=1, source_target_pairs={{0,4},{1,5},{2,6},{3,7},{4,0},{5,1},{6,2},{7,3},{8,12},{9,13},{10,... | collective-permute-start | bytes 3538952 | tf_op jit(solution)/shard_map/ppermute | solution.py:529
  159.6 14.2 %trailing_two.1 = (f32[23,128,128]{2,1,0:T(8,128)}, f32[23,128,128]{2,1,0:T(8,128)}, f32[25,128,128]{2,1,0:T(8,128)}, f32[25,128,128]{2,1,0:T(8,128)}) custom-call(s32[86]{0:T(128)} %concatenate.3.s_ref, f32[768,768]{1,0:T(8,128)} %own_one.1.own_ref, f32[768,768]{1,0:T(8,128)} %get-tuple-element.69.cross_ref, f32[1024,1024]{1,0:T(8,128)} %bitcast.24), custom_call_target="tpu_custom_call" | custom-call | bytes 15204352 | tf_op jit(solution)/shard_map/trailing_two/pallas_call | solution.py:40
  173.8 4.0 %collective-permute-start.11 = (f32[23,128,128]{2,1,0:T(8,128)}, f32[23,128,128]{2,1,0:T(8,128)}, u32[]{:S(2)}, u32[]{:S(2)}) collective-permute-start(f32[23,128,128]{2,1,0:T(8,128)} %get-tuple-element.84), channel_id=1, source_target_pairs={{0,4},{1,5},{2,6},{3,7},{4,0},{5,1},{6,2},{7,3},{8,12},{9,13},{10,... | collective-permute-start | bytes 4521992 | tf_op jit(solution)/shard_map/ppermute | solution.py:529
  177.8 5.3 %collective-permute-done.7.x1 = f32[18,128,128]{2,1,0:T(8,128)S(1)} collective-permute-done((f32[18,128,128]{2,1,0:T(8,128)}, f32[18,128,128]{2,1,0:T(8,128)S(1)}, u32[]{:S(2)}, u32[]{:S(2)}) %collective-permute-start.7) | collective-permute-done | bytes 1179680 | tf_op jit(solution)/shard_map/ppermute | solution.py:529
  190.7 9.8 %collective-permute-done.5.refs_1_ = f32[10,128,128]{2,1,0:T(8,128)} collective-permute-done((f32[10,128,128]{2,1,0:T(8,128)}, f32[10,128,128]{2,1,0:T(8,128)}, u32[]{:S(2)}, u32[]{:S(2)}) %collective-permute-start.5) | collective-permute-done | bytes 655392 | tf_op jit(solution)/shard_map/ppermute | solution.py:529
  200.8 37.1 %factor_two.1 = (f32[192,768]{1,0:T(8,128)}, bf16[768,768]{1,0:T(8,128)(2,1)}, bf16[768,768]{1,0:T(8,128)(2,1)}, bf16[768,128]{1,0:T(8,128)(2,1)}, bf16[768,128]{1,0:T(8,128)(2,1)}) custom-call(s32[86]{0:T(128)} %concatenate.3.s_ref, f32[10,128,128]{2,1,0:T(8,128)} %add.88.refs_0_, f32[10,128,128]{2,1,0:T(8,128)} %collective-permute-done.5.refs_1_, ...), custom_call_target="tpu_custom_call" | custom-call | flops 20000000000 | bytes 8847360 | tf_op jit(solution)/shard_map/factor_two/pallas_call | solution.py:40
  237.9 6.2 %collective-permute-done.8.x2 = f32[9,128,128]{2,1,0:T(8,128)S(1)} collective-permute-done((f32[9,128,128]{2,1,0:T(8,128)}, f32[9,128,128]{2,1,0:T(8,128)S(1)}, u32[]{:S(2)}, u32[]{:S(2)}) %collective-permute-start.8) | collective-permute-done | bytes 589856 | tf_op jit(solution)/shard_map/ppermute | solution.py:529
  245.0 9.6 %panel_two.1.p_ref = f32[384,768]{1,0:T(8,128)} custom-call(s32[86]{0:T(128)} %concatenate.3.s_ref, f32[384,2304]{1,0:T(8,128)} %bitcast.25, f32[18,128,128]{2,1,0:T(8,128)} %get-tuple-element.75.xk, f32[18,128,128]{2,1,0:T(8,128)} %copy-done.7, f32[9,128,128]{2,1,0:T(8,128)} %copy-done.14, f32[18,128,128]{2,1,0:T(8,128)} %get-tuple-element.77.zk, ...), custom_call_target="tpu_custom_call" | custom-call | flops 2000000000 | bytes 16121856 | tf_op jit(solution)/shard_map/panel_two/pallas_call | solution.py:40
  264.3 20.9 %collective-permute-done.16.pz = f32[384,768]{1,0:T(8,128)S(1)} collective-permute-done((f32[384,768]{1,0:T(8,128)}, f32[384,768]{1,0:T(8,128)S(1)}, u32[]{:S(2)}, u32[]{:S(2)}) %collective-permute-start.16) | collective-permute-done | bytes 1179680 | tf_op jit(solution)/shard_map/ppermute | solution.py:529
  289.0 18.5 %collective-permute-done.12.x2 = f32[16,128,128]{2,1,0:T(8,128)S(1)} collective-permute-done((f32[16,128,128]{2,1,0:T(8,128)S(1)}, f32[16,128,128]{2,1,0:T(8,128)S(1)}, u32[]{:S(2)}, u32[]{:S(2)}) %collective-permute-start.12) | collective-permute-done | bytes 1048608 | tf_op jit(solution)/shard_map/ppermute | solution.py:529
  310.8 8.6 %schur_base.1.b_ref = f32[384,1536]{1,0:T(8,128)} custom-call(s32[86]{0:T(128)} %concatenate.3.s_ref, f32[384,2304]{1,0:T(8,128)} %bitcast.26, f32[384,768]{1,0:T(8,128)} %panel_two.1.p_ref, f32[23,128,128]{2,1,0:T(8,128)} %get-tuple-element.83.xk, f32[23,128,128]{2,1,0:T(8,128)} %collective-permute-done.11.x1, f32[16,128,128]{2,1,0:T(8,128)} %copy-done.10, ...), custom_call_target="tpu_custom_call" | custom-call | flops 1000000000 | bytes 15532032 | tf_op jit(solution)/shard_map/schur_base/pallas_call | solution.py:40
  320.2 8.2 %schur_two.1 = f32[384,1536]{1,0:T(8,128)} custom-call(s32[86]{0:T(128)} %concatenate.3.s_ref, f32[384,1536]{1,0:T(8,128)} %schur_base.1.b_ref, f32[384,768]{1,0:T(8,128)} %panel_two.1.p_ref, f32[384,768]{1,0:T(8,128)} %copy-done.16, f32[384,768]{1,0:T(8,128)} %copy-done.15, f32[192,768]{1,0:T(8,128)} %copy-done.19, f32[192,768]{1,0:T(8,128)} %collective-permute-done.18.pd1), custom_call_target="tpu_custom_call" | custom-call | flops 3000000000 | bytes 9437184 | tf_op jit(solution)/shard_map/schur_two/pallas_call | solution.py:40
  (86 shorter events, 43.1 us)
Async XLA Ops:
  8.5 33.6 %collective-permute-start = (f32[21,128,128]{2,1,0:T(8,128)}, f32[21,128,128]{2,1,0:T(8,128)S(1)}, u32[]{:S(2)}, u32[]{:S(2)}) collective-permute-start(f32[21,128,128]{2,1,0:T(8,128)} %get-tuple-element.53.refs_0_), channel_id=1, source_target_pairs={{0,64},{8,72},{16,80},{24,88},{32,96},{40,104},{48,112},{56,120},{... | collective-permute-start | bytes 4128776 | tf_op jit(solution)/shard_map/ppermute | solution.py:529
  18.9 23.2 %copy-start.18 = (f32[16,128,128]{2,1,0:T(8,128)S(1)}, f32[16,128,128]{2,1,0:T(8,128)}, u32[]{:S(2)}) copy-start(f32[16,128,128]{2,1,0:T(8,128)} %get-tuple-element.57) | copy-start | bytes 3145732
  42.1 28.0 %collective-permute-start.1 = (f32[16,128,128]{2,1,0:T(8,128)S(1)}, f32[16,128,128]{2,1,0:T(8,128)}, u32[]{:S(2)}, u32[]{:S(2)}) collective-permute-start(f32[16,128,128]{2,1,0:T(8,128)S(1)} %copy-done.18), channel_id=1, source_target_pairs={{0,64},{8,72},{16,80},{24,88},{32,96},{40,104},{48,112},{56,120},{... | collective-permute-start | bytes 3145736 | tf_op jit(solution)/shard_map/ppermute | solution.py:529
  79.8 25.9 %collective-permute-start.2 = (f32[768,384]{1,0:T(8,128)}, f32[768,384]{1,0:T(8,128)S(1)}, u32[]{:S(2)}, u32[]{:S(2)}) collective-permute-start(f32[768,384]{1,0:T(8,128)} %get-tuple-element.63), channel_id=1, source_target_pairs={{0,64},{8,72},{16,80},{24,88},{32,96},{40,104},{48,112},{56,120},{... | collective-permute-start | bytes 3538952 | tf_op jit(solution)/shard_map/ppermute | solution.py:529
  117.5 34.8 %collective-permute-start.4 = (f32[11,128,128]{2,1,0:T(8,128)}, f32[11,128,128]{2,1,0:T(8,128)S(1)}, u32[]{:S(2)}, u32[]{:S(2)}) collective-permute-start(f32[11,128,128]{2,1,0:T(8,128)} %get-tuple-element.68), channel_id=1, source_target_pairs={{0,64},{8,72},{16,80},{24,88},{32,96},{40,104},{48,112},{56,120},{... | collective-permute-start | bytes 2162696 | tf_op jit(solution)/shard_map/ppermute | solution.py:529
  118.4 33.1 %collective-permute-start.3 = (f32[10,128,128]{2,1,0:T(8,128)}, f32[10,128,128]{2,1,0:T(8,128)S(1)}, u32[]{:S(2)}, u32[]{:S(2)}) collective-permute-start(f32[10,128,128]{2,1,0:T(8,128)} %get-tuple-element.67), channel_id=1, source_target_pairs={{0,4},{1,5},{2,6},{3,7},{4,0},{5,1},{6,2},{7,3},{8,12},{9,13},{10,... | collective-permute-start | bytes 1966088 | tf_op jit(solution)/shard_map/ppermute | solution.py:529
  152.5 21.4 %copy-start.11 = (f32[11,128,128]{2,1,0:T(8,128)}, f32[11,128,128]{2,1,0:T(8,128)S(1)}, u32[]{:S(2)}) copy-start(f32[11,128,128]{2,1,0:T(8,128)S(1)} %add.89.refs_2_) | copy-start | bytes 2162692
  152.5 33.6 %copy-start.5 = (f32[18,128,128]{2,1,0:T(8,128)S(1)}, f32[18,128,128]{2,1,0:T(8,128)}, u32[]{:S(2)}) copy-start(f32[18,128,128]{2,1,0:T(8,128)} %get-tuple-element.75.xk) | copy-start | bytes 3538948
  152.5 30.6 %collective-permute-start.7 = (f32[18,128,128]{2,1,0:T(8,128)}, f32[18,128,128]{2,1,0:T(8,128)S(1)}, u32[]{:S(2)}, u32[]{:S(2)}) collective-permute-start(f32[18,128,128]{2,1,0:T(8,128)} %get-tuple-element.76), channel_id=1, source_target_pairs={{0,4},{1,5},{2,6},{3,7},{4,0},{5,1},{6,2},{7,3},{8,12},{9,13},{10,... | collective-permute-start | bytes 3538952 | tf_op jit(solution)/shard_map/ppermute | solution.py:529
  155.8 32.2 %collective-permute-start.9 = (f32[18,128,128]{2,1,0:T(8,128)}, f32[18,128,128]{2,1,0:T(8,128)}, u32[]{:S(2)}, u32[]{:S(2)}) collective-permute-start(f32[18,128,128]{2,1,0:T(8,128)} %get-tuple-element.78), channel_id=1, source_target_pairs={{0,64},{8,72},{16,80},{24,88},{32,96},{40,104},{48,112},{56,120},{... | collective-permute-start | bytes 3538952 | tf_op jit(solution)/shard_map/ppermute | solution.py:529
  157.7 43.1 %collective-permute-start.6 = (f32[11,128,128]{2,1,0:T(8,128)S(1)}, f32[11,128,128]{2,1,0:T(8,128)}, u32[]{:S(2)}, u32[]{:S(2)}) collective-permute-start(f32[11,128,128]{2,1,0:T(8,128)S(1)} %add.89.refs_2_), channel_id=1, source_target_pairs={{0,4},{1,5},{2,6},{3,7},{4,0},{5,1},{6,2},{7,3},{8,12},{9,13},{10,... | collective-permute-start | bytes 2162696 | tf_op jit(solution)/shard_map/ppermute | solution.py:529
  158.0 42.5 %collective-permute-start.5 = (f32[10,128,128]{2,1,0:T(8,128)}, f32[10,128,128]{2,1,0:T(8,128)}, u32[]{:S(2)}, u32[]{:S(2)}) collective-permute-start(f32[10,128,128]{2,1,0:T(8,128)} %add.88.refs_0_), channel_id=1, source_target_pairs={{0,64},{8,72},{16,80},{24,88},{32,96},{40,104},{48,112},{56,120},{... | collective-permute-start | bytes 1966088 | tf_op jit(solution)/shard_map/ppermute | solution.py:529
  173.8 87.0 %collective-permute-start.11 = (f32[23,128,128]{2,1,0:T(8,128)}, f32[23,128,128]{2,1,0:T(8,128)}, u32[]{:S(2)}, u32[]{:S(2)}) collective-permute-start(f32[23,128,128]{2,1,0:T(8,128)} %get-tuple-element.84), channel_id=1, source_target_pairs={{0,4},{1,5},{2,6},{3,7},{4,0},{5,1},{6,2},{7,3},{8,12},{9,13},{10,... | collective-permute-start | bytes 4521992 | tf_op jit(solution)/shard_map/ppermute | solution.py:529
  184.1 73.1 %collective-permute-start.13 = (f32[25,128,128]{2,1,0:T(8,128)}, f32[25,128,128]{2,1,0:T(8,128)S(1)}, u32[]{:S(2)}, u32[]{:S(2)}) collective-permute-start(f32[25,128,128]{2,1,0:T(8,128)} %get-tuple-element.86), channel_id=1, source_target_pairs={{0,64},{8,72},{16,80},{24,88},{32,96},{40,104},{48,112},{56,120},{... | collective-permute-start | bytes 4915208 | tf_op jit(solution)/shard_map/ppermute | solution.py:529
  188.0 56.2 %collective-permute-start.8 = (f32[9,128,128]{2,1,0:T(8,128)}, f32[9,128,128]{2,1,0:T(8,128)S(1)}, u32[]{:S(2)}, u32[]{:S(2)}) collective-permute-start(f32[9,128,128]{2,1,0:T(8,128)} %slice_add_fusion.3), channel_id=1, source_target_pairs={{0,64},{8,72},{16,80},{24,88},{32,96},{40,104},{48,112},{56,120},{... | collective-permute-start | bytes 1769480 | tf_op jit(solution)/shard_map/ppermute | solution.py:529
  200.5 43.7 %collective-permute-start.10 = (f32[9,128,128]{2,1,0:T(8,128)S(1)}, f32[9,128,128]{2,1,0:T(8,128)}, u32[]{:S(2)}, u32[]{:S(2)}) collective-permute-start(f32[9,128,128]{2,1,0:T(8,128)S(1)} %slice_add_fusion.2), channel_id=1, source_target_pairs={{0,4},{1,5},{2,6},{3,7},{4,0},{5,1},{6,2},{7,3},{8,12},{9,13},{10,... | collective-permute-start | bytes 1769480 | tf_op jit(solution)/shard_map/ppermute | solution.py:529
  254.6 30.6 %collective-permute-start.16 = (f32[384,768]{1,0:T(8,128)}, f32[384,768]{1,0:T(8,128)S(1)}, u32[]{:S(2)}, u32[]{:S(2)}) collective-permute-start(f32[384,768]{1,0:T(8,128)} %panel_two.1.p_ref), channel_id=1, source_target_pairs={{0,64},{8,72},{16,80},{24,88},{32,96},{40,104},{48,112},{56,120},{... | collective-permute-start | bytes 3538952 | tf_op jit(solution)/shard_map/ppermute | solution.py:529
  256.1 30.6 %collective-permute-start.15 = (f32[384,768]{1,0:T(8,128)}, f32[384,768]{1,0:T(8,128)S(1)}, u32[]{:S(2)}, u32[]{:S(2)}) collective-permute-start(f32[384,768]{1,0:T(8,128)} %panel_two.1.p_ref), channel_id=1, source_target_pairs={{0,4},{1,5},{2,6},{3,7},{4,0},{5,1},{6,2},{7,3},{8,12},{9,13},{10,... | collective-permute-start | bytes 3538952 | tf_op jit(solution)/shard_map/ppermute | solution.py:529
  258.4 51.4 %collective-permute-start.14 = (f32[17,128,128]{2,1,0:T(8,128)S(1)}, f32[17,128,128]{2,1,0:T(8,128)S(1)}, u32[]{:S(2)}, u32[]{:S(2)}) collective-permute-start(f32[17,128,128]{2,1,0:T(8,128)S(1)} %slice_add_fusion), channel_id=1, source_target_pairs={{0,4},{1,5},{2,6},{3,7},{4,0},{5,1},{6,2},{7,3},{8,12},{9,13},{10,... | collective-permute-start | bytes 3342344 | tf_op jit(solution)/shard_map/ppermute | solution.py:529
  262.2 45.4 %collective-permute-start.12 = (f32[16,128,128]{2,1,0:T(8,128)S(1)}, f32[16,128,128]{2,1,0:T(8,128)S(1)}, u32[]{:S(2)}, u32[]{:S(2)}) collective-permute-start(f32[16,128,128]{2,1,0:T(8,128)S(1)} %slice_add_fusion.1), channel_id=1, source_target_pairs={{0,64},{8,72},{16,80},{24,88},{32,96},{40,104},{48,112},{56,120},{... | collective-permute-start | bytes 3145736 | tf_op jit(solution)/shard_map/ppermute | solution.py:529
  285.1 22.5 %copy-start.15 = (f32[384,768]{1,0:T(8,128)}, f32[384,768]{1,0:T(8,128)S(1)}, u32[]{:S(2)}) copy-start(f32[384,768]{1,0:T(8,128)S(1)} %collective-permute-done.16.pz) | copy-start | bytes 3538948
  285.2 34.2 %collective-permute-start.17 = (f32[192,768]{1,0:T(8,128)S(1)}, f32[192,768]{1,0:T(8,128)S(1)}, u32[]{:S(2)}, u32[]{:S(2)}) collective-permute-start(f32[192,768]{1,0:T(8,128)S(1)} %slice.44), channel_id=1, source_target_pairs={{0,4},{1,5},{2,6},{3,7},{4,0},{5,1},{6,2},{7,3},{8,12},{9,13},{10,... | collective-permute-start | bytes 1769480 | tf_op jit(solution)/shard_map/ppermute | solution.py:529
  286.7 20.9 %copy-start.16 = (f32[384,768]{1,0:T(8,128)}, f32[384,768]{1,0:T(8,128)S(1)}, u32[]{:S(2)}) copy-start(f32[384,768]{1,0:T(8,128)S(1)} %collective-permute-done.15.px) | copy-start | bytes 3538948
  286.7 32.7 %collective-permute-start.18 = (f32[192,768]{1,0:T(8,128)S(1)}, f32[192,768]{1,0:T(8,128)}, u32[]{:S(2)}, u32[]{:S(2)}) collective-permute-start(f32[192,768]{1,0:T(8,128)S(1)} %slice.45), channel_id=1, source_target_pairs={{0,64},{8,72},{16,80},{24,88},{32,96},{40,104},{48,112},{56,120},{... | collective-permute-start | bytes 1769480 | tf_op jit(solution)/shard_map/ppermute | solution.py:529
  (15 other events, 78.7 us)

commit v3 on v2

--- a/solution.py
+++ b/solution.py
@@ -6,18 +6,20 @@
 from jax.experimental.pallas import tpu as pltpu
 from jax.sharding import PartitionSpec as P
 
+
 T = 128
 NP = 6
 NU = 12
 NC = 8
 f32 = jnp.float32
 bf16 = jnp.bfloat16
-NN = ((1,), (0,))
 NT = ((1,), (1,))
 OWN, OTH, MAP2, SLO, SHI, LIVE1, LIVE2, FILL1, FILL2 = 0, 8, 16, 28, 29, 30, 31, 32, 68
 
 
 def tl(i):
+    if isinstance(i, int):
+        return slice(i * T, i * T + T)
     return pl.ds(pl.multiple_of(i * T, T), T)
 
 
@@ -33,7 +35,7 @@
     return f(ah, bh) + (f(ah, bl) + f(al, bh))
 
 
-def call(kernel, args, specs, outs, scratch, name, flops=0, grid=(1,)):
+def call(kernel, args, specs, outs, scratch, flops=0, grid=(1,)):
     whole = pl.BlockSpec(memory_space=pltpu.VMEM)
     in_specs = [whole if s is None else s for s in specs]
     nbytes = sum(4 * a.size for a in args[1:]) + sum(4 * o.size for o in outs)
@@ -49,7 +51,6 @@
         out_shape=outs,
         compiler_params=pltpu.CompilerParams(vmem_limit_bytes=60 * 1024 * 1024),
         cost_estimate=pl.CostEstimate(flops=flops, bytes_accessed=nbytes, transcendentals=0),
-        name=name,
     )(*args)
 
 
@@ -68,33 +69,33 @@
         inv_ref[s_ref[first + i]] = i
 
 
-def gather_one_kernel(half_lo, s_ref, c_ref, p_ref, piv_ref, coup_ref, inv):
+def gather_one_kernel(half_lo, s_ref, c_ref, p_ref, a_ref, b_ref, coup_ref, inv):
     side = lax.axis_index("lo") // half_lo
     invert(s_ref, OWN, NC, inv, 18)
 
-    def piv_row(r, _):
-        local = r - 3 * side
-
-        def piv_col(c, _):
-            at = r * (r + 1) // 2 + c
+    for c in range(NP):
+        out_ref = a_ref if c < 2 else b_ref
+        base = BY_COL.index((c, c)) - (0 if c < 2 else 11) - c
+
+        def tile(r, _):
+            at = base + r
+            local = r - 3 * side
 
             @pl.when((local >= 0) & (local < 3))
             def _():
-                piv_ref[at] = p_ref[tl(local), tl(c)]
+                out_ref[at] = p_ref[tl(local), tl(c)]
 
             @pl.when((local < 0) | (local >= 3))
             def _():
-                piv_ref[at] = jnp.zeros((T, T), f32)
+                out_ref[at] = jnp.zeros((T, T), f32)
 
             @pl.when((inv[r] >= 0) & (inv[c] >= 0))
             def _():
-                piv_ref[at] += c_ref[tl(inv[r]), tl(inv[c])]
+                out_ref[at] += c_ref[tl(inv[r]), tl(inv[c])]
 
             return 0
 
-        return lax.fori_loop(0, r + 1, piv_col, 0)
-
-    lax.fori_loop(0, NP, piv_row, 0)
+        lax.fori_loop(c, NP, tile, 0)
 
     def coup_tile(t, count):
         row = inv[NP + (1 - side) * 6 + t // NP]
@@ -110,65 +111,89 @@
     lax.fori_loop(0, 36, coup_tile, 0)
 
 
-def factor_tile(d_ref, w_ref, u_ref):
+def factor_tile(x_ref, w_ref, u_ref):
     lane = lax.broadcasted_iota(jnp.int32, (8, T), 1)
-    row = lax.broadcasted_iota(jnp.int32, (8, T), 0)
+    wide = lambda v: jnp.broadcast_to(v, (8, T))
+    cols = lambda x, r0: [wide(x[:, r0 + k : r0 + k + 1]) for k in range(8)]
+    diag = cols(x_ref[0:8, :], 0)
+    x = x_ref[8:16, :]
+    ahead = (cols(x, 0), cols(x, 8))
     for g in range(16):
         r0 = 8 * g
-        w_ref[r0 : r0 + 8, :] = jnp.where(lane == row + r0, 1.0, 0.0).astype(f32)
-    for g in range(16):
-        r0 = 8 * g
-        rows = [jnp.broadcast_to(d_ref[r0 + i : r0 + i + 1, :], (8, T)) for i in range(8)]
-        wrows = [jnp.broadcast_to(w_ref[r0 + i : r0 + i + 1, :], (8, T)) for i in range(8)]
-        e = [
-            [jnp.broadcast_to(rows[i][:, r0 + k : r0 + k + 1], (8, T)) for k in range(i + 1)]
-            for i in range(8)
-        ]
+        inside = (lane >= r0) & (lane < r0 + 8)
+        e = [[wide(diag[k][i : i + 1, :]) for k in range(i + 1)] for i in range(8)]
         l = [[None] * 8 for _ in range(8)]
         rinv = [None] * 8
         for j in range(8):
             rinv[j] = lax.rsqrt(e[j][j])
+            l[j][j] = e[j][j] * rinv[j]
             for i in range(j + 1, 8):
                 l[i][j] = e[i][j] * rinv[j]
             for i in range(j + 1, 8):
                 for k in range(j + 1, i + 1):
                     e[i][k] = e[i][k] - l[i][j] * l[k][j]
-        u = [None] * 8
-        w = [None] * 8
-        for j in range(8):
-            a = rows[j]
-            b = wrows[j]
-            for k in range(j):
-                a = a - l[j][k] * u[k]
-                b = b - l[j][k] * w[k]
-            u[j] = a * rinv[j]
-            w[j] = b * rinv[j]
-            u_ref[r0 + j : r0 + j + 1, :] = jnp.where(lane[:1] >= r0 + j, u[j][:1], 0.0)
-            w_ref[r0 + j : r0 + j + 1, :] = w[j][:1]
-        for r in range(g + 1, 16):
-            q = 8 * r
-            dr = d_ref[q : q + 8, :]
-            wr = w_ref[q : q + 8, :]
-            c = [jnp.broadcast_to(dr[:, r0 + k : r0 + k + 1], (8, T)) for k in range(8)]
+
+        def eliminate(c):
             for j in range(8):
                 a = c[j]
                 for k in range(j):
                     a = a - l[j][k] * c[k]
                 c[j] = a * rinv[j]
+            return c
+
+        if g < 15:
+            c1 = eliminate(ahead[0])
+            diag = ahead[1]
             for j in range(8):
-                dr = dr - c[j] * u[j]
-                wr = wr - c[j] * w[j]
-            d_ref[q : q + 8, :] = dr
-            w_ref[q : q + 8, :] = wr
-
-
-def factor_kernel(counts, live_at, take, s_ref, *refs):
+                for k in range(8):
+                    diag[k] = diag[k] - c1[j] * wide(c1[j][k : k + 1, :])
+        z = [None] * 8
+        for j in range(8):
+            row = wide(x_ref[r0 + j : r0 + j + 1, :])
+            a = jnp.where(inside, jnp.where(lane == r0 + j, 1.0, 0.0), row)
+            for k in range(j):
+                a = a - l[j][k] * z[k]
+            z[j] = a * rinv[j]
+            d = jnp.where(lane < r0, 0.0, z[j])
+            for k in range(j, 8):
+                d = jnp.where(lane == r0 + k, l[k][j], d)
+            if j:
+                d = jnp.where(lane < r0 + j, 0.0, d)
+            u_ref[r0 + j : r0 + j + 1, :] = d[:1]
+            w_ref[r0 + j : r0 + j + 1, :] = jnp.where(lane < r0 + 8, z[j], 0.0)[:1]
+        y = [None] * 8
+        for j in reversed(range(8)):
+            a = z[j]
+            for i in range(j + 1, 8):
+                a = a - l[i][j] * y[i]
+            y[j] = a * rinv[j]
+        for r in range(g + 1, 16):
+            q = 8 * r
+            x = x_ref[q : q + 8, :]
+            if r == g + 1:
+                c, v = c1, z
+            else:
+                c, v = cols(x, r0), y
+            x = jnp.where(inside, 0.0, x)
+            for j in range(8):
+                x = x - c[j] * v[j]
+            x_ref[q : q + 8, :] = x
+            if r == g + 2:
+                ahead = (cols(x, r0 + 8), cols(x, r0 + 16))
+
+
+BY_ROW = [(r, c) for r in range(NP) for c in range(r + 1)]
+BY_COL = [(r, c) for c in range(NP) for r in range(c, NP)]
+
+
+def factor_kernel(spots, counts, k0, k1, live_at, take, s_ref, *refs):
     n_in = 2 * len(counts)
     ins = refs[:n_in]
-    low_ref, lh_ref, ll_ref, wh_ref, wl_ref, a_s, l_s, d_s, w_s, u_s = refs[n_in:]
+    prev = refs[n_in : n_in + 5] if k0 else ()
+    low_ref, lh_ref, ll_ref, wh_ref, wl_ref, a_s, l_s, d_s, w_s, u_s = refs[n_in + len(prev) :]
     live = s_ref[live_at]
+    last = jnp.minimum(live, k1)
     first = 0
-    spots = [(r, c) for r in range(NP) for c in range(r + 1)]
     for n, count in enumerate(counts):
         for t in range(count):
             r, c = spots[first + t]
@@ -183,8 +208,21 @@
         l_s[tl(k), tl(k)] = eye
         return 0
 
-    lax.fori_loop(live, NP, dead, 0)
+    lax.fori_loop(last, k1, dead, 0)
     tile_row = lax.broadcasted_iota(jnp.int32, (NP * T, T), 0) // T
+    if k0:
+        old = slice(0, k0 * T)
+        for ref, src in zip((l_s, lh_ref, ll_ref), prev[:3]):
+            ref[:, old] = src[...]
+        for ref, src in zip((wh_ref, wl_ref), prev[3:]):
+            ref[old, :] = src[...]
+
+        def catch_up(j, _):
+            xj = (prev[1][tl(j), :], prev[2][tl(j), :])
+            a_s[:, tl(j)] = a_s[:, tl(j)] - dot3((prev[1][...], prev[2][...]), xj, NT)
+            return 0
+
+        lax.fori_loop(k0, last, catch_up, 0)
 
     def step(k, _):
         s = tl(k)
@@ -193,7 +231,6 @@
         w = split(w_s[...])
         wh_ref[s, :] = w[0]
         wl_ref[s, :] = w[1]
-
         x = dot3(split(a_s[:, s]), w, NT)
         lh_ref[:, s], ll_ref[:, s] = split(x)
         l_s[:, s] = jnp.where((tile_row > k) & (tile_row < live), x, 0.0)
@@ -204,23 +241,26 @@
             a_s[:, tl(j)] = a_s[:, tl(j)] - dot3((lh_ref[:, s], ll_ref[:, s]), xj, NT)
             return 0
 
-        return lax.fori_loop(k + 1, live, col, 0)
-
-    lax.fori_loop(0, live, step, 0)
-    low_ref[...] = l_s[pl.ds(pl.multiple_of(take(s_ref), 64), low_ref.shape[0]), :]
-
-
-def factor(scalars, pairs, live_at, take, rows, name):
+        return lax.fori_loop(k + 1, last, col, 0)
+
+    lax.fori_loop(k0, last, step, 0)
+    if take is None:
+        low_ref[...] = l_s[...]
+    else:
+        low_ref[...] = l_s[pl.ds(pl.multiple_of(take(s_ref), 64), low_ref.shape[0]), :]
+
+
+def factor(scalars, pairs, spots, k0, k1, prev, live_at, take, rows):
     counts = tuple(x.shape[0] for x, _ in pairs)
     n = NP * T
+    wide = k1 * T
     return call(
-        functools.partial(factor_kernel, counts, live_at, take),
-        [scalars] + [x for pair in pairs for x in pair],
-        [None] * (2 * len(pairs)),
-        [shape(rows, n), shape(n, n, dtype=bf16), shape(n, n, dtype=bf16)]
-        + [shape(n, T, dtype=bf16)] * 2,
-        [pltpu.VMEM((n, n), f32)] * 2 + [pltpu.VMEM((T, T), f32)] * 3,
-        name,
+        functools.partial(factor_kernel, spots, counts, k0, k1, live_at, take),
+        [scalars] + [x for pair in pairs for x in pair] + list(prev),
+        [None] * (2 * len(pairs) + len(prev)),
+        [shape(rows, wide), shape(n, wide, dtype=bf16), shape(n, wide, dtype=bf16)]
+        + [shape(wide, T, dtype=bf16)] * 2,
+        [pltpu.VMEM((n, wide), f32)] * 2 + [pltpu.VMEM((T, T), f32)] * 3,
         flops=20_000_000_000,
     )
 
@@ -398,7 +438,7 @@
         lax.fori_loop(0, 6 * half, tile, 0)
 
 
-def rows_two(scalars, own, cross, block_c, first, width, name):
+def rows_two(scalars, own, cross, block_c, first, width):
     count = 3 * width
     return call(
         functools.partial(rows_two_kernel, first, width),
@@ -406,7 +446,6 @@
         [None] * 3,
         [shape(count, T, T)] * 4,
         [pltpu.SMEM((18,), jnp.int32)] * 2,
-        name,
     )
 
 
@@ -529,7 +568,7 @@
     return lax.ppermute(values, axis, [(i, i ^ (size // 2)) for i in range(size)])
 
 
-def body(
+def program(
     contribution,
     pivot_one,
     rows_one,
@@ -560,18 +599,17 @@
     smem = pltpu.SMEM((18,), i32)
     n = NP * T
 
-    piv, coup = call(
+    piv_a, piv_b, coup = call(
         functools.partial(gather_one_kernel, half_lo),
         [map_one[hi, lo], c, pivot_one[0, 0]],
         [None, None],
-        [shape(21, T, T), shape(16, T, T)],
+        [shape(11, T, T), shape(10, T, T), shape(16, T, T)],
         [smem],
-        "gather_one",
-    )
-    piv, map_one, map_two, fill_one, fill_two, live_one, live_two = lax.optimization_barrier(
-        (piv, map_one, map_two, fill_one, fill_two, live_one, live_two)
-    )
-    piv_got = across("lo", piv)
+    )
+    piv_a, map_one, map_two, fill_one, fill_two, live_one, live_two = lax.optimization_barrier(
+        (piv_a, map_one, map_two, fill_one, fill_two, live_one, live_two)
+    )
+    got_a = across("lo", piv_a)
     scalars = jnp.concatenate(
         [
             map_one[hi, lo],
@@ -585,17 +623,15 @@
         ]
     )
     (x_one,) = call(
-        couple_one_kernel,
-        [scalars, rows1, c],
-        [block(n, n, 0), None],
-        [shape(n, n)],
-        [smem],
-        "couple_one",
-    )
-    coup, piv_got = lax.optimization_barrier((coup, piv_got))
+        couple_one_kernel, [scalars, rows1, c], [block(n, n, 0), None], [shape(n, n)], [smem]
+    )
+    piv_b, got_a = lax.optimization_barrier((piv_b, got_a))
+    got_b = across("lo", piv_b)
+    part = factor(scalars, [(piv_a, got_a)], BY_COL, 0, 2, (), LIVE1, None, n)
+    coup, got_b = lax.optimization_barrier((coup, got_b))
     coup_got = across("lo", coup)
     lower_one, *fac1 = factor(
-        scalars, [(piv, piv_got)], LIVE1, lambda s: s[SLO] * 384, 384, "factor_one"
+        scalars, [(piv_b, got_b)], BY_COL[11:], 2, NP, part, LIVE1, lambda s: s[SLO] * 384, 384
     )
     panel_one, send = call(
         panel_one_kernel,
@@ -603,7 +639,6 @@
         [None] * 6,
         [shape(n, n), shape(n, n // 2)],
         [pltpu.VMEM((n, n), bf16)] * 2 + [smem],
-        "panel_one",
         flops=3_000_000_000,
     )
     got = across("lo", send)
@@ -613,7 +648,6 @@
         [None, block(n, n, 1), block(n, n, 2)],
         [shape(n, n)],
         [pltpu.VMEM((n, n), bf16)] * 2,
-        "own_one",
         flops=4_000_000_000,
     )
     cross, pa, pb = call(
@@ -622,13 +656,12 @@
         [None, None, block(n, n, 2), None, None, None],
         [shape(n, n), shape(10, T, T), shape(11, T, T)],
         [pltpu.VMEM((2 * T, n), f32), smem, smem],
-        "cross_one",
         flops=2_000_000_000,
     )
     pa1 = across("hi", pa)
     pb1 = across("lo", pb)
     pa, pb, cross = lax.optimization_barrier((pa, pb, cross))
-    cxs, cxk, czs, czk = rows_two(scalars, own, cross, c, 0, NP, "coupling_two")
+    cxs, cxk, czs, czk = rows_two(scalars, own, cross, c, 0, NP)
     pa = pa + pa1
     pb = pb + pb1
     pa, pb, cxs, czs = lax.optimization_barrier((pa, pb, cxs, czs))
@@ -642,31 +675,35 @@
         [None] * 3,
         [shape(23, T, T)] * 2 + [shape(25, T, T)] * 2,
         [smem, smem] + [pltpu.SMEM((32,), i32)] * 2,
-        "trailing_two",
     )
     tx1 = across("hi", txs)
     tz1 = across("lo", tzs)
     lower_two, *fac2 = factor(
         scalars,
         [(pa, pa2), (pb, pb2)],
+        BY_ROW,
+        0,
+        NP,
+        (),
         LIVE2,
         lambda s: (2 * s[SHI] + s[SLO]) * 192,
         192,
-        "factor_two",
     )
     cx2 = across("lo", cxk[:9] + cx1[:9])
     cz2 = across("hi", czk[:9] + cz1[:9])
+    tx = txk[:16] + tx1[:16]
+    tz = tzk[:17] + tz1[:17]
+    tx, tz, cx2, cz2 = lax.optimization_barrier((tx, tz, cx2, cz2))
+    tx2 = across("lo", tx)
+    tz2 = across("hi", tz)
     (panel_two,) = call(
         panel_two_kernel,
         [scalars, rows2, cxk, cx1, cx2, czk, cz1, cz2, *fac2],
         [block(384, n, 0)] + [None] * 10,
         [shape(384, n)],
         [pltpu.VMEM((384, n), bf16)] * 2,
-        "panel_two",
         flops=2_000_000_000,
     )
-    tx2 = across("lo", txk[:16] + tx1[:16])
-    tz2 = across("hi", tzk[:17] + tz1[:17])
     px = across("hi", panel_two)
     pz = across("lo", panel_two)
     pd0 = across("hi", pz[:192])
@@ -677,7 +714,6 @@
         [None] * 8,
         [shape(384, NU * T)],
         [],
-        "schur_base",
         flops=1_000_000_000,
     )
     (schur_two,) = call(
@@ -686,7 +722,6 @@
         [None] * 6,
         [shape(384, NU * T)],
         [],
-        "schur_two",
         flops=3_000_000_000,
     )
     return tuple(
@@ -697,7 +732,7 @@
 def solution(mesh):
     split_spec = P("hi", "lo", None, None)
     return jax.shard_map(
-        body,
+        program,
         mesh=mesh,
         in_specs=(split_spec,) * 5 + (P(),) * 6,
         out_specs=(split_spec,) * 5,

time: 330 us -> 327 us (level)
  the two profiles are of different devices: /device:TPU:34 before, /device:TPU:0 now
where the time goes in v3:
time: 327 us; the launch traced here: 323 us
  Pallas kernels  159 us (49%)
  waiting for transfers between devices  93.5 us (29%)
  starting transfers between devices  46.1 us (14%)
  local copies, waits for them, and re-layouts  17.4 us (5%)
  other arithmetic  5.72 us (2%)
    pallas_call x13, Pallas kernels, call(): pl.pallas_call(kernel, grid_spec=pltpu.PrefetchScalarGridSpec(num_scalar_...  159 us
    ppermute x20, waiting for transfers between devices, across(): return lax.ppermute(values, axis, [(i, i ^ size // 2) for i in range(size)])  93.5 us
    ppermute x20, starting transfers between devices, across(): return lax.ppermute(values, axis, [(i, i ^ size // 2) for i in range(size)])  46.1 us
    unnamed x48, local copies, waits for them, and re-layouts  6.86 us
  transfers between devices with their start and end apart: 20, of which 11 were waited for; matrix products, arithmetic and copies ran while one was open for 5% of the time, Pallas kernels for 35%

profile of v3, /device:TPU:0, one launch (start us, length us, event | category | flops | bytes accessed | tf_op | source)
XLA Modules:
  0.0 322.7 jit_solution(14621023020082941686)
XLA Ops:
  2.1 6.1 %shard_map.146 = (f32[11,128,128]{2,1,0:T(8,128)}, f32[10,128,128]{2,1,0:T(8,128)}, f32[16,128,128]{2,1,0:T(8,128)}) custom-call(s32[8]{0:T(128)} %dynamic-slice_reduce_fusion.2.s_ref, f32[1024,1024]{1,0:T(8,128)} %bitcast.20, f32[384,768]{1,0:T(8,128)} %bitcast.29), custom_call_target="tpu_custom_call" | custom-call | bytes 7798784 | tf_op jit(solution)/shard_map/pallas_call | solution.py:42
  8.2 4.1 %collective-permute-start = (f32[11,128,128]{2,1,0:T(8,128)}, f32[11,128,128]{2,1,0:T(8,128)S(1)}, u32[]{:S(2)}, u32[]{:S(2)}) collective-permute-start(f32[11,128,128]{2,1,0:T(8,128)} %get-tuple-element.66.refs_0_), channel_id=1, source_target_pairs={{0,64},{8,72},{16,80},{24,88},{32,96},{40,104},{48,112},{56,120},{... | collective-permute-start | bytes 2162696 | tf_op jit(solution)/shard_map/ppermute | solution.py:568
  19.6 6.0 %shard_map.149.x_ref = f32[768,768]{1,0:T(8,128)} custom-call(s32[86]{0:T(128)} %concatenate.3.s_ref, f32[768,2304]{1,0:T(8,128)} %bitcast.16, f32[1024,1024]{1,0:T(8,128)} %bitcast.21), custom_call_target="tpu_custom_call" | custom-call | bytes 13631488 | tf_op jit(solution)/shard_map/pallas_call | solution.py:42
  25.6 3.1 collective-permute-done.refs_1_
  28.8 3.2 %collective-permute-start.1 = (f32[10,128,128]{2,1,0:T(8,128)S(1)}, f32[10,128,128]{2,1,0:T(8,128)S(1)}, u32[]{:S(2)}, u32[]{:S(2)}) collective-permute-start(f32[10,128,128]{2,1,0:T(8,128)S(1)} %copy-done.22), channel_id=1, source_target_pairs={{0,64},{8,72},{16,80},{24,88},{32,96},{40,104},{48,112},{56,120},{... | collective-permute-start | bytes 1966088 | tf_op jit(solution)/shard_map/ppermute | solution.py:568
  32.0 10.3 %shard_map.147 = (f32[768,256]{1,0:T(8,128)}, bf16[768,256]{1,0:T(8,128)(2,1)}, bf16[768,256]{1,0:T(8,128)(2,1)}, bf16[256,128]{1,0:T(8,128)(2,1)}, bf16[256,128]{1,0:T(8,128)(2,1)}) custom-call(s32[86]{0:T(128)} %concatenate.3.s_ref, f32[11,128,128]{2,1,0:T(8,128)} %get-tuple-element.66.refs_0_, f32[11,128,128]{2,1,0:T(8,128)} %copy-done.21), custom_call_target="tpu_custom_call" | custom-call | flops 20000000000 | bytes 4063232 | tf_op jit(solution)/shard_map/pallas_call | solution.py:42
  42.3 4.0 %collective-permute-done.1.refs_1_ = f32[10,128,128]{2,1,0:T(8,128)S(1)} collective-permute-done((f32[10,128,128]{2,1,0:T(8,128)S(1)}, f32[10,128,128]{2,1,0:T(8,128)S(1)}, u32[]{:S(2)}, u32[]{:S(2)}) %collective-permute-start.1) | collective-permute-done | bytes 655392 | tf_op jit(solution)/shard_map/ppermute | solution.py:568
  49.2 21.7 %shard_map.148 = (f32[384,768]{1,0:T(8,128)}, bf16[768,768]{1,0:T(8,128)(2,1)}, bf16[768,768]{1,0:T(8,128)(2,1)}, bf16[768,128]{1,0:T(8,128)(2,1)}, bf16[768,128]{1,0:T(8,128)(2,1)}) custom-call(s32[86]{0:T(128)} %concatenate.3.s_ref, f32[10,128,128]{2,1,0:T(8,128)} %get-tuple-element.67.refs_0_, f32[10,128,128]{2,1,0:T(8,128)} %copy-done.23, ...), custom_call_target="tpu_custom_call" | custom-call | flops 20000000000 | bytes 10616832 | tf_op jit(solution)/shard_map/pallas_call | solution.py:42
  72.3 12.4 %shard_map.150 = (f32[768,768]{1,0:T(8,128)}, f32[768,384]{1,0:T(8,128)}) custom-call(s32[86]{0:T(128)} %concatenate.3.s_ref, f32[768,768]{1,0:T(8,128)} %shard_map.149.x_ref, f32[16,128,128]{2,1,0:T(8,128)} %copy-done.20, bf16[768,768]{1,0:T(8,128)(2,1)} %get-tuple-element.78.lh, bf16[768,768]{1,0:T(8,128)(2,1)} %get-tuple-element.79.ll, ...), custom_call_target="tpu_custom_call" | custom-call | flops 3000000000 | bytes 12451840 | tf_op jit(solution)/shard_map/pallas_call | solution.py:42
  87.3 8.1 %shard_map.151.own_ref = f32[768,768]{1,0:T(8,128)} custom-call(s32[86]{0:T(128)} %concatenate.3.s_ref, f32[768,768]{1,0:T(8,128)} %get-tuple-element.82.p_ref, f32[768,2304]{1,0:T(8,128)} %bitcast.17, f32[768,2304]{1,0:T(8,128)} %bitcast.18), custom_call_target="tpu_custom_call" | custom-call | flops 4000000000 | bytes 18874368 | tf_op jit(solution)/shard_map/pallas_call | solution.py:42
  95.4 12.9 %collective-permute-done.3.q_ref = f32[768,384]{1,0:T(8,128)S(1)} collective-permute-done((f32[768,384]{1,0:T(8,128)}, f32[768,384]{1,0:T(8,128)S(1)}, u32[]{:S(2)}, u32[]{:S(2)}) %collective-permute-start.3) | collective-permute-done | bytes 1179680 | tf_op jit(solution)/shard_map/ppermute | solution.py:568
  109.4 11.0 %shard_map.152 = (f32[768,768]{1,0:T(8,128)}, f32[10,128,128]{2,1,0:T(8,128)}, f32[11,128,128]{2,1,0:T(8,128)}) custom-call(s32[86]{0:T(128)} %concatenate.3.s_ref, f32[768,768]{1,0:T(8,128)} %get-tuple-element.82.p_ref, f32[768,384]{1,0:T(8,128)} %copy-done.7, f32[768,2304]{1,0:T(8,128)} %bitcast.19, f32[768,768]{1,0:T(8,128)} %shard_map.151.own_ref, ...), custom_call_target="tpu_custom_call" | custom-call | flops 2000000000 | bytes 21495808 | tf_op jit(solution)/shard_map/pallas_call | solution.py:42
  122.7 6.3 %collective-permute-start.4 = (f32[10,128,128]{2,1,0:T(8,128)}, f32[10,128,128]{2,1,0:T(8,128)S(1)}, u32[]{:S(2)}, u32[]{:S(2)}) collective-permute-start(f32[10,128,128]{2,1,0:T(8,128)} %get-tuple-element.87), channel_id=1, source_target_pairs={{0,4},{1,5},{2,6},{3,7},{4,0},{5,1},{6,2},{7,3},{8,12},{9,13},{10,... | collective-permute-start | bytes 1966088 | tf_op jit(solution)/shard_map/ppermute | solution.py:568
  129.0 13.0 %shard_map.153 = (f32[18,128,128]{2,1,0:T(8,128)}, f32[18,128,128]{2,1,0:T(8,128)}, f32[18,128,128]{2,1,0:T(8,128)}, f32[18,128,128]{2,1,0:T(8,128)}) custom-call(s32[86]{0:T(128)} %concatenate.3.s_ref, f32[768,768]{1,0:T(8,128)} %shard_map.151.own_ref, f32[768,768]{1,0:T(8,128)} %get-tuple-element.89.cross_ref, f32[1024,1024]{1,0:T(8,128)} %bitcast.23), custom_call_target="tpu_custom_call" | custom-call | bytes 13631488 | tf_op jit(solution)/shard_map/pallas_call | solution.py:42
  147.3 14.9 %shard_map.155 = (f32[23,128,128]{2,1,0:T(8,128)}, f32[23,128,128]{2,1,0:T(8,128)}, f32[25,128,128]{2,1,0:T(8,128)}, f32[25,128,128]{2,1,0:T(8,128)}) custom-call(s32[86]{0:T(128)} %concatenate.3.s_ref, f32[768,768]{1,0:T(8,128)} %shard_map.151.own_ref, f32[768,768]{1,0:T(8,128)} %get-tuple-element.89.cross_ref, f32[1024,1024]{1,0:T(8,128)} %bitcast.24), custom_call_target="tpu_custom_call" | custom-call | bytes 15204352 | tf_op jit(solution)/shard_map/pallas_call | solution.py:42
  169.3 29.3 %shard_map.154 = (f32[192,768]{1,0:T(8,128)}, bf16[768,768]{1,0:T(8,128)(2,1)}, bf16[768,768]{1,0:T(8,128)(2,1)}, bf16[768,128]{1,0:T(8,128)(2,1)}, bf16[768,128]{1,0:T(8,128)(2,1)}) custom-call(s32[86]{0:T(128)} %concatenate.3.s_ref, f32[10,128,128]{2,1,0:T(8,128)} %add.88.refs_0_, f32[10,128,128]{2,1,0:T(8,128)} %collective-permute-done.6.refs_1_, ...), custom_call_target="tpu_custom_call" | custom-call | flops 20000000000 | bytes 8847360 | tf_op jit(solution)/shard_map/pallas_call | solution.py:42
  198.6 22.0 %collective-permute-done.8.x1 = f32[18,128,128]{2,1,0:T(8,128)} collective-permute-done((f32[18,128,128]{2,1,0:T(8,128)}, f32[18,128,128]{2,1,0:T(8,128)}, u32[]{:S(2)}, u32[]{:S(2)}) %collective-permute-start.8) | collective-permute-done | bytes 1179680 | tf_op jit(solution)/shard_map/ppermute | solution.py:568
  223.5 4.2 %collective-permute-done.12.z1 = f32[18,128,128]{2,1,0:T(8,128)} collective-permute-done((f32[18,128,128]{2,1,0:T(8,128)}, f32[18,128,128]{2,1,0:T(8,128)}, u32[]{:S(2)}, u32[]{:S(2)}) %collective-permute-start.12) | collective-permute-done | bytes 1179680 | tf_op jit(solution)/shard_map/ppermute | solution.py:568
  233.8 3.4 %collective-permute-done.11.x2 = f32[9,128,128]{2,1,0:T(8,128)S(1)} collective-permute-done((f32[9,128,128]{2,1,0:T(8,128)S(1)}, f32[9,128,128]{2,1,0:T(8,128)S(1)}, u32[]{:S(2)}, u32[]{:S(2)}) %collective-permute-start.11) | collective-permute-done | bytes 589856 | tf_op jit(solution)/shard_map/ppermute | solution.py:568
  241.1 9.6 %shard_map.156.p_ref = f32[384,768]{1,0:T(8,128)} custom-call(s32[86]{0:T(128)} %concatenate.3.s_ref, f32[384,2304]{1,0:T(8,128)} %bitcast.25, f32[18,128,128]{2,1,0:T(8,128)} %get-tuple-element.95.xk, f32[18,128,128]{2,1,0:T(8,128)} %collective-permute-done.8.x1, f32[9,128,128]{2,1,0:T(8,128)} %copy-done.15, f32[18,128,128]{2,1,0:T(8,128)} %get-tuple-element.101.zk, ...), custom_call_target="tpu_custom_call" | custom-call | flops 2000000000 | bytes 16121856 | tf_op jit(solution)/shard_map/pallas_call | solution.py:42
  257.7 23.5 %collective-permute-done.17.pz = f32[384,768]{1,0:T(8,128)S(1)} collective-permute-done((f32[384,768]{1,0:T(8,128)}, f32[384,768]{1,0:T(8,128)S(1)}, u32[]{:S(2)}, u32[]{:S(2)}) %collective-permute-start.17) | collective-permute-done | bytes 1179680 | tf_op jit(solution)/shard_map/ppermute | solution.py:568
  286.9 15.5 %collective-permute-done.14.x2 = f32[16,128,128]{2,1,0:T(8,128)S(1)} collective-permute-done((f32[16,128,128]{2,1,0:T(8,128)S(1)}, f32[16,128,128]{2,1,0:T(8,128)S(1)}, u32[]{:S(2)}, u32[]{:S(2)}) %collective-permute-start.14) | collective-permute-done | bytes 1048608 | tf_op jit(solution)/shard_map/ppermute | solution.py:568
  305.9 8.6 %shard_map.157.b_ref = f32[384,1536]{1,0:T(8,128)} custom-call(s32[86]{0:T(128)} %concatenate.3.s_ref, f32[384,2304]{1,0:T(8,128)} %bitcast.26, f32[384,768]{1,0:T(8,128)} %shard_map.156.p_ref, f32[23,128,128]{2,1,0:T(8,128)} %get-tuple-element.97.xk, f32[23,128,128]{2,1,0:T(8,128)} %copy-done.5, f32[16,128,128]{2,1,0:T(8,128)} %copy-done.11, ...), custom_call_target="tpu_custom_call" | custom-call | flops 1000000000 | bytes 15532032 | tf_op jit(solution)/shard_map/pallas_call | solution.py:42
  314.5 8.2 %shard_map.158 = f32[384,1536]{1,0:T(8,128)} custom-call(s32[86]{0:T(128)} %concatenate.3.s_ref, f32[384,1536]{1,0:T(8,128)} %shard_map.157.b_ref, f32[384,768]{1,0:T(8,128)} %shard_map.156.p_ref, f32[384,768]{1,0:T(8,128)} %copy-done.18, f32[384,768]{1,0:T(8,128)} %copy-done.17, f32[192,768]{1,0:T(8,128)} %collective-permute-done.18.pd0, ...), custom_call_target="tpu_custom_call" | custom-call | flops 3000000000 | bytes 9437184 | tf_op jit(solution)/shard_map/pallas_call | solution.py:42
  (97 shorter events, 60.4 us)
Async XLA Ops:
  8.2 20.5 %collective-permute-start = (f32[11,128,128]{2,1,0:T(8,128)}, f32[11,128,128]{2,1,0:T(8,128)S(1)}, u32[]{:S(2)}, u32[]{:S(2)}) collective-permute-start(f32[11,128,128]{2,1,0:T(8,128)} %get-tuple-element.66.refs_0_), channel_id=1, source_target_pairs={{0,64},{8,72},{16,80},{24,88},{32,96},{40,104},{48,112},{56,120},{... | collective-permute-start | bytes 2162696 | tf_op jit(solution)/shard_map/ppermute | solution.py:568
  28.8 17.5 %collective-permute-start.1 = (f32[10,128,128]{2,1,0:T(8,128)S(1)}, f32[10,128,128]{2,1,0:T(8,128)S(1)}, u32[]{:S(2)}, u32[]{:S(2)}) collective-permute-start(f32[10,128,128]{2,1,0:T(8,128)S(1)} %copy-done.22), channel_id=1, source_target_pairs={{0,64},{8,72},{16,80},{24,88},{32,96},{40,104},{48,112},{56,120},{... | collective-permute-start | bytes 1966088 | tf_op jit(solution)/shard_map/ppermute | solution.py:568
  46.3 25.1 %collective-permute-start.2 = (f32[16,128,128]{2,1,0:T(8,128)S(1)}, f32[16,128,128]{2,1,0:T(8,128)S(1)}, u32[]{:S(2)}, u32[]{:S(2)}) collective-permute-start(f32[16,128,128]{2,1,0:T(8,128)S(1)} %copy-done.19), channel_id=1, source_target_pairs={{0,64},{8,72},{16,80},{24,88},{32,96},{40,104},{48,112},{56,120},{... | collective-permute-start | bytes 3145736 | tf_op jit(solution)/shard_map/ppermute | solution.py:568
  84.7 23.7 %collective-permute-start.3 = (f32[768,384]{1,0:T(8,128)}, f32[768,384]{1,0:T(8,128)S(1)}, u32[]{:S(2)}, u32[]{:S(2)}) collective-permute-start(f32[768,384]{1,0:T(8,128)} %get-tuple-element.83), channel_id=1, source_target_pairs={{0,64},{8,72},{16,80},{24,88},{32,96},{40,104},{48,112},{56,120},{... | collective-permute-start | bytes 3538952 | tf_op jit(solution)/shard_map/ppermute | solution.py:568
  120.4 22.6 %collective-permute-start.5 = (f32[11,128,128]{2,1,0:T(8,128)}, f32[11,128,128]{2,1,0:T(8,128)S(1)}, u32[]{:S(2)}, u32[]{:S(2)}) collective-permute-start(f32[11,128,128]{2,1,0:T(8,128)} %get-tuple-element.88), channel_id=1, source_target_pairs={{0,64},{8,72},{16,80},{24,88},{32,96},{40,104},{48,112},{56,120},{... | collective-permute-start | bytes 2162696 | tf_op jit(solution)/shard_map/ppermute | solution.py:568
  122.7 19.4 %collective-permute-start.4 = (f32[10,128,128]{2,1,0:T(8,128)}, f32[10,128,128]{2,1,0:T(8,128)S(1)}, u32[]{:S(2)}, u32[]{:S(2)}) collective-permute-start(f32[10,128,128]{2,1,0:T(8,128)} %get-tuple-element.87), channel_id=1, source_target_pairs={{0,4},{1,5},{2,6},{3,7},{4,0},{5,1},{6,2},{7,3},{8,12},{9,13},{10,... | collective-permute-start | bytes 1966088 | tf_op jit(solution)/shard_map/ppermute | solution.py:568
  143.5 25.8 %collective-permute-start.7 = (f32[11,128,128]{2,1,0:T(8,128)S(1)}, f32[11,128,128]{2,1,0:T(8,128)}, u32[]{:S(2)}, u32[]{:S(2)}) collective-permute-start(f32[11,128,128]{2,1,0:T(8,128)S(1)} %add.89.refs_2_), channel_id=1, source_target_pairs={{0,4},{1,5},{2,6},{3,7},{4,0},{5,1},{6,2},{7,3},{8,12},{9,13},{10,... | collective-permute-start | bytes 2162696 | tf_op jit(solution)/shard_map/ppermute | solution.py:568
  146.0 21.5 %collective-permute-start.6 = (f32[10,128,128]{2,1,0:T(8,128)}, f32[10,128,128]{2,1,0:T(8,128)}, u32[]{:S(2)}, u32[]{:S(2)}) collective-permute-start(f32[10,128,128]{2,1,0:T(8,128)} %add.88.refs_0_), channel_id=1, source_target_pairs={{0,64},{8,72},{16,80},{24,88},{32,96},{40,104},{48,112},{56,120},{... | collective-permute-start | bytes 1966088 | tf_op jit(solution)/shard_map/ppermute | solution.py:568
  162.2 67.7 %collective-permute-start.9 = (f32[23,128,128]{2,1,0:T(8,128)}, f32[23,128,128]{2,1,0:T(8,128)S(1)}, u32[]{:S(2)}, u32[]{:S(2)}) collective-permute-start(f32[23,128,128]{2,1,0:T(8,128)} %get-tuple-element.98), channel_id=1, source_target_pairs={{0,4},{1,5},{2,6},{3,7},{4,0},{5,1},{6,2},{7,3},{8,12},{9,13},{10,... | collective-permute-start | bytes 4521992 | tf_op jit(solution)/shard_map/ppermute | solution.py:568
  162.5 68.6 %collective-permute-start.10 = (f32[25,128,128]{2,1,0:T(8,128)}, f32[25,128,128]{2,1,0:T(8,128)S(1)}, u32[]{:S(2)}, u32[]{:S(2)}) collective-permute-start(f32[25,128,128]{2,1,0:T(8,128)} %get-tuple-element.100), channel_id=1, source_target_pairs={{0,64},{8,72},{16,80},{24,88},{32,96},{40,104},{48,112},{56,120},{... | collective-permute-start | bytes 4915208 | tf_op jit(solution)/shard_map/ppermute | solution.py:568
  164.9 55.6 %collective-permute-start.8 = (f32[18,128,128]{2,1,0:T(8,128)}, f32[18,128,128]{2,1,0:T(8,128)}, u32[]{:S(2)}, u32[]{:S(2)}) collective-permute-start(f32[18,128,128]{2,1,0:T(8,128)} %get-tuple-element.96), channel_id=1, source_target_pairs={{0,4},{1,5},{2,6},{3,7},{4,0},{5,1},{6,2},{7,3},{8,12},{9,13},{10,... | collective-permute-start | bytes 3538952 | tf_op jit(solution)/shard_map/ppermute | solution.py:568
  167.5 60.1 %collective-permute-start.12 = (f32[18,128,128]{2,1,0:T(8,128)}, f32[18,128,128]{2,1,0:T(8,128)}, u32[]{:S(2)}, u32[]{:S(2)}) collective-permute-start(f32[18,128,128]{2,1,0:T(8,128)} %get-tuple-element.102), channel_id=1, source_target_pairs={{0,64},{8,72},{16,80},{24,88},{32,96},{40,104},{48,112},{56,120},{... | collective-permute-start | bytes 3538952 | tf_op jit(solution)/shard_map/ppermute | solution.py:568
  198.6 29.0 %copy-start.6 = (f32[18,128,128]{2,1,0:T(8,128)S(1)}, f32[18,128,128]{2,1,0:T(8,128)}, u32[]{:S(2)}) copy-start(f32[18,128,128]{2,1,0:T(8,128)} %get-tuple-element.101.zk) | copy-start | bytes 3538948
  221.9 15.3 %collective-permute-start.11 = (f32[9,128,128]{2,1,0:T(8,128)S(1)}, f32[9,128,128]{2,1,0:T(8,128)S(1)}, u32[]{:S(2)}, u32[]{:S(2)}) collective-permute-start(f32[9,128,128]{2,1,0:T(8,128)S(1)} %slice_add_fusion.3), channel_id=1, source_target_pairs={{0,64},{8,72},{16,80},{24,88},{32,96},{40,104},{48,112},{56,120},{... | collective-permute-start | bytes 1769480 | tf_op jit(solution)/shard_map/ppermute | solution.py:568
  228.8 11.5 %collective-permute-start.13 = (f32[9,128,128]{2,1,0:T(8,128)S(1)}, f32[9,128,128]{2,1,0:T(8,128)S(1)}, u32[]{:S(2)}, u32[]{:S(2)}) collective-permute-start(f32[9,128,128]{2,1,0:T(8,128)S(1)} %slice_add_fusion.2), channel_id=1, source_target_pairs={{0,4},{1,5},{2,6},{3,7},{4,0},{5,1},{6,2},{7,3},{8,12},{9,13},{10,... | collective-permute-start | bytes 1769480 | tf_op jit(solution)/shard_map/ppermute | solution.py:568
  230.0 20.7 %copy-start.5 = (f32[23,128,128]{2,1,0:T(8,128)}, f32[23,128,128]{2,1,0:T(8,128)S(1)}, u32[]{:S(2)}) copy-start(f32[23,128,128]{2,1,0:T(8,128)S(1)} %collective-permute-done.9.x1) | copy-start | bytes 4521988
  250.7 30.6 %collective-permute-start.17 = (f32[384,768]{1,0:T(8,128)}, f32[384,768]{1,0:T(8,128)S(1)}, u32[]{:S(2)}, u32[]{:S(2)}) collective-permute-start(f32[384,768]{1,0:T(8,128)} %shard_map.156.p_ref), channel_id=1, source_target_pairs={{0,64},{8,72},{16,80},{24,88},{32,96},{40,104},{48,112},{56,120},{... | collective-permute-start | bytes 3538952 | tf_op jit(solution)/shard_map/ppermute | solution.py:568
  251.8 31.4 %collective-permute-start.16 = (f32[384,768]{1,0:T(8,128)}, f32[384,768]{1,0:T(8,128)S(1)}, u32[]{:S(2)}, u32[]{:S(2)}) collective-permute-start(f32[384,768]{1,0:T(8,128)} %shard_map.156.p_ref), channel_id=1, source_target_pairs={{0,4},{1,5},{2,6},{3,7},{4,0},{5,1},{6,2},{7,3},{8,12},{9,13},{10,... | collective-permute-start | bytes 3538952 | tf_op jit(solution)/shard_map/ppermute | solution.py:568
  254.5 50.4 %collective-permute-start.15 = (f32[17,128,128]{2,1,0:T(8,128)S(1)}, f32[17,128,128]{2,1,0:T(8,128)S(1)}, u32[]{:S(2)}, u32[]{:S(2)}) collective-permute-start(f32[17,128,128]{2,1,0:T(8,128)S(1)} %copy-done.9), channel_id=1, source_target_pairs={{0,4},{1,5},{2,6},{3,7},{4,0},{5,1},{6,2},{7,3},{8,12},{9,13},{10,... | collective-permute-start | bytes 3342344 | tf_op jit(solution)/shard_map/ppermute | solution.py:568
  255.4 47.1 %collective-permute-start.14 = (f32[16,128,128]{2,1,0:T(8,128)S(1)}, f32[16,128,128]{2,1,0:T(8,128)S(1)}, u32[]{:S(2)}, u32[]{:S(2)}) collective-permute-start(f32[16,128,128]{2,1,0:T(8,128)S(1)} %copy-done.10), channel_id=1, source_target_pairs={{0,64},{8,72},{16,80},{24,88},{32,96},{40,104},{48,112},{56,120},{... | collective-permute-start | bytes 3145736 | tf_op jit(solution)/shard_map/ppermute | solution.py:568
  281.2 21.3 %copy-start.17 = (f32[384,768]{1,0:T(8,128)}, f32[384,768]{1,0:T(8,128)S(1)}, u32[]{:S(2)}) copy-start(f32[384,768]{1,0:T(8,128)S(1)} %collective-permute-done.17.pz) | copy-start | bytes 3538948
  282.2 32.3 %collective-permute-start.18 = (f32[192,768]{1,0:T(8,128)}, f32[192,768]{1,0:T(8,128)}, u32[]{:S(2)}, u32[]{:S(2)}) collective-permute-start(f32[192,768]{1,0:T(8,128)} %slice.44), channel_id=1, source_target_pairs={{0,4},{1,5},{2,6},{3,7},{4,0},{5,1},{6,2},{7,3},{8,12},{9,13},{10,... | collective-permute-start | bytes 1769480 | tf_op jit(solution)/shard_map/ppermute | solution.py:568
  283.3 19.2 %copy-start.18 = (f32[384,768]{1,0:T(8,128)}, f32[384,768]{1,0:T(8,128)S(1)}, u32[]{:S(2)}) copy-start(f32[384,768]{1,0:T(8,128)S(1)} %collective-permute-done.16.px) | copy-start | bytes 3538948
  284.2 30.3 %collective-permute-start.19 = (f32[192,768]{1,0:T(8,128)}, f32[192,768]{1,0:T(8,128)}, u32[]{:S(2)}, u32[]{:S(2)}) collective-permute-start(f32[192,768]{1,0:T(8,128)} %slice.45), channel_id=1, source_target_pairs={{0,64},{8,72},{16,80},{24,88},{32,96},{40,104},{48,112},{56,120},{... | collective-permute-start | bytes 1769480 | tf_op jit(solution)/shard_map/ppermute | solution.py:568
  (20 other events, 137.5 us)

commit v4 on v3

--- a/solution.py
+++ b/solution.py
@@ -35,7 +35,7 @@
     return f(ah, bh) + (f(ah, bl) + f(al, bh))
 
 
-def call(kernel, args, specs, outs, scratch, flops=0, grid=(1,)):
+def call(kernel, args, specs, outs, scratch, flops=0, out_specs=None, aliases=None):
     whole = pl.BlockSpec(memory_space=pltpu.VMEM)
     in_specs = [whole if s is None else s for s in specs]
     nbytes = sum(4 * a.size for a in args[1:]) + sum(4 * o.size for o in outs)
@@ -43,12 +43,13 @@
         kernel,
         grid_spec=pltpu.PrefetchScalarGridSpec(
             num_scalar_prefetch=1,
-            grid=grid,
+            grid=(1,),
             in_specs=in_specs,
-            out_specs=[whole] * len(outs),
+            out_specs=out_specs or [whole] * len(outs),
             scratch_shapes=scratch,
         ),
         out_shape=outs,
+        input_output_aliases=aliases or {},
         compiler_params=pltpu.CompilerParams(vmem_limit_bytes=60 * 1024 * 1024),
         cost_estimate=pl.CostEstimate(flops=flops, bytes_accessed=nbytes, transcendentals=0),
     )(*args)
@@ -69,13 +70,9 @@
         inv_ref[s_ref[first + i]] = i
 
 
-def gather_one_kernel(half_lo, s_ref, c_ref, p_ref, a_ref, b_ref, coup_ref, inv):
-    side = lax.axis_index("lo") // half_lo
-    invert(s_ref, OWN, NC, inv, 18)
-
-    for c in range(NP):
-        out_ref = a_ref if c < 2 else b_ref
-        base = BY_COL.index((c, c)) - (0 if c < 2 else 11) - c
+def gather_tiles(side, inv, c_ref, p_ref, out_ref, first, last, skip):
+    for c in range(first, last):
+        base = BY_COL.index((c, c)) - skip - c
 
         def tile(r, _):
             at = base + r
@@ -96,6 +93,18 @@
             return 0
 
         lax.fori_loop(c, NP, tile, 0)
+
+
+def gather_a_kernel(half_lo, s_ref, c_ref, p_ref, a_ref, inv):
+    side = lax.axis_index("lo") // half_lo
+    invert(s_ref, OWN, NC, inv, 18)
+    gather_tiles(side, inv, c_ref, p_ref, a_ref, 0, 2, 0)
+
+
+def gather_b_kernel(half_lo, s_ref, c_ref, p_ref, b_ref, coup_ref, inv):
+    side = lax.axis_index("lo") // half_lo
+    invert(s_ref, OWN, NC, inv, 18)
+    gather_tiles(side, inv, c_ref, p_ref, b_ref, 2, NP, 11)
 
     def coup_tile(t, count):
         row = inv[NP + (1 - side) * 6 + t // NP]
@@ -330,13 +339,36 @@
     send_ref[...] = p_ref[:, pl.ds(pl.multiple_of((1 - side) * 384, T), 384)]
 
 
-def own_kernel(s_ref, p_ref, t0_ref, t1_ref, own_ref, ph, plo):
+def own_kernel(
+    s_ref, p_ref, t0_ref, t1_ref, c_ref, pv_ref, own_ref, piv_ref, ph, plo, wide, inv, inv2
+):
     side = s_ref[SLO]
+    quarter = 2 * s_ref[SHI] + side
     ph[...], plo[...] = split(p_ref[...])
     for n in range(3):
         s = slice(n * 256, n * 256 + 256)
         base = jnp.where(side == 0, t0_ref[:, s], t1_ref[:, s])
         own_ref[:, s] = base - dot3((ph[...], plo[...]), (ph[s, :], plo[s, :]), NT)
+    invert(s_ref, OWN, NC, inv, 18)
+    invert(s_ref, MAP2, NU, inv2, 18)
+    wide[...] = jnp.zeros_like(wide)
+    wide[pl.ds(pl.multiple_of((quarter % 2) * 64, 64), 192), :] = pv_ref[...]
+    base = (3 * quarter) // 2
+
+    def emit(row, _):
+        def col(c, _):
+            at = row * (row + 1) // 2 + c
+            source_tile(side, inv, inv2, own_ref, None, c_ref, piv_ref, at, row, c)
+
+            @pl.when((row >= base) & (row < base + 2))
+            def _():
+                piv_ref[at] += wide[tl(row - base), tl(c)]
+
+            return 0
+
+        return lax.fori_loop(0, row + 1, col, 0)
+
+    lax.fori_loop(0, NP, emit, 0)
 
 
 def source_tile(side, inv, inv2, own_ref, cross_ref, c_ref, out_ref, at, r, c):
@@ -354,15 +386,20 @@
     def _():
         out_ref[at] = own_ref[tl(li), tl(lj)]
 
-    @pl.when(used & mi & jnp.logical_not(mj))
-    def _():
-        out_ref[at] = cross_ref[tl(li), tl(lj)]
-
-    @pl.when(used & jnp.logical_not(mi) & mj)
-    def _():
-        out_ref[at] = cross_ref[tl(lj), tl(li)].T
-
-    @pl.when(jnp.logical_not(used) | (jnp.logical_not(mi) & jnp.logical_not(mj)))
+    if cross_ref is None:
+        empty = jnp.logical_not(used & mi & mj)
+    else:
+        empty = jnp.logical_not(used) | (jnp.logical_not(mi) & jnp.logical_not(mj))
+
+        @pl.when(used & mi & jnp.logical_not(mj))
+        def _():
+            out_ref[at] = cross_ref[tl(li), tl(lj)]
+
+        @pl.when(used & jnp.logical_not(mi) & mj)
+        def _():
+            out_ref[at] = cross_ref[tl(lj), tl(li)].T
+
+    @pl.when(empty)
     def _():
         out_ref[at] = jnp.zeros((T, T), f32)
 
@@ -374,32 +411,36 @@
         out_ref[at] += c_ref[tl(ci), tl(cj)]
 
 
-def cross_kernel(
-    s_ref, p_ref, q_ref, t1_ref, own_ref, c_ref, pv_ref, cross_ref, a_ref, b_ref, wide, inv, inv2
-):
+def cross_kernel(s_ref, p_ref, q_ref, t1_ref, piv_ref, cross_ref, a_ref, b_ref, inv2):
     side = s_ref[SLO]
-    quarter = 2 * s_ref[SHI] + side
-    mine = pl.ds(pl.multiple_of(side * 384, T), 384)
-    pc = split(p_ref[:, mine])
+    pc = split(p_ref[...])
     qh, ql = split(q_ref[...])
     for n in range(3):
         s = slice(n * 256, n * 256 + 256)
         base = jnp.where(side == 0, t1_ref[:, s], 0.0)
         cross_ref[:, s] = base - dot3(pc, (qh[s, :], ql[s, :]), NT)
-    invert(s_ref, OWN, NC, inv, 18)
     invert(s_ref, MAP2, NU, inv2, 18)
-    wide[...] = jnp.zeros_like(wide)
-    wide[pl.ds(pl.multiple_of((quarter % 2) * 64, 64), 192), :] = pv_ref[...]
-    base = (3 * quarter) // 2
+    a_ref[...] = piv_ref[0:10]
+    b_ref[...] = piv_ref[10:21]
 
     def emit(out_ref, first, row):
         def col(c, _):
             at = row * (row + 1) // 2 + c - first
-            source_tile(side, inv, inv2, own_ref, cross_ref, c_ref, out_ref, at, row, c)
-
-            @pl.when((row >= base) & (row < base + 2))
+            i = inv2[row]
+            j = inv2[c]
+            used = (i >= 0) & (j >= 0)
+            i = jnp.maximum(i, 0)
+            j = jnp.maximum(j, 0)
+            mi = (i // 6) == side
+            mj = (j // 6) == side
+
+            @pl.when(used & mi & jnp.logical_not(mj))
             def _():
-                out_ref[at] += wide[tl(row - base), tl(c)]
+                out_ref[at] += cross_ref[tl(i % 6), tl(j % 6)]
+
+            @pl.when(used & jnp.logical_not(mi) & mj)
+            def _():
+                out_ref[at] += cross_ref[tl(j % 6), tl(i % 6)].T
 
             return 0
 
@@ -547,20 +588,19 @@
             add(pair, r, c, v)
 
 
-def schur_kernel(s_ref, b_ref, p_ref, px, pz, pd0, pd1, out_ref):
+def schur_near_kernel(s_ref, b_ref, p_ref, px, pz, out_ref):
     hi = s_ref[SHI]
     lo = s_ref[SLO]
     mine = split(p_ref[...])
-
-    def minus(a, b, other):
+    out_ref[...] = b_ref[...]
+    for a, b, other in ((1 - hi, lo, px), (hi, 1 - lo, pz)):
         cols = pl.ds(pl.multiple_of((2 * a + b) * 384, T), 384)
-        out_ref[:, cols] = b_ref[:, cols] - dot3(mine, split(other), NT)
-
-    minus(1 - hi, lo, px[...])
-    minus(hi, 1 - lo, pz[...])
-    minus(1 - hi, 1 - lo, jnp.concatenate([pd0[...], pd1[...]], axis=0))
-    cols = pl.ds(pl.multiple_of((2 * hi + lo) * 384, T), 384)
-    out_ref[:, cols] = b_ref[:, cols]
+        out_ref[:, cols] = b_ref[:, cols] - dot3(mine, split(other[...]), NT)
+
+
+def schur_far_kernel(s_ref, b_ref, p_ref, pd0, pd1, out_ref):
+    other = split(jnp.concatenate([pd0[...], pd1[...]], axis=0))
+    out_ref[...] = b_ref[...] - dot3(split(p_ref[...]), other, NT)
 
 
 def across(axis, values):
@@ -599,17 +639,27 @@
     smem = pltpu.SMEM((18,), i32)
     n = NP * T
 
-    piv_a, piv_b, coup = call(
-        functools.partial(gather_one_kernel, half_lo),
-        [map_one[hi, lo], c, pivot_one[0, 0]],
+    own_map = map_one[hi, lo]
+    (piv_a,) = call(
+        functools.partial(gather_a_kernel, half_lo),
+        [own_map, c, pivot_one[0, 0]],
+        [None, block(384, 256, 0)],
+        [shape(11, T, T)],
+        [smem],
+    )
+    piv_a, map_one, map_two, fill_one, fill_two, live_one, live_two, own_map = (
+        lax.optimization_barrier(
+            (piv_a, map_one, map_two, fill_one, fill_two, live_one, live_two, own_map)
+        )
+    )
+    got_a = across("lo", piv_a)
+    piv_b, coup = call(
+        functools.partial(gather_b_kernel, half_lo),
+        [own_map, c, pivot_one[0, 0]],
         [None, None],
-        [shape(11, T, T), shape(10, T, T), shape(16, T, T)],
+        [shape(10, T, T), shape(16, T, T)],
         [smem],
     )
-    piv_a, map_one, map_two, fill_one, fill_two, live_one, live_two = lax.optimization_barrier(
-        (piv_a, map_one, map_two, fill_one, fill_two, live_one, live_two)
-    )
-    got_a = across("lo", piv_a)
     scalars = jnp.concatenate(
         [
             map_one[hi, lo],
@@ -642,20 +692,20 @@
         flops=3_000_000_000,
     )
     got = across("lo", send)
-    (own,) = call(
+    own, piv = call(
         own_kernel,
-        [scalars, panel_one, rows1, rows1],
-        [None, block(n, n, 1), block(n, n, 2)],
-        [shape(n, n)],
-        [pltpu.VMEM((n, n), bf16)] * 2,
+        [scalars, panel_one, rows1, rows1, c, pivot_two[0, 0]],
+        [None, block(n, n, 1), block(n, n, 2), None, None],
+        [shape(n, n), shape(21, T, T)],
+        [pltpu.VMEM((n, n), bf16)] * 2 + [pltpu.VMEM((2 * T, n), f32), smem, smem],
         flops=4_000_000_000,
     )
     cross, pa, pb = call(
         cross_kernel,
-        [scalars, panel_one, got, rows1, own, c, pivot_two[0, 0]],
-        [None, None, block(n, n, 2), None, None, None],
+        [scalars, panel_one, got, rows1, piv],
+        [pl.BlockSpec((n, n // 2), lambda i, s: (0, s[SLO])), None, block(n, n, 2), None],
         [shape(n, n), shape(10, T, T), shape(11, T, T)],
-        [pltpu.VMEM((2 * T, n), f32), smem, smem],
+        [smem],
         flops=2_000_000_000,
     )
     pa1 = across("hi", pa)
@@ -716,13 +766,24 @@
         [],
         flops=1_000_000_000,
     )
-    (schur_two,) = call(
-        schur_kernel,
-        [scalars, base_two, panel_two, px, pz, pd0, pd1],
-        [None] * 6,
+    (near_two,) = call(
+        schur_near_kernel,
+        [scalars, base_two, panel_two, px, pz],
+        [None] * 4,
         [shape(384, NU * T)],
         [],
-        flops=3_000_000_000,
+        flops=2_000_000_000,
+    )
+    far = pl.BlockSpec((384, 384), lambda i, s: (0, 2 * (1 - s[SHI]) + 1 - s[SLO]))
+    (schur_two,) = call(
+        schur_far_kernel,
+        [scalars, near_two, panel_two, pd0, pd1],
+        [far, None, None, None],
+        [shape(384, NU * T)],
+        [],
+        flops=1_000_000_000,
+        out_specs=[far],
+        aliases={1: 0},
     )
     return tuple(
         out[None, None] for out in (lower_one, panel_one, lower_two, panel_two, schur_two)

time: 327 us -> 328 us (level)
  Pallas kernels: 159 us -> 165 us
  starting transfers between devices: 46.1 us -> 40.3 us
    pallas_call x13 -> x15, Pallas kernels: 159 us -> 165 us  [call(): pl.pallas_call(kernel, grid_spec=pltpu.PrefetchScalarGridSpec(num_scalar_...]
    ppermute x20, starting transfers between devices: 46.1 us -> 40.3 us  [across(): return lax.ppermute(values, axis, [(i, i ^ size // 2) for i in range(size)])]
    unnamed x48 -> x42, local copies, waits for them, and re-layouts: 6.86 us -> 5.89 us
  transfers between devices with their start and end apart: 20 -> 20, of which waited for: 11 -> 11; matrix products, arithmetic and copies ran while one was open for 5% -> 5% of each run, Pallas kernels for 35% -> 39%
where the time goes in v4:
time: 328 us; the launch traced here: 323 us
  Pallas kernels  165 us (50%)
  waiting for transfers between devices  94.8 us (29%)
  starting transfers between devices  40.3 us (12%)
  local copies, waits for them, and re-layouts  16.5 us (5%)
  other arithmetic  5.7 us (2%)
    pallas_call x15, Pallas kernels, call(): pl.pallas_call(kernel, grid_spec=pltpu.PrefetchScalarGridSpec(num_scalar_...  165 us
    ppermute x20, waiting for transfers between devices, across(): return lax.ppermute(values, axis, [(i, i ^ size // 2) for i in range(size)])  94.8 us
    ppermute x20, starting transfers between devices, across(): return lax.ppermute(values, axis, [(i, i ^ size // 2) for i in range(size)])  40.3 us
  transfers between devices with their start and end apart: 20, of which 11 were waited for; matrix products, arithmetic and copies ran while one was open for 5% of the time, Pallas kernels for 39%

profile of v4, /device:TPU:0, one launch (start us, length us, event | category | flops | bytes accessed | tf_op | source)
XLA Modules:
  0.0 323.4 jit_solution(1812281153872152709)
XLA Ops:
  2.1 4.1 %shard_map.146.refs_0_ = f32[11,128,128]{2,1,0:T(8,128)} custom-call(s32[8]{0:T(128)} %dynamic-slice_reduce_fusion.2.s_ref, f32[1024,1024]{1,0:T(8,128)} %bitcast.16, f32[384,768]{1,0:T(8,128)} %bitcast.31), custom_call_target="tpu_custom_call" | custom-call | bytes 6094848 | tf_op jit(solution)/shard_map/pallas_call | solution.py:42
  6.2 4.0 %collective-permute-start = (f32[11,128,128]{2,1,0:T(8,128)}, f32[11,128,128]{2,1,0:T(8,128)S(1)}, u32[]{:S(2)}, u32[]{:S(2)}) collective-permute-start(f32[11,128,128]{2,1,0:T(8,128)} %shard_map.146.refs_0_), channel_id=1, source_target_pairs={{0,64},{8,72},{16,80},{24,88},{32,96},{40,104},{48,112},{56,120},{... | collective-permute-start | bytes 2162696 | tf_op jit(solution)/shard_map/ppermute | solution.py:608
  14.0 5.6 %shard_map.147 = (f32[10,128,128]{2,1,0:T(8,128)}, f32[16,128,128]{2,1,0:T(8,128)}) custom-call(s32[8]{0:T(128)} %dynamic-slice_reduce_fusion.2.s_ref, f32[1024,1024]{1,0:T(8,128)} %bitcast.17, f32[384,768]{1,0:T(8,128)} %bitcast.32), custom_call_target="tpu_custom_call" | custom-call | bytes 7077888 | tf_op jit(solution)/shard_map/pallas_call | solution.py:42
  23.0 6.0 %shard_map.150.x_ref = f32[768,768]{1,0:T(8,128)} custom-call(s32[86]{0:T(128)} %concatenate.3.s_ref, f32[768,2304]{1,0:T(8,128)} %bitcast.22, f32[1024,1024]{1,0:T(8,128)} %bitcast.18), custom_call_target="tpu_custom_call" | custom-call | bytes 13631488 | tf_op jit(solution)/shard_map/pallas_call | solution.py:42
  29.9 10.3 %shard_map.148 = (f32[768,256]{1,0:T(8,128)}, bf16[768,256]{1,0:T(8,128)(2,1)}, bf16[768,256]{1,0:T(8,128)(2,1)}, bf16[256,128]{1,0:T(8,128)(2,1)}, bf16[256,128]{1,0:T(8,128)(2,1)}) custom-call(s32[86]{0:T(128)} %concatenate.3.s_ref, f32[11,128,128]{2,1,0:T(8,128)} %shard_map.146.refs_0_, f32[11,128,128]{2,1,0:T(8,128)} %copy-done.18), custom_call_target="tpu_custom_call" | custom-call | flops 20000000000 | bytes 4063232 | tf_op jit(solution)/shard_map/pallas_call | solution.py:42
  40.2 6.8 %collective-permute-done.1.refs_1_ = f32[10,128,128]{2,1,0:T(8,128)S(1)} collective-permute-done((f32[10,128,128]{2,1,0:T(8,128)S(1)}, f32[10,128,128]{2,1,0:T(8,128)S(1)}, u32[]{:S(2)}, u32[]{:S(2)}) %collective-permute-start.1) | collective-permute-done | bytes 655392 | tf_op jit(solution)/shard_map/ppermute | solution.py:608
  47.9 21.7 %shard_map.149 = (f32[384,768]{1,0:T(8,128)}, bf16[768,768]{1,0:T(8,128)(2,1)}, bf16[768,768]{1,0:T(8,128)(2,1)}, bf16[768,128]{1,0:T(8,128)(2,1)}, bf16[768,128]{1,0:T(8,128)(2,1)}) custom-call(s32[86]{0:T(128)} %concatenate.3.s_ref, f32[10,128,128]{2,1,0:T(8,128)} %get-tuple-element.69.refs_0_, f32[10,128,128]{2,1,0:T(8,128)} %copy-done.20, ...), custom_call_target="tpu_custom_call" | custom-call | flops 20000000000 | bytes 10616832 | tf_op jit(solution)/shard_map/pallas_call | solution.py:42
  73.5 12.4 %shard_map.151 = (f32[768,768]{1,0:T(8,128)}, f32[768,384]{1,0:T(8,128)}) custom-call(s32[86]{0:T(128)} %concatenate.3.s_ref, f32[768,768]{1,0:T(8,128)} %shard_map.150.x_ref, f32[16,128,128]{2,1,0:T(8,128)} %copy-done.17, bf16[768,768]{1,0:T(8,128)(2,1)} %get-tuple-element.80.lh, bf16[768,768]{1,0:T(8,128)(2,1)} %get-tuple-element.81.ll, ...), custom_call_target="tpu_custom_call" | custom-call | flops 3000000000 | bytes 12451840 | tf_op jit(solution)/shard_map/pallas_call | solution.py:42
  86.1 11.2 %shard_map.152 = (f32[768,768]{1,0:T(8,128)}, f32[21,128,128]{2,1,0:T(8,128)}) custom-call(s32[86]{0:T(128)} %concatenate.3.s_ref, f32[768,768]{1,0:T(8,128)} %get-tuple-element.84.p_ref, f32[768,2304]{1,0:T(8,128)} %bitcast.23, f32[768,2304]{1,0:T(8,128)} %bitcast.24, f32[1024,1024]{1,0:T(8,128)} %bitcast.19, f32[192,768]{1,0:T(8,128)} %bitcast.33), custom_call_target="tpu_custom_call" | custom-call | flops 4000000000 | bytes 25034752 | tf_op jit(solution)/shard_map/pallas_call | solution.py:42
  97.3 12.7 %collective-permute-done.3.q_ref = f32[768,384]{1,0:T(8,128)S(1)} collective-permute-done((f32[768,384]{1,0:T(8,128)}, f32[768,384]{1,0:T(8,128)S(1)}, u32[]{:S(2)}, u32[]{:S(2)}) %collective-permute-start.3) | collective-permute-done | bytes 1179680 | tf_op jit(solution)/shard_map/ppermute | solution.py:608
  110.9 8.4 %shard_map.153 = (f32[768,768]{1,0:T(8,128)}, f32[10,128,128]{2,1,0:T(8,128)}, f32[11,128,128]{2,1,0:T(8,128)}) custom-call(s32[86]{0:T(128)} %concatenate.3.s_ref, f32[768,768]{1,0:T(8,128)} %get-tuple-element.84.p_ref, f32[768,384]{1,0:T(8,128)} %copy-done.9, f32[768,2304]{1,0:T(8,128)} %bitcast.25, f32[21,128,128]{2,1,0:T(8,128)} %get-tuple-element.86.piv_ref), custom_call_target="tpu_custom_call" | custom-call | flops 2000000000 | bytes 15728640 | tf_op jit(solution)/shard_map/pallas_call | solution.py:42
  119.6 6.6 %collective-permute-start.4 = (f32[10,128,128]{2,1,0:T(8,128)}, f32[10,128,128]{2,1,0:T(8,128)S(1)}, u32[]{:S(2)}, u32[]{:S(2)}) collective-permute-start(f32[10,128,128]{2,1,0:T(8,128)} %get-tuple-element.90), channel_id=1, source_target_pairs={{0,4},{1,5},{2,6},{3,7},{4,0},{5,1},{6,2},{7,3},{8,12},{9,13},{10,... | collective-permute-start | bytes 1966088 | tf_op jit(solution)/shard_map/ppermute | solution.py:608
  126.2 12.8 %shard_map.154 = (f32[18,128,128]{2,1,0:T(8,128)}, f32[18,128,128]{2,1,0:T(8,128)}, f32[18,128,128]{2,1,0:T(8,128)}, f32[18,128,128]{2,1,0:T(8,128)}) custom-call(s32[86]{0:T(128)} %concatenate.3.s_ref, f32[768,768]{1,0:T(8,128)} %get-tuple-element.92.own_ref, f32[768,768]{1,0:T(8,128)} %get-tuple-element.93.cross_ref, f32[1024,1024]{1,0:T(8,128)} %bitcast.20), custom_call_target="tpu_custom_call" | custom-call | bytes 13631488 | tf_op jit(solution)/shard_map/pallas_call | solution.py:42
  146.7 14.4 %shard_map.156 = (f32[23,128,128]{2,1,0:T(8,128)}, f32[23,128,128]{2,1,0:T(8,128)}, f32[25,128,128]{2,1,0:T(8,128)}, f32[25,128,128]{2,1,0:T(8,128)}) custom-call(s32[86]{0:T(128)} %concatenate.3.s_ref, f32[768,768]{1,0:T(8,128)} %get-tuple-element.92.own_ref, f32[768,768]{1,0:T(8,128)} %get-tuple-element.93.cross_ref, f32[1024,1024]{1,0:T(8,128)} %bitcast.21), custom_call_target="tpu_custom_call" | custom-call | bytes 15204352 | tf_op jit(solution)/shard_map/pallas_call | solution.py:42
  168.2 29.3 %shard_map.155 = (f32[192,768]{1,0:T(8,128)}, bf16[768,768]{1,0:T(8,128)(2,1)}, bf16[768,768]{1,0:T(8,128)(2,1)}, bf16[768,128]{1,0:T(8,128)(2,1)}, bf16[768,128]{1,0:T(8,128)(2,1)}) custom-call(s32[86]{0:T(128)} %concatenate.3.s_ref, f32[10,128,128]{2,1,0:T(8,128)} %add.88.refs_0_, f32[10,128,128]{2,1,0:T(8,128)} %collective-permute-done.6.refs_1_, ...), custom_call_target="tpu_custom_call" | custom-call | flops 20000000000 | bytes 8847360 | tf_op jit(solution)/shard_map/pallas_call | solution.py:42
  197.5 22.3 %collective-permute-done.8.x1 = f32[18,128,128]{2,1,0:T(8,128)} collective-permute-done((f32[18,128,128]{2,1,0:T(8,128)}, f32[18,128,128]{2,1,0:T(8,128)}, u32[]{:S(2)}, u32[]{:S(2)}) %collective-permute-start.8) | collective-permute-done | bytes 1179680 | tf_op jit(solution)/shard_map/ppermute | solution.py:608
  221.9 3.6 %collective-permute-done.12.z1 = f32[18,128,128]{2,1,0:T(8,128)} collective-permute-done((f32[18,128,128]{2,1,0:T(8,128)}, f32[18,128,128]{2,1,0:T(8,128)}, u32[]{:S(2)}, u32[]{:S(2)}) %collective-permute-start.12) | collective-permute-done | bytes 1179680 | tf_op jit(solution)/shard_map/ppermute | solution.py:608
  238.9 9.4 %shard_map.157.p_ref = f32[384,768]{1,0:T(8,128)} custom-call(s32[86]{0:T(128)} %concatenate.3.s_ref, f32[384,2304]{1,0:T(8,128)} %bitcast.27, f32[18,128,128]{2,1,0:T(8,128)} %get-tuple-element.99.xk, f32[18,128,128]{2,1,0:T(8,128)} %collective-permute-done.8.x1, f32[9,128,128]{2,1,0:T(8,128)} %copy-done.14, f32[18,128,128]{2,1,0:T(8,128)} %get-tuple-element.105.zk, ...), custom_call_target="tpu_custom_call" | custom-call | flops 2000000000 | bytes 16121856 | tf_op jit(solution)/shard_map/pallas_call | solution.py:42
  248.9 3.5 %collective-permute-start.16 = (f32[384,768]{1,0:T(8,128)}, f32[384,768]{1,0:T(8,128)S(1)}, u32[]{:S(2)}, u32[]{:S(2)}) collective-permute-start(f32[384,768]{1,0:T(8,128)} %shard_map.157.p_ref), channel_id=1, source_target_pairs={{0,4},{1,5},{2,6},{3,7},{4,0},{5,1},{6,2},{7,3},{8,12},{9,13},{10,... | collective-permute-start | bytes 3538952 | tf_op jit(solution)/shard_map/ppermute | solution.py:608
  255.4 23.5 %collective-permute-done.17.pz = f32[384,768]{1,0:T(8,128)S(1)} collective-permute-done((f32[384,768]{1,0:T(8,128)}, f32[384,768]{1,0:T(8,128)S(1)}, u32[]{:S(2)}, u32[]{:S(2)}) %collective-permute-start.17) | collective-permute-done | bytes 1179680 | tf_op jit(solution)/shard_map/ppermute | solution.py:608
  284.9 16.3 %collective-permute-done.14.x2 = f32[16,128,128]{2,1,0:T(8,128)} collective-permute-done((f32[16,128,128]{2,1,0:T(8,128)}, f32[16,128,128]{2,1,0:T(8,128)}, u32[]{:S(2)}, u32[]{:S(2)}) %collective-permute-start.14) | collective-permute-done | bytes 1048608 | tf_op jit(solution)/shard_map/ppermute | solution.py:608
  303.5 8.5 %shard_map.158.b_ref = f32[384,1536]{1,0:T(8,128)} custom-call(s32[86]{0:T(128)} %concatenate.3.s_ref, f32[384,2304]{1,0:T(8,128)} %bitcast.28, f32[384,768]{1,0:T(8,128)} %shard_map.157.p_ref, f32[23,128,128]{2,1,0:T(8,128)} %get-tuple-element.101.xk, f32[23,128,128]{2,1,0:T(8,128)} %copy-done.5, f32[16,128,128]{2,1,0:T(8,128)} %collective-permute-done.14.x2, ...), custom_call_target="tpu_custom_call" | custom-call | flops 1000000000 | bytes 15532032 | tf_op jit(solution)/shard_map/pallas_call | solution.py:42
  312.1 6.9 %shard_map.159.b_ref = f32[384,1536]{1,0:T(8,128)} custom-call(s32[86]{0:T(128)} %concatenate.3.s_ref, f32[384,1536]{1,0:T(8,128)} %shard_map.158.b_ref, f32[384,768]{1,0:T(8,128)} %shard_map.157.p_ref, f32[384,768]{1,0:T(8,128)} %copy-done.8, f32[384,768]{1,0:T(8,128)} %copy-done.7), custom_call_target="tpu_custom_call" | custom-call | flops 2000000000 | bytes 8257536 | tf_op jit(solution)/shard_map/pallas_call | solution.py:42
  318.9 4.5 %shard_map.160 = f32[384,1536]{1,0:T(8,128)} custom-call(s32[86]{0:T(128)} %concatenate.3.s_ref, f32[384,1536]{1,0:T(8,128)} %shard_map.159.b_ref, f32[384,768]{1,0:T(8,128)} %shard_map.157.p_ref, f32[192,768]{1,0:T(8,128)} %collective-permute-done.18.pd0, f32[192,768]{1,0:T(8,128)} %collective-permute-done.19.pd1), custom_call_target="tpu_custom_call", output_to_operand_aliasing={{}: (1, {})} | custom-call | flops 1000000000 | bytes 7077888 | tf_op jit(solution)/shard_map/pallas_call | solution.py:42
  (93 shorter events, 58.0 us)
Async XLA Ops:
  6.2 22.9 %collective-permute-start = (f32[11,128,128]{2,1,0:T(8,128)}, f32[11,128,128]{2,1,0:T(8,128)S(1)}, u32[]{:S(2)}, u32[]{:S(2)}) collective-permute-start(f32[11,128,128]{2,1,0:T(8,128)} %shard_map.146.refs_0_), channel_id=1, source_target_pairs={{0,64},{8,72},{16,80},{24,88},{32,96},{40,104},{48,112},{56,120},{... | collective-permute-start | bytes 2162696 | tf_op jit(solution)/shard_map/ppermute | solution.py:608
  29.1 18.0 %collective-permute-start.1 = (f32[10,128,128]{2,1,0:T(8,128)S(1)}, f32[10,128,128]{2,1,0:T(8,128)S(1)}, u32[]{:S(2)}, u32[]{:S(2)}) collective-permute-start(f32[10,128,128]{2,1,0:T(8,128)S(1)} %copy-done.19), channel_id=1, source_target_pairs={{0,64},{8,72},{16,80},{24,88},{32,96},{40,104},{48,112},{56,120},{... | collective-permute-start | bytes 1966088 | tf_op jit(solution)/shard_map/ppermute | solution.py:608
  47.0 25.5 %collective-permute-start.2 = (f32[16,128,128]{2,1,0:T(8,128)S(1)}, f32[16,128,128]{2,1,0:T(8,128)S(1)}, u32[]{:S(2)}, u32[]{:S(2)}) collective-permute-start(f32[16,128,128]{2,1,0:T(8,128)S(1)} %copy-done.16), channel_id=1, source_target_pairs={{0,64},{8,72},{16,80},{24,88},{32,96},{40,104},{48,112},{56,120},{... | collective-permute-start | bytes 3145736 | tf_op jit(solution)/shard_map/ppermute | solution.py:608
  85.9 24.1 %collective-permute-start.3 = (f32[768,384]{1,0:T(8,128)}, f32[768,384]{1,0:T(8,128)S(1)}, u32[]{:S(2)}, u32[]{:S(2)}) collective-permute-start(f32[768,384]{1,0:T(8,128)} %get-tuple-element.85), channel_id=1, source_target_pairs={{0,64},{8,72},{16,80},{24,88},{32,96},{40,104},{48,112},{56,120},{... | collective-permute-start | bytes 3538952 | tf_op jit(solution)/shard_map/ppermute | solution.py:608
  119.3 21.4 %collective-permute-start.5 = (f32[11,128,128]{2,1,0:T(8,128)}, f32[11,128,128]{2,1,0:T(8,128)S(1)}, u32[]{:S(2)}, u32[]{:S(2)}) collective-permute-start(f32[11,128,128]{2,1,0:T(8,128)} %get-tuple-element.91), channel_id=1, source_target_pairs={{0,64},{8,72},{16,80},{24,88},{32,96},{40,104},{48,112},{56,120},{... | collective-permute-start | bytes 2162696 | tf_op jit(solution)/shard_map/ppermute | solution.py:608
  119.6 20.2 %collective-permute-start.4 = (f32[10,128,128]{2,1,0:T(8,128)}, f32[10,128,128]{2,1,0:T(8,128)S(1)}, u32[]{:S(2)}, u32[]{:S(2)}) collective-permute-start(f32[10,128,128]{2,1,0:T(8,128)} %get-tuple-element.90), channel_id=1, source_target_pairs={{0,4},{1,5},{2,6},{3,7},{4,0},{5,1},{6,2},{7,3},{8,12},{9,13},{10,... | collective-permute-start | bytes 1966088 | tf_op jit(solution)/shard_map/ppermute | solution.py:608
  140.8 20.3 %copy-start.11 = (f32[11,128,128]{2,1,0:T(8,128)}, f32[11,128,128]{2,1,0:T(8,128)S(1)}, u32[]{:S(2)}) copy-start(f32[11,128,128]{2,1,0:T(8,128)S(1)} %add.89.refs_2_) | copy-start | bytes 2162692
  140.8 27.4 %collective-permute-start.7 = (f32[11,128,128]{2,1,0:T(8,128)S(1)}, f32[11,128,128]{2,1,0:T(8,128)}, u32[]{:S(2)}, u32[]{:S(2)}) collective-permute-start(f32[11,128,128]{2,1,0:T(8,128)S(1)} %add.89.refs_2_), channel_id=1, source_target_pairs={{0,4},{1,5},{2,6},{3,7},{4,0},{5,1},{6,2},{7,3},{8,12},{9,13},{10,... | collective-permute-start | bytes 2162696 | tf_op jit(solution)/shard_map/ppermute | solution.py:608
  144.1 20.9 %collective-permute-start.6 = (f32[10,128,128]{2,1,0:T(8,128)}, f32[10,128,128]{2,1,0:T(8,128)}, u32[]{:S(2)}, u32[]{:S(2)}) collective-permute-start(f32[10,128,128]{2,1,0:T(8,128)} %add.88.refs_0_), channel_id=1, source_target_pairs={{0,64},{8,72},{16,80},{24,88},{32,96},{40,104},{48,112},{56,120},{... | collective-permute-start | bytes 1966088 | tf_op jit(solution)/shard_map/ppermute | solution.py:608
  161.1 68.5 %collective-permute-start.9 = (f32[23,128,128]{2,1,0:T(8,128)}, f32[23,128,128]{2,1,0:T(8,128)S(1)}, u32[]{:S(2)}, u32[]{:S(2)}) collective-permute-start(f32[23,128,128]{2,1,0:T(8,128)} %get-tuple-element.102), channel_id=1, source_target_pairs={{0,4},{1,5},{2,6},{3,7},{4,0},{5,1},{6,2},{7,3},{8,12},{9,13},{10,... | collective-permute-start | bytes 4521992 | tf_op jit(solution)/shard_map/ppermute | solution.py:608
  161.1 69.6 %collective-permute-start.10 = (f32[25,128,128]{2,1,0:T(8,128)}, f32[25,128,128]{2,1,0:T(8,128)S(1)}, u32[]{:S(2)}, u32[]{:S(2)}) collective-permute-start(f32[25,128,128]{2,1,0:T(8,128)} %get-tuple-element.104), channel_id=1, source_target_pairs={{0,64},{8,72},{16,80},{24,88},{32,96},{40,104},{48,112},{56,120},{... | collective-permute-start | bytes 4915208 | tf_op jit(solution)/shard_map/ppermute | solution.py:608
  161.7 58.0 %collective-permute-start.8 = (f32[18,128,128]{2,1,0:T(8,128)}, f32[18,128,128]{2,1,0:T(8,128)}, u32[]{:S(2)}, u32[]{:S(2)}) collective-permute-start(f32[18,128,128]{2,1,0:T(8,128)} %get-tuple-element.100), channel_id=1, source_target_pairs={{0,4},{1,5},{2,6},{3,7},{4,0},{5,1},{6,2},{7,3},{8,12},{9,13},{10,... | collective-permute-start | bytes 3538952 | tf_op jit(solution)/shard_map/ppermute | solution.py:608
  165.0 60.5 %collective-permute-start.12 = (f32[18,128,128]{2,1,0:T(8,128)}, f32[18,128,128]{2,1,0:T(8,128)}, u32[]{:S(2)}, u32[]{:S(2)}) collective-permute-start(f32[18,128,128]{2,1,0:T(8,128)} %get-tuple-element.106), channel_id=1, source_target_pairs={{0,64},{8,72},{16,80},{24,88},{32,96},{40,104},{48,112},{56,120},{... | collective-permute-start | bytes 3538952 | tf_op jit(solution)/shard_map/ppermute | solution.py:608
  197.5 28.0 %copy-start.6 = (f32[18,128,128]{2,1,0:T(8,128)S(1)}, f32[18,128,128]{2,1,0:T(8,128)}, u32[]{:S(2)}) copy-start(f32[18,128,128]{2,1,0:T(8,128)} %get-tuple-element.105.zk) | copy-start | bytes 3538948
  221.1 14.8 %collective-permute-start.11 = (f32[9,128,128]{2,1,0:T(8,128)S(1)}, f32[9,128,128]{2,1,0:T(8,128)S(1)}, u32[]{:S(2)}, u32[]{:S(2)}) collective-permute-start(f32[9,128,128]{2,1,0:T(8,128)S(1)} %slice_add_fusion.3), channel_id=1, source_target_pairs={{0,64},{8,72},{16,80},{24,88},{32,96},{40,104},{48,112},{56,120},{... | collective-permute-start | bytes 1769480 | tf_op jit(solution)/shard_map/ppermute | solution.py:608
  226.6 11.5 %collective-permute-start.13 = (f32[9,128,128]{2,1,0:T(8,128)S(1)}, f32[9,128,128]{2,1,0:T(8,128)S(1)}, u32[]{:S(2)}, u32[]{:S(2)}) collective-permute-start(f32[9,128,128]{2,1,0:T(8,128)S(1)} %slice_add_fusion.2), channel_id=1, source_target_pairs={{0,4},{1,5},{2,6},{3,7},{4,0},{5,1},{6,2},{7,3},{8,12},{9,13},{10,... | collective-permute-start | bytes 1769480 | tf_op jit(solution)/shard_map/ppermute | solution.py:608
  248.4 30.6 %collective-permute-start.17 = (f32[384,768]{1,0:T(8,128)}, f32[384,768]{1,0:T(8,128)S(1)}, u32[]{:S(2)}, u32[]{:S(2)}) collective-permute-start(f32[384,768]{1,0:T(8,128)} %shard_map.157.p_ref), channel_id=1, source_target_pairs={{0,64},{8,72},{16,80},{24,88},{32,96},{40,104},{48,112},{56,120},{... | collective-permute-start | bytes 3538952 | tf_op jit(solution)/shard_map/ppermute | solution.py:608
  248.9 33.8 %collective-permute-start.16 = (f32[384,768]{1,0:T(8,128)}, f32[384,768]{1,0:T(8,128)S(1)}, u32[]{:S(2)}, u32[]{:S(2)}) collective-permute-start(f32[384,768]{1,0:T(8,128)} %shard_map.157.p_ref), channel_id=1, source_target_pairs={{0,4},{1,5},{2,6},{3,7},{4,0},{5,1},{6,2},{7,3},{8,12},{9,13},{10,... | collective-permute-start | bytes 3538952 | tf_op jit(solution)/shard_map/ppermute | solution.py:608
  252.5 50.0 %collective-permute-start.15 = (f32[17,128,128]{2,1,0:T(8,128)}, f32[17,128,128]{2,1,0:T(8,128)S(1)}, u32[]{:S(2)}, u32[]{:S(2)}) collective-permute-start(f32[17,128,128]{2,1,0:T(8,128)} %slice_add_fusion), channel_id=1, source_target_pairs={{0,4},{1,5},{2,6},{3,7},{4,0},{5,1},{6,2},{7,3},{8,12},{9,13},{10,... | collective-permute-start | bytes 3342344 | tf_op jit(solution)/shard_map/ppermute | solution.py:608
  252.5 48.6 %collective-permute-start.14 = (f32[16,128,128]{2,1,0:T(8,128)}, f32[16,128,128]{2,1,0:T(8,128)}, u32[]{:S(2)}, u32[]{:S(2)}) collective-permute-start(f32[16,128,128]{2,1,0:T(8,128)} %slice_add_fusion.1), channel_id=1, source_target_pairs={{0,64},{8,72},{16,80},{24,88},{32,96},{40,104},{48,112},{56,120},{... | collective-permute-start | bytes 3145736 | tf_op jit(solution)/shard_map/ppermute | solution.py:608
  278.9 33.1 %copy-start.7 = (f32[384,768]{1,0:T(8,128)}, f32[384,768]{1,0:T(8,128)S(1)}, u32[]{:S(2)}) copy-start(f32[384,768]{1,0:T(8,128)S(1)} %collective-permute-done.17.pz) | copy-start | bytes 3538948
  279.8 39.1 %collective-permute-start.18 = (f32[192,768]{1,0:T(8,128)}, f32[192,768]{1,0:T(8,128)}, u32[]{:S(2)}, u32[]{:S(2)}) collective-permute-start(f32[192,768]{1,0:T(8,128)} %slice.44), channel_id=1, source_target_pairs={{0,4},{1,5},{2,6},{3,7},{4,0},{5,1},{6,2},{7,3},{8,12},{9,13},{10,... | collective-permute-start | bytes 1769480 | tf_op jit(solution)/shard_map/ppermute | solution.py:608
  282.7 29.3 %copy-start.8 = (f32[384,768]{1,0:T(8,128)}, f32[384,768]{1,0:T(8,128)S(1)}, u32[]{:S(2)}) copy-start(f32[384,768]{1,0:T(8,128)S(1)} %collective-permute-done.16.px) | copy-start | bytes 3538948
  283.7 35.3 %collective-permute-start.19 = (f32[192,768]{1,0:T(8,128)}, f32[192,768]{1,0:T(8,128)}, u32[]{:S(2)}, u32[]{:S(2)}) collective-permute-start(f32[192,768]{1,0:T(8,128)} %slice.45), channel_id=1, source_target_pairs={{0,64},{8,72},{16,80},{24,88},{32,96},{40,104},{48,112},{56,120},{... | collective-permute-start | bytes 1769480 | tf_op jit(solution)/shard_map/ppermute | solution.py:608
  (17 other events, 97.1 us)

commit v5 on v4

--- a/solution.py
+++ b/solution.py
@@ -13,6 +13,7 @@
 NC = 8
 f32 = jnp.float32
 bf16 = jnp.bfloat16
+NN = ((1,), (0,))
 NT = ((1,), (1,))
 OWN, OTH, MAP2, SLO, SHI, LIVE1, LIVE2, FILL1, FILL2 = 0, 8, 16, 28, 29, 30, 31, 32, 68
 
@@ -274,23 +275,40 @@
     )
 
 
-def solve(x_ref, live, lh_ref, ll_ref, wh_ref, wl_ref, ph, plo):
-    for k in range(NP):
-        s = slice(k * T, k * T + T)
-
-        @pl.when(k < live)
+def solve(x_ref, live, lh_ref, ll_ref, wh_ref, wl_ref, ph, plo, gh, gl):
+    for m in range(NP // 2):
+        a = slice(2 * m * T, 2 * m * T + T)
+        b = slice(2 * m * T + T, 2 * m * T + 2 * T)
+        for g, w in ((gh, wh_ref), (gl, wl_ref)):
+            g[a, :T] = w[a, :]
+            g[a, T:] = jnp.zeros((T, T), bf16)
+
+        @pl.when(2 * m + 1 < live)
+        def _():
+            t = dot3((lh_ref[b, a], ll_ref[b, a]), (wh_ref[a, :], wl_ref[a, :]), NN)
+            gh[b, :T], gl[b, :T] = split(-dot3((wh_ref[b, :], wl_ref[b, :]), split(t), NN))
+            gh[b, T:] = wh_ref[b, :]
+            gl[b, T:] = wl_ref[b, :]
+
+        @pl.when(2 * m + 1 >= live)
+        def _():
+            gh[b, :] = jnp.zeros((T, 2 * T), bf16)
+            gl[b, :] = jnp.zeros((T, 2 * T), bf16)
+
+    for m in range(NP // 2):
+        s = slice(2 * m * T, 2 * m * T + 2 * T)
+
+        @pl.when(2 * m < live)
         def _():
             x = x_ref[:, s]
-            if k:
-                b = slice(0, k * T)
+            if m:
+                b = slice(0, 2 * m * T)
                 x = x - dot3((ph[:, b], plo[:, b]), (lh_ref[s, b], ll_ref[s, b]), NT)
-            x = dot3(split(x), (wh_ref[s, :], wl_ref[s, :]), NT)
+            x = dot3(split(x), (gh[s, :], gl[s, :]), NT)
             x_ref[:, s] = x
-            xh, xl = split(x)
-            ph[:, s] = xh
-            plo[:, s] = xl
-
-        @pl.when(k >= live)
+            ph[:, s], plo[:, s] = split(x)
+
+        @pl.when(2 * m >= live)
         def _():
             x_ref[:, s] = jnp.zeros_like(x_ref[:, s])
             ph[:, s] = jnp.zeros_like(ph[:, s])
@@ -317,7 +335,9 @@
     lax.fori_loop(0, 36, tile, 0)
 
 
-def panel_one_kernel(s_ref, x_ref, got_ref, lh, ll, wh, wl, p_ref, send_ref, ph, plo, inv2):
+def panel_one_kernel(
+    s_ref, x_ref, got_ref, lh, ll, wh, wl, p_ref, send_ref, ph, plo, gh, gl, inv2
+):
     side = s_ref[SLO]
     invert(s_ref, OTH, NC, inv2, 18)
     p_ref[...] = x_ref[...]
@@ -335,7 +355,7 @@
         return count + hit.astype(jnp.int32)
 
     lax.fori_loop(0, 36, tile, 0)
-    solve(p_ref, s_ref[LIVE1], lh, ll, wh, wl, ph, plo)
+    solve(p_ref, s_ref[LIVE1], lh, ll, wh, wl, ph, plo, gh, gl)
     send_ref[...] = p_ref[:, pl.ds(pl.multiple_of((1 - side) * 384, T), 384)]
 
 
@@ -543,7 +563,7 @@
 
 
 def panel_two_kernel(
-    s_ref, r_ref, xk, x1, x2, zk, z1, z2, lh, ll, wh, wl, p_ref, ph, plo
+    s_ref, r_ref, xk, x1, x2, zk, z1, z2, lh, ll, wh, wl, p_ref, ph, plo, gh, gl
 ):
     for r in range(3):
         for c in range(3):
@@ -554,7 +574,7 @@
             dst = (dst[0], slice((c + 3) * T, (c + 4) * T))
             fill = s_ref[FILL2 + 6 * r + c + 3].astype(f32)
             p_ref[dst] = r_ref[dst] * fill + ((zk[9 + t] + z1[9 + t]) + z2[t])
-    solve(p_ref, s_ref[LIVE2], lh, ll, wh, wl, ph, plo)
+    solve(p_ref, s_ref[LIVE2], lh, ll, wh, wl, ph, plo, gh, gl)
 
 
 def schur_base_kernel(s_ref, r_ref, p_ref, xk, x1, x2, zk, z1, z2, out_ref):
@@ -672,23 +692,36 @@
             lax.dynamic_slice_in_dim(fill_two[front_hi, front_lo], quarter * 3, 3, 0).reshape(18),
         ]
     )
-    (x_one,) = call(
-        couple_one_kernel, [scalars, rows1, c], [block(n, n, 0), None], [shape(n, n)], [smem]
-    )
     piv_b, got_a = lax.optimization_barrier((piv_b, got_a))
     got_b = across("lo", piv_b)
     part = factor(scalars, [(piv_a, got_a)], BY_COL, 0, 2, (), LIVE1, None, n)
+    later, *part = lax.optimization_barrier((scalars, *part))
+    (x_one,) = call(
+        couple_one_kernel,
+        [later, rows1, c],
+        [block(n, n, 0), None],
+        [shape(n, n)],
+        [smem],
+    )
     coup, got_b = lax.optimization_barrier((coup, got_b))
     coup_got = across("lo", coup)
     lower_one, *fac1 = factor(
-        scalars, [(piv_b, got_b)], BY_COL[11:], 2, NP, part, LIVE1, lambda s: s[SLO] * 384, 384
+        scalars,
+        [(piv_b, got_b)],
+        BY_COL[11:],
+        2,
+        NP,
+        part,
+        LIVE1,
+        lambda s: s[SLO] * 384,
+        384,
     )
     panel_one, send = call(
         panel_one_kernel,
         [scalars, x_one, coup_got, *fac1],
         [None] * 6,
         [shape(n, n), shape(n, n // 2)],
-        [pltpu.VMEM((n, n), bf16)] * 2 + [smem],
+        [pltpu.VMEM((n, n), bf16)] * 2 + [pltpu.VMEM((n, 2 * T), bf16)] * 2 + [smem],
         flops=3_000_000_000,
     )
     got = across("lo", send)
@@ -743,7 +776,6 @@
     cz2 = across("hi", czk[:9] + cz1[:9])
     tx = txk[:16] + tx1[:16]
     tz = tzk[:17] + tz1[:17]
-    tx, tz, cx2, cz2 = lax.optimization_barrier((tx, tz, cx2, cz2))
     tx2 = across("lo", tx)
     tz2 = across("hi", tz)
     (panel_two,) = call(
@@ -751,7 +783,7 @@
         [scalars, rows2, cxk, cx1, cx2, czk, cz1, cz2, *fac2],
         [block(384, n, 0)] + [None] * 10,
         [shape(384, n)],
-        [pltpu.VMEM((384, n), bf16)] * 2,
+        [pltpu.VMEM((384, n), bf16)] * 2 + [pltpu.VMEM((n, 2 * T), bf16)] * 2,
         flops=2_000_000_000,
     )
     px = across("hi", panel_two)

time: 328 us -> 321 us (0.979)
  waiting for transfers between devices: 94.8 us -> 87.5 us
    ppermute x20, waiting for transfers between devices: 94.8 us -> 87.5 us  [across(): return lax.ppermute(values, axis, [(i, i ^ size // 2) for i in range(size)])]
    unnamed x42 -> x46, local copies, waits for them, and re-layouts: 5.89 us -> 9.65 us
  transfers between devices with their start and end apart: 20 -> 20, of which waited for: 11 -> 9; matrix products, arithmetic and copies ran while one was open for 5% -> 4% of each run, Pallas kernels for 39% -> 43%
where the time goes in v5:
time: 321 us; the launch traced here: 317 us
  Pallas kernels  164 us (51%)
  waiting for transfers between devices  87.5 us (27%)
  starting transfers between devices  40.3 us (13%)
  local copies, waits for them, and re-layouts  19.2 us (6%)
  other arithmetic  5.57 us (2%)
    pallas_call x15, Pallas kernels, call(): pl.pallas_call(kernel, grid_spec=pltpu.PrefetchScalarGridSpec(num_scalar_...  164 us
    ppermute x20, waiting for transfers between devices, across(): return lax.ppermute(values, axis, [(i, i ^ size // 2) for i in range(size)])  87.5 us
    ppermute x20, starting transfers between devices, across(): return lax.ppermute(values, axis, [(i, i ^ size // 2) for i in range(size)])  40.3 us
    unnamed x46, local copies, waits for them, and re-layouts  9.65 us
  transfers between devices with their start and end apart: 20, of which 9 were waited for; matrix products, arithmetic and copies ran while one was open for 4% of the time, Pallas kernels for 43%

profile of v5, /device:TPU:0, one launch (start us, length us, event | category | flops | bytes accessed | tf_op | source)
XLA Modules:
  0.0 317.1 jit_solution(2762162298648019672)
XLA Ops:
  2.1 4.1 %shard_map.146.refs_0_ = f32[11,128,128]{2,1,0:T(8,128)} custom-call(s32[8]{0:T(128)} %dynamic-slice_reduce_fusion.2.s_ref, f32[1024,1024]{1,0:T(8,128)} %bitcast.16, f32[384,768]{1,0:T(8,128)} %bitcast.31), custom_call_target="tpu_custom_call" | custom-call | bytes 6094848 | tf_op jit(solution)/shard_map/pallas_call | solution.py:43
  6.1 4.0 %collective-permute-start = (f32[11,128,128]{2,1,0:T(8,128)}, f32[11,128,128]{2,1,0:T(8,128)S(1)}, u32[]{:S(2)}, u32[]{:S(2)}) collective-permute-start(f32[11,128,128]{2,1,0:T(8,128)} %shard_map.146.refs_0_), channel_id=1, source_target_pairs={{0,64},{8,72},{16,80},{24,88},{32,96},{40,104},{48,112},{56,120},{... | collective-permute-start | bytes 2162696 | tf_op jit(solution)/shard_map/ppermute | solution.py:628
  13.9 5.6 %shard_map.147 = (f32[10,128,128]{2,1,0:T(8,128)}, f32[16,128,128]{2,1,0:T(8,128)}) custom-call(s32[8]{0:T(128)} %dynamic-slice_reduce_fusion.2.s_ref, f32[1024,1024]{1,0:T(8,128)} %bitcast.17, f32[384,768]{1,0:T(8,128)} %bitcast.32), custom_call_target="tpu_custom_call" | custom-call | bytes 7077888 | tf_op jit(solution)/shard_map/pallas_call | solution.py:43
  22.9 3.7 %collective-permute-done.refs_1_ = f32[11,128,128]{2,1,0:T(8,128)S(1)} collective-permute-done((f32[11,128,128]{2,1,0:T(8,128)}, f32[11,128,128]{2,1,0:T(8,128)S(1)}, u32[]{:S(2)}, u32[]{:S(2)}) %collective-permute-start) | collective-permute-done | bytes 720928 | tf_op jit(solution)/shard_map/ppermute | solution.py:628
  29.8 10.3 %shard_map.148 = (f32[768,256]{1,0:T(8,128)}, bf16[768,256]{1,0:T(8,128)(2,1)}, bf16[768,256]{1,0:T(8,128)(2,1)}, bf16[256,128]{1,0:T(8,128)(2,1)}, bf16[256,128]{1,0:T(8,128)(2,1)}) custom-call(s32[86]{0:T(128)} %concatenate.3.s_ref, f32[11,128,128]{2,1,0:T(8,128)} %shard_map.146.refs_0_, f32[11,128,128]{2,1,0:T(8,128)} %copy-done.21), custom_call_target="tpu_custom_call" | custom-call | flops 20000000000 | bytes 4063232 | tf_op jit(solution)/shard_map/pallas_call | solution.py:43
  40.1 6.0 %shard_map.150.x_ref = f32[768,768]{1,0:T(8,128)} custom-call(s32[86]{0:T(128)} %concatenate.3.s_ref, f32[768,2304]{1,0:T(8,128)} %bitcast.22, f32[1024,1024]{1,0:T(8,128)} %bitcast.18), custom_call_target="tpu_custom_call" | custom-call | bytes 13631488 | tf_op jit(solution)/shard_map/pallas_call | solution.py:43
  47.3 21.7 %shard_map.149 = (f32[384,768]{1,0:T(8,128)}, bf16[768,768]{1,0:T(8,128)(2,1)}, bf16[768,768]{1,0:T(8,128)(2,1)}, bf16[768,128]{1,0:T(8,128)(2,1)}, bf16[768,128]{1,0:T(8,128)(2,1)}) custom-call(s32[86]{0:T(128)} %concatenate.3.s_ref, f32[10,128,128]{2,1,0:T(8,128)} %get-tuple-element.71.refs_0_, f32[10,128,128]{2,1,0:T(8,128)} %copy-done.22, ...), custom_call_target="tpu_custom_call" | custom-call | flops 20000000000 | bytes 10616832 | tf_op jit(solution)/shard_map/pallas_call | solution.py:43
  72.6 11.2 %shard_map.151 = (f32[768,768]{1,0:T(8,128)}, f32[768,384]{1,0:T(8,128)}) custom-call(s32[86]{0:T(128)} %concatenate.3.s_ref, f32[768,768]{1,0:T(8,128)} %shard_map.150.x_ref, f32[16,128,128]{2,1,0:T(8,128)} %copy-done.20, bf16[768,768]{1,0:T(8,128)(2,1)} %get-tuple-element.88.lh, bf16[768,768]{1,0:T(8,128)(2,1)} %get-tuple-element.89.ll, ...), custom_call_target="tpu_custom_call" | custom-call | flops 3000000000 | bytes 12451840 | tf_op jit(solution)/shard_map/pallas_call | solution.py:43
  84.9 11.2 %shard_map.152 = (f32[768,768]{1,0:T(8,128)}, f32[21,128,128]{2,1,0:T(8,128)}) custom-call(s32[86]{0:T(128)} %concatenate.3.s_ref, f32[768,768]{1,0:T(8,128)} %get-tuple-element.92.p_ref, f32[768,2304]{1,0:T(8,128)} %bitcast.23, f32[768,2304]{1,0:T(8,128)} %bitcast.24, f32[1024,1024]{1,0:T(8,128)} %bitcast.19, f32[192,768]{1,0:T(8,128)} %bitcast.33), custom_call_target="tpu_custom_call" | custom-call | flops 4000000000 | bytes 25034752 | tf_op jit(solution)/shard_map/pallas_call | solution.py:43
  96.1 13.0 %collective-permute-done.3.q_ref = f32[768,384]{1,0:T(8,128)S(1)} collective-permute-done((f32[768,384]{1,0:T(8,128)}, f32[768,384]{1,0:T(8,128)S(1)}, u32[]{:S(2)}, u32[]{:S(2)}) %collective-permute-start.3) | collective-permute-done | bytes 1179680 | tf_op jit(solution)/shard_map/ppermute | solution.py:628
  110.1 8.3 %shard_map.153 = (f32[768,768]{1,0:T(8,128)}, f32[10,128,128]{2,1,0:T(8,128)}, f32[11,128,128]{2,1,0:T(8,128)}) custom-call(s32[86]{0:T(128)} %concatenate.3.s_ref, f32[768,768]{1,0:T(8,128)} %get-tuple-element.92.p_ref, f32[768,384]{1,0:T(8,128)} %copy-done.10, f32[768,2304]{1,0:T(8,128)} %bitcast.25, f32[21,128,128]{2,1,0:T(8,128)} %get-tuple-element.94.piv_ref), custom_call_target="tpu_custom_call" | custom-call | flops 2000000000 | bytes 15728640 | tf_op jit(solution)/shard_map/pallas_call | solution.py:43
  119.7 5.3 %collective-permute-start.4 = (f32[10,128,128]{2,1,0:T(8,128)}, f32[10,128,128]{2,1,0:T(8,128)S(1)}, u32[]{:S(2)}, u32[]{:S(2)}) collective-permute-start(f32[10,128,128]{2,1,0:T(8,128)} %get-tuple-element.98), channel_id=1, source_target_pairs={{0,4},{1,5},{2,6},{3,7},{4,0},{5,1},{6,2},{7,3},{8,12},{9,13},{10,... | collective-permute-start | bytes 1966088 | tf_op jit(solution)/shard_map/ppermute | solution.py:628
  125.0 12.8 %shard_map.154 = (f32[18,128,128]{2,1,0:T(8,128)}, f32[18,128,128]{2,1,0:T(8,128)}, f32[18,128,128]{2,1,0:T(8,128)}, f32[18,128,128]{2,1,0:T(8,128)}) custom-call(s32[86]{0:T(128)} %concatenate.3.s_ref, f32[768,768]{1,0:T(8,128)} %get-tuple-element.100.own_ref, f32[768,768]{1,0:T(8,128)} %get-tuple-element.101.cross_ref, f32[1024,1024]{1,0:T(8,128)} %bitcast.20), custom_call_target="tpu_custom_call" | custom-call | bytes 13631488 | tf_op jit(solution)/shard_map/pallas_call | solution.py:43
  146.4 14.2 %shard_map.157 = (f32[23,128,128]{2,1,0:T(8,128)}, f32[23,128,128]{2,1,0:T(8,128)}, f32[25,128,128]{2,1,0:T(8,128)}, f32[25,128,128]{2,1,0:T(8,128)}) custom-call(s32[86]{0:T(128)} %concatenate.3.s_ref, f32[768,768]{1,0:T(8,128)} %get-tuple-element.100.own_ref, f32[768,768]{1,0:T(8,128)} %get-tuple-element.101.cross_ref, f32[1024,1024]{1,0:T(8,128)} %bitcast.21), custom_call_target="tpu_custom_call" | custom-call | bytes 15204352 | tf_op jit(solution)/shard_map/pallas_call | solution.py:43
  162.3 7.5 %collective-permute-done.8.x1 = f32[18,128,128]{2,1,0:T(8,128)S(1)} collective-permute-done((f32[18,128,128]{2,1,0:T(8,128)}, f32[18,128,128]{2,1,0:T(8,128)S(1)}, u32[]{:S(2)}, u32[]{:S(2)}) %collective-permute-start.8) | collective-permute-done | bytes 1179680 | tf_op jit(solution)/shard_map/ppermute | solution.py:628
  177.5 9.0 %collective-permute-done.6.refs_1_ = f32[10,128,128]{2,1,0:T(8,128)} collective-permute-done((f32[10,128,128]{2,1,0:T(8,128)}, f32[10,128,128]{2,1,0:T(8,128)}, u32[]{:S(2)}, u32[]{:S(2)}) %collective-permute-start.6) | collective-permute-done | bytes 655392 | tf_op jit(solution)/shard_map/ppermute | solution.py:628
  187.6 29.3 %shard_map.155 = (f32[192,768]{1,0:T(8,128)}, bf16[768,768]{1,0:T(8,128)(2,1)}, bf16[768,768]{1,0:T(8,128)(2,1)}, bf16[768,128]{1,0:T(8,128)(2,1)}, bf16[768,128]{1,0:T(8,128)(2,1)}) custom-call(s32[86]{0:T(128)} %concatenate.3.s_ref, f32[10,128,128]{2,1,0:T(8,128)} %add.88.refs_0_, f32[10,128,128]{2,1,0:T(8,128)} %collective-permute-done.6.refs_1_, ...), custom_call_target="tpu_custom_call" | custom-call | flops 20000000000 | bytes 8847360 | tf_op jit(solution)/shard_map/pallas_call | solution.py:43
  216.9 12.6 %collective-permute-done.9.x2 = f32[9,128,128]{2,1,0:T(8,128)S(1)} collective-permute-done((f32[9,128,128]{2,1,0:T(8,128)}, f32[9,128,128]{2,1,0:T(8,128)S(1)}, u32[]{:S(2)}, u32[]{:S(2)}) %collective-permute-start.9) | collective-permute-done | bytes 589856 | tf_op jit(solution)/shard_map/ppermute | solution.py:628
  230.3 9.1 %shard_map.156.p_ref = f32[384,768]{1,0:T(8,128)} custom-call(s32[86]{0:T(128)} %concatenate.3.s_ref, f32[384,2304]{1,0:T(8,128)} %bitcast.27, f32[18,128,128]{2,1,0:T(8,128)} %get-tuple-element.107.xk, f32[18,128,128]{2,1,0:T(8,128)} %copy-done.7, f32[9,128,128]{2,1,0:T(8,128)} %copy-done.18, f32[18,128,128]{2,1,0:T(8,128)} %get-tuple-element.109.zk, ...), custom_call_target="tpu_custom_call" | custom-call | flops 2000000000 | bytes 16121856 | tf_op jit(solution)/shard_map/pallas_call | solution.py:43
  249.1 21.9 %collective-permute-done.17.pz = f32[384,768]{1,0:T(8,128)S(1)} collective-permute-done((f32[384,768]{1,0:T(8,128)}, f32[384,768]{1,0:T(8,128)S(1)}, u32[]{:S(2)}, u32[]{:S(2)}) %collective-permute-start.17) | collective-permute-done | bytes 1179680 | tf_op jit(solution)/shard_map/ppermute | solution.py:628
  276.6 16.8 %collective-permute-done.13.x2 = f32[16,128,128]{2,1,0:T(8,128)S(1)} collective-permute-done((f32[16,128,128]{2,1,0:T(8,128)S(1)}, f32[16,128,128]{2,1,0:T(8,128)S(1)}, u32[]{:S(2)}, u32[]{:S(2)}) %collective-permute-start.13) | collective-permute-done | bytes 1048608 | tf_op jit(solution)/shard_map/ppermute | solution.py:628
  295.5 8.6 %shard_map.158.b_ref = f32[384,1536]{1,0:T(8,128)} custom-call(s32[86]{0:T(128)} %concatenate.3.s_ref, f32[384,2304]{1,0:T(8,128)} %bitcast.28, f32[384,768]{1,0:T(8,128)} %shard_map.156.p_ref, f32[23,128,128]{2,1,0:T(8,128)} %get-tuple-element.115.xk, f32[23,128,128]{2,1,0:T(8,128)} %collective-permute-done.12.x1, f32[16,128,128]{2,1,0:T(8,128)} %copy-done.12, ...), custom_call_target="tpu_custom_call" | custom-call | flops 1000000000 | bytes 15532032 | tf_op jit(solution)/shard_map/pallas_call | solution.py:43
  304.1 6.9 %shard_map.159.b_ref = f32[384,1536]{1,0:T(8,128)} custom-call(s32[86]{0:T(128)} %concatenate.3.s_ref, f32[384,1536]{1,0:T(8,128)} %shard_map.158.b_ref, f32[384,768]{1,0:T(8,128)} %shard_map.156.p_ref, f32[384,768]{1,0:T(8,128)} %copy-done.8, f32[384,768]{1,0:T(8,128)} %copy-done.9), custom_call_target="tpu_custom_call" | custom-call | flops 2000000000 | bytes 8257536 | tf_op jit(solution)/shard_map/pallas_call | solution.py:43
  312.6 4.5 %shard_map.160 = f32[384,1536]{1,0:T(8,128)} custom-call(s32[86]{0:T(128)} %concatenate.3.s_ref, f32[384,1536]{1,0:T(8,128)} %shard_map.159.b_ref, f32[384,768]{1,0:T(8,128)} %shard_map.156.p_ref, f32[192,768]{1,0:T(8,128)} %copy-done.16, f32[192,768]{1,0:T(8,128)} %copy-done.17), custom_call_target="tpu_custom_call", output_to_operand_aliasing={{}: (1, {})} | custom-call | flops 1000000000 | bytes 7077888 | tf_op jit(solution)/shard_map/pallas_call | solution.py:43
  (97 shorter events, 58.9 us)
Async XLA Ops:
  6.1 20.4 %collective-permute-start = (f32[11,128,128]{2,1,0:T(8,128)}, f32[11,128,128]{2,1,0:T(8,128)S(1)}, u32[]{:S(2)}, u32[]{:S(2)}) collective-permute-start(f32[11,128,128]{2,1,0:T(8,128)} %shard_map.146.refs_0_), channel_id=1, source_target_pairs={{0,64},{8,72},{16,80},{24,88},{32,96},{40,104},{48,112},{56,120},{... | collective-permute-start | bytes 2162696 | tf_op jit(solution)/shard_map/ppermute | solution.py:628
  26.6 19.5 %collective-permute-start.1 = (f32[10,128,128]{2,1,0:T(8,128)}, f32[10,128,128]{2,1,0:T(8,128)S(1)}, u32[]{:S(2)}, u32[]{:S(2)}) collective-permute-start(f32[10,128,128]{2,1,0:T(8,128)} %get-tuple-element.71.refs_0_), channel_id=1, source_target_pairs={{0,64},{8,72},{16,80},{24,88},{32,96},{40,104},{48,112},{56,120},{... | collective-permute-start | bytes 1966088 | tf_op jit(solution)/shard_map/ppermute | solution.py:628
  46.1 25.5 %collective-permute-start.2 = (f32[16,128,128]{2,1,0:T(8,128)S(1)}, f32[16,128,128]{2,1,0:T(8,128)S(1)}, u32[]{:S(2)}, u32[]{:S(2)}) collective-permute-start(f32[16,128,128]{2,1,0:T(8,128)S(1)} %copy-done.19), channel_id=1, source_target_pairs={{0,64},{8,72},{16,80},{24,88},{32,96},{40,104},{48,112},{56,120},{... | collective-permute-start | bytes 3145736 | tf_op jit(solution)/shard_map/ppermute | solution.py:628
  83.8 25.3 %collective-permute-start.3 = (f32[768,384]{1,0:T(8,128)}, f32[768,384]{1,0:T(8,128)S(1)}, u32[]{:S(2)}, u32[]{:S(2)}) collective-permute-start(f32[768,384]{1,0:T(8,128)} %get-tuple-element.93), channel_id=1, source_target_pairs={{0,64},{8,72},{16,80},{24,88},{32,96},{40,104},{48,112},{56,120},{... | collective-permute-start | bytes 3538952 | tf_op jit(solution)/shard_map/ppermute | solution.py:628
  118.4 20.3 %collective-permute-start.5 = (f32[11,128,128]{2,1,0:T(8,128)}, f32[11,128,128]{2,1,0:T(8,128)S(1)}, u32[]{:S(2)}, u32[]{:S(2)}) collective-permute-start(f32[11,128,128]{2,1,0:T(8,128)} %get-tuple-element.99), channel_id=1, source_target_pairs={{0,64},{8,72},{16,80},{24,88},{32,96},{40,104},{48,112},{56,120},{... | collective-permute-start | bytes 2162696 | tf_op jit(solution)/shard_map/ppermute | solution.py:628
  119.7 18.1 %collective-permute-start.4 = (f32[10,128,128]{2,1,0:T(8,128)}, f32[10,128,128]{2,1,0:T(8,128)S(1)}, u32[]{:S(2)}, u32[]{:S(2)}) collective-permute-start(f32[10,128,128]{2,1,0:T(8,128)} %get-tuple-element.98), channel_id=1, source_target_pairs={{0,4},{1,5},{2,6},{3,7},{4,0},{5,1},{6,2},{7,3},{8,12},{9,13},{10,... | collective-permute-start | bytes 1966088 | tf_op jit(solution)/shard_map/ppermute | solution.py:628
  139.2 21.4 %copy-start.13 = (f32[11,128,128]{2,1,0:T(8,128)}, f32[11,128,128]{2,1,0:T(8,128)S(1)}, u32[]{:S(2)}) copy-start(f32[11,128,128]{2,1,0:T(8,128)S(1)} %add.89.refs_2_) | copy-start | bytes 2162692
  139.2 33.9 %copy-start.5 = (f32[18,128,128]{2,1,0:T(8,128)S(1)}, f32[18,128,128]{2,1,0:T(8,128)}, u32[]{:S(2)}) copy-start(f32[18,128,128]{2,1,0:T(8,128)} %get-tuple-element.107.xk) | copy-start | bytes 3538948
  139.2 30.6 %collective-permute-start.8 = (f32[18,128,128]{2,1,0:T(8,128)}, f32[18,128,128]{2,1,0:T(8,128)S(1)}, u32[]{:S(2)}, u32[]{:S(2)}) collective-permute-start(f32[18,128,128]{2,1,0:T(8,128)} %get-tuple-element.108), channel_id=1, source_target_pairs={{0,4},{1,5},{2,6},{3,7},{4,0},{5,1},{6,2},{7,3},{8,12},{9,13},{10,... | collective-permute-start | bytes 3538952 | tf_op jit(solution)/shard_map/ppermute | solution.py:628
  141.8 33.3 %collective-permute-start.10 = (f32[18,128,128]{2,1,0:T(8,128)}, f32[18,128,128]{2,1,0:T(8,128)}, u32[]{:S(2)}, u32[]{:S(2)}) collective-permute-start(f32[18,128,128]{2,1,0:T(8,128)} %get-tuple-element.110), channel_id=1, source_target_pairs={{0,64},{8,72},{16,80},{24,88},{32,96},{40,104},{48,112},{56,120},{... | collective-permute-start | bytes 3538952 | tf_op jit(solution)/shard_map/ppermute | solution.py:628
  143.5 44.0 %collective-permute-start.7 = (f32[11,128,128]{2,1,0:T(8,128)S(1)}, f32[11,128,128]{2,1,0:T(8,128)}, u32[]{:S(2)}, u32[]{:S(2)}) collective-permute-start(f32[11,128,128]{2,1,0:T(8,128)S(1)} %add.89.refs_2_), channel_id=1, source_target_pairs={{0,4},{1,5},{2,6},{3,7},{4,0},{5,1},{6,2},{7,3},{8,12},{9,13},{10,... | collective-permute-start | bytes 2162696 | tf_op jit(solution)/shard_map/ppermute | solution.py:628
  145.1 41.5 %collective-permute-start.6 = (f32[10,128,128]{2,1,0:T(8,128)}, f32[10,128,128]{2,1,0:T(8,128)}, u32[]{:S(2)}, u32[]{:S(2)}) collective-permute-start(f32[10,128,128]{2,1,0:T(8,128)} %add.88.refs_0_), channel_id=1, source_target_pairs={{0,64},{8,72},{16,80},{24,88},{32,96},{40,104},{48,112},{56,120},{... | collective-permute-start | bytes 1966088 | tf_op jit(solution)/shard_map/ppermute | solution.py:628
  160.6 15.8 %copy-start.6 = (f32[18,128,128]{2,1,0:T(8,128)S(1)}, f32[18,128,128]{2,1,0:T(8,128)}, u32[]{:S(2)}) copy-start(f32[18,128,128]{2,1,0:T(8,128)} %get-tuple-element.109.zk) | copy-start | bytes 3538948
  160.6 84.6 %collective-permute-start.12 = (f32[23,128,128]{2,1,0:T(8,128)}, f32[23,128,128]{2,1,0:T(8,128)}, u32[]{:S(2)}, u32[]{:S(2)}) collective-permute-start(f32[23,128,128]{2,1,0:T(8,128)} %get-tuple-element.116), channel_id=1, source_target_pairs={{0,4},{1,5},{2,6},{3,7},{4,0},{5,1},{6,2},{7,3},{8,12},{9,13},{10,... | collective-permute-start | bytes 4521992 | tf_op jit(solution)/shard_map/ppermute | solution.py:628
  170.9 72.2 %collective-permute-start.14 = (f32[25,128,128]{2,1,0:T(8,128)}, f32[25,128,128]{2,1,0:T(8,128)S(1)}, u32[]{:S(2)}, u32[]{:S(2)}) collective-permute-start(f32[25,128,128]{2,1,0:T(8,128)} %get-tuple-element.118), channel_id=1, source_target_pairs={{0,64},{8,72},{16,80},{24,88},{32,96},{40,104},{48,112},{56,120},{... | collective-permute-start | bytes 4915208 | tf_op jit(solution)/shard_map/ppermute | solution.py:628
  175.1 54.4 %collective-permute-start.9 = (f32[9,128,128]{2,1,0:T(8,128)}, f32[9,128,128]{2,1,0:T(8,128)S(1)}, u32[]{:S(2)}, u32[]{:S(2)}) collective-permute-start(f32[9,128,128]{2,1,0:T(8,128)} %slice_add_fusion.3), channel_id=1, source_target_pairs={{0,64},{8,72},{16,80},{24,88},{32,96},{40,104},{48,112},{56,120},{... | collective-permute-start | bytes 1769480 | tf_op jit(solution)/shard_map/ppermute | solution.py:628
  186.5 42.9 %collective-permute-start.11 = (f32[9,128,128]{2,1,0:T(8,128)S(1)}, f32[9,128,128]{2,1,0:T(8,128)}, u32[]{:S(2)}, u32[]{:S(2)}) collective-permute-start(f32[9,128,128]{2,1,0:T(8,128)S(1)} %slice_add_fusion.2), channel_id=1, source_target_pairs={{0,4},{1,5},{2,6},{3,7},{4,0},{5,1},{6,2},{7,3},{8,12},{9,13},{10,... | collective-permute-start | bytes 1769480 | tf_op jit(solution)/shard_map/ppermute | solution.py:628
  230.3 12.9 %copy-start.2 = (f32[25,128,128]{2,1,0:T(8,128)S(1)}, f32[25,128,128]{2,1,0:T(8,128)}, u32[]{:S(2)}) copy-start(f32[25,128,128]{2,1,0:T(8,128)} %get-tuple-element.117.zk) | copy-start | bytes 4915204
  239.4 34.2 %collective-permute-start.16 = (f32[384,768]{1,0:T(8,128)}, f32[384,768]{1,0:T(8,128)S(1)}, u32[]{:S(2)}, u32[]{:S(2)}) collective-permute-start(f32[384,768]{1,0:T(8,128)} %shard_map.156.p_ref), channel_id=1, source_target_pairs={{0,4},{1,5},{2,6},{3,7},{4,0},{5,1},{6,2},{7,3},{8,12},{9,13},{10,... | collective-permute-start | bytes 3538952 | tf_op jit(solution)/shard_map/ppermute | solution.py:628
  240.4 30.6 %collective-permute-start.17 = (f32[384,768]{1,0:T(8,128)}, f32[384,768]{1,0:T(8,128)S(1)}, u32[]{:S(2)}, u32[]{:S(2)}) collective-permute-start(f32[384,768]{1,0:T(8,128)} %shard_map.156.p_ref), channel_id=1, source_target_pairs={{0,64},{8,72},{16,80},{24,88},{32,96},{40,104},{48,112},{56,120},{... | collective-permute-start | bytes 3538952 | tf_op jit(solution)/shard_map/ppermute | solution.py:628
  244.3 49.5 %collective-permute-start.15 = (f32[17,128,128]{2,1,0:T(8,128)S(1)}, f32[17,128,128]{2,1,0:T(8,128)S(1)}, u32[]{:S(2)}, u32[]{:S(2)}) collective-permute-start(f32[17,128,128]{2,1,0:T(8,128)S(1)} %slice_add_fusion), channel_id=1, source_target_pairs={{0,4},{1,5},{2,6},{3,7},{4,0},{5,1},{6,2},{7,3},{8,12},{9,13},{10,... | collective-permute-start | bytes 3342344 | tf_op jit(solution)/shard_map/ppermute | solution.py:628
  246.6 46.9 %collective-permute-start.13 = (f32[16,128,128]{2,1,0:T(8,128)S(1)}, f32[16,128,128]{2,1,0:T(8,128)S(1)}, u32[]{:S(2)}, u32[]{:S(2)}) collective-permute-start(f32[16,128,128]{2,1,0:T(8,128)S(1)} %slice_add_fusion.1), channel_id=1, source_target_pairs={{0,64},{8,72},{16,80},{24,88},{32,96},{40,104},{48,112},{56,120},{... | collective-permute-start | bytes 3145736 | tf_op jit(solution)/shard_map/ppermute | solution.py:628
  271.0 39.9 %collective-permute-start.18 = (f32[192,768]{1,0:T(8,128)S(1)}, f32[192,768]{1,0:T(8,128)S(1)}, u32[]{:S(2)}, u32[]{:S(2)}) collective-permute-start(f32[192,768]{1,0:T(8,128)S(1)} %slice.44), channel_id=1, source_target_pairs={{0,4},{1,5},{2,6},{3,7},{4,0},{5,1},{6,2},{7,3},{8,12},{9,13},{10,... | collective-permute-start | bytes 1769480 | tf_op jit(solution)/shard_map/ppermute | solution.py:628
  275.5 35.4 %collective-permute-start.19 = (f32[192,768]{1,0:T(8,128)}, f32[192,768]{1,0:T(8,128)S(1)}, u32[]{:S(2)}, u32[]{:S(2)}) collective-permute-start(f32[192,768]{1,0:T(8,128)} %slice.45), channel_id=1, source_target_pairs={{0,64},{8,72},{16,80},{24,88},{32,96},{40,104},{48,112},{56,120},{... | collective-permute-start | bytes 1769480 | tf_op jit(solution)/shard_map/ppermute | solution.py:628
  (19 other events, 57.4 us)

commit v6 on v5

--- a/solution.py
+++ b/solution.py
@@ -359,6 +359,17 @@
     send_ref[...] = p_ref[:, pl.ds(pl.multiple_of((1 - side) * 384, T), 384)]
 
 
+def mixed(side, inv2, r, c):
+    i = inv2[r]
+    j = inv2[c]
+    used = (i >= 0) & (j >= 0)
+    i = jnp.maximum(i, 0)
+    j = jnp.maximum(j, 0)
+    mi = (i // 6) == side
+    mj = (j // 6) == side
+    return i % 6, j % 6, used & mi & jnp.logical_not(mj), used & jnp.logical_not(mi) & mj
+
+
 def own_kernel(
     s_ref, p_ref, t0_ref, t1_ref, c_ref, pv_ref, own_ref, piv_ref, ph, plo, wide, inv, inv2
 ):
@@ -379,6 +390,15 @@
         def col(c, _):
             at = row * (row + 1) // 2 + c
             source_tile(side, inv, inv2, own_ref, None, c_ref, piv_ref, at, row, c)
+            i, j, ahead, behind = mixed(side, inv2, row, c)
+
+            @pl.when(ahead & (side == 0))
+            def _():
+                piv_ref[at] += t1_ref[tl(i), tl(j)]
+
+            @pl.when(behind & (side == 0))
+            def _():
+                piv_ref[at] += t1_ref[tl(j), tl(i)].T
 
             @pl.when((row >= base) & (row < base + 2))
             def _():
@@ -431,7 +451,34 @@
         out_ref[at] += c_ref[tl(ci), tl(cj)]
 
 
-def cross_kernel(s_ref, p_ref, q_ref, t1_ref, piv_ref, cross_ref, a_ref, b_ref, inv2):
+def cross_pivot_kernel(s_ref, p_ref, q_ref, piv_ref, a_ref, b_ref, inv2):
+    side = s_ref[SLO]
+    invert(s_ref, MAP2, NU, inv2, 18)
+    a_ref[...] = piv_ref[0:10]
+    b_ref[...] = piv_ref[10:21]
+
+    def emit(out_ref, first, row):
+        def col(c, _):
+            at = row * (row + 1) // 2 + c - first
+            i, j, ahead, behind = mixed(side, inv2, row, c)
+
+            @pl.when(ahead)
+            def _():
+                out_ref[at] -= dot3(split(p_ref[tl(i), :]), split(q_ref[tl(j), :]), NT)
+
+            @pl.when(behind)
+            def _():
+                out_ref[at] -= dot3(split(q_ref[tl(i), :]), split(p_ref[tl(j), :]), NT)
+
+            return 0
+
+        lax.fori_loop(0, row + 1, col, 0)
+
+    lax.fori_loop(0, 4, lambda r, _: (emit(a_ref, 0, r), 0)[1], 0)
+    lax.fori_loop(4, 6, lambda r, _: (emit(b_ref, 10, r), 0)[1], 0)
+
+
+def cross_kernel(s_ref, p_ref, q_ref, t1_ref, cross_ref):
     side = s_ref[SLO]
     pc = split(p_ref[...])
     qh, ql = split(q_ref[...])
@@ -439,35 +486,6 @@
         s = slice(n * 256, n * 256 + 256)
         base = jnp.where(side == 0, t1_ref[:, s], 0.0)
         cross_ref[:, s] = base - dot3(pc, (qh[s, :], ql[s, :]), NT)
-    invert(s_ref, MAP2, NU, inv2, 18)
-    a_ref[...] = piv_ref[0:10]
-    b_ref[...] = piv_ref[10:21]
-
-    def emit(out_ref, first, row):
-        def col(c, _):
-            at = row * (row + 1) // 2 + c - first
-            i = inv2[row]
-            j = inv2[c]
-            used = (i >= 0) & (j >= 0)
-            i = jnp.maximum(i, 0)
-            j = jnp.maximum(j, 0)
-            mi = (i // 6) == side
-            mj = (j // 6) == side
-
-            @pl.when(used & mi & jnp.logical_not(mj))
-            def _():
-                out_ref[at] += cross_ref[tl(i % 6), tl(j % 6)]
-
-            @pl.when(used & jnp.logical_not(mi) & mj)
-            def _():
-                out_ref[at] += cross_ref[tl(j % 6), tl(i % 6)].T
-
-            return 0
-
-        lax.fori_loop(0, row + 1, col, 0)
-
-    lax.fori_loop(0, 4, lambda r, _: (emit(a_ref, 0, r), 0)[1], 0)
-    lax.fori_loop(4, 6, lambda r, _: (emit(b_ref, 10, r), 0)[1], 0)
 
 
 def rows_two_kernel(first, width, s_ref, own_ref, cross_ref, c_ref, *refs):
@@ -733,21 +751,29 @@
         [pltpu.VMEM((n, n), bf16)] * 2 + [pltpu.VMEM((2 * T, n), f32), smem, smem],
         flops=4_000_000_000,
     )
-    cross, pa, pb = call(
-        cross_kernel,
-        [scalars, panel_one, got, rows1, piv],
-        [pl.BlockSpec((n, n // 2), lambda i, s: (0, s[SLO])), None, block(n, n, 2), None],
-        [shape(n, n), shape(10, T, T), shape(11, T, T)],
+    half_cols = pl.BlockSpec((n, n // 2), lambda i, s: (0, s[SLO]))
+    pa, pb = call(
+        cross_pivot_kernel,
+        [scalars, panel_one, got, piv],
+        [half_cols, None, None],
+        [shape(10, T, T), shape(11, T, T)],
         [smem],
-        flops=2_000_000_000,
+        flops=500_000_000,
     )
     pa1 = across("hi", pa)
     pb1 = across("lo", pb)
-    pa, pb, cross = lax.optimization_barrier((pa, pb, cross))
+    pa, pb, got = lax.optimization_barrier((pa, pb, got))
+    (cross,) = call(
+        cross_kernel,
+        [scalars, panel_one, got, rows1],
+        [half_cols, None, block(n, n, 2)],
+        [shape(n, n)],
+        [],
+        flops=2_000_000_000,
+    )
     cxs, cxk, czs, czk = rows_two(scalars, own, cross, c, 0, NP)
     pa = pa + pa1
     pb = pb + pb1
-    pa, pb, cxs, czs = lax.optimization_barrier((pa, pb, cxs, czs))
     pa2 = across("lo", pa)
     pb2 = across("hi", pb)
     cx1 = across("hi", cxs)

time: 321 us -> 344 us (1.072)
  waiting for transfers between devices: 87.5 us -> 104 us
  Pallas kernels: 164 us -> 168 us
    ppermute x20, waiting for transfers between devices: 87.5 us -> 104 us  [across(): return lax.ppermute(values, axis, [(i, i ^ size // 2) for i in range(size)])]
    pallas_call x15 -> x16, Pallas kernels: 164 us -> 168 us  [call(): pl.pallas_call(kernel, grid_spec=pltpu.PrefetchScalarGridSpec(num_scalar_...]
    unnamed x46 -> x44, local copies, waits for them, and re-layouts: 9.65 us -> 9.23 us
  transfers between devices with their start and end apart: 20 -> 20, of which waited for: 9 -> 8; matrix products, arithmetic and copies ran while one was open for 4% -> 4% of each run, Pallas kernels for 43% -> 37%
where the time goes in v6:
time: 344 us; the launch traced here: 338 us
  Pallas kernels  168 us (49%)
  waiting for transfers between devices  104 us (30%)
  starting transfers between devices  39.2 us (11%)
  local copies, waits for them, and re-layouts  19.1 us (6%)
  other arithmetic  6.68 us (2%)
    pallas_call x16, Pallas kernels, call(): pl.pallas_call(kernel, grid_spec=pltpu.PrefetchScalarGridSpec(num_scalar_...  168 us
    ppermute x20, waiting for transfers between devices, across(): return lax.ppermute(values, axis, [(i, i ^ size // 2) for i in range(size)])  104 us
    ppermute x20, starting transfers between devices, across(): return lax.ppermute(values, axis, [(i, i ^ size // 2) for i in range(size)])  39.2 us
    unnamed x44, local copies, waits for them, and re-layouts  9.23 us
  transfers between devices with their start and end apart: 20, of which 8 were waited for; matrix products, arithmetic and copies ran while one was open for 4% of the time, Pallas kernels for 37%

profile of v6, /device:TPU:0, one launch (start us, length us, event | category | flops | bytes accessed | tf_op | source)
XLA Modules:
  0.0 338.4 jit_solution(17402690082672696223)
XLA Ops:
  2.1 4.1 %shard_map.146.refs_0_ = f32[11,128,128]{2,1,0:T(8,128)} custom-call(s32[8]{0:T(128)} %dynamic-slice_reduce_fusion.2.s_ref, f32[1024,1024]{1,0:T(8,128)} %bitcast.16, f32[384,768]{1,0:T(8,128)} %bitcast.31), custom_call_target="tpu_custom_call" | custom-call | bytes 6094848 | tf_op jit(solution)/shard_map/pallas_call | solution.py:43
  6.2 4.0 %collective-permute-start = (f32[11,128,128]{2,1,0:T(8,128)}, f32[11,128,128]{2,1,0:T(8,128)S(1)}, u32[]{:S(2)}, u32[]{:S(2)}) collective-permute-start(f32[11,128,128]{2,1,0:T(8,128)} %shard_map.146.refs_0_), channel_id=1, source_target_pairs={{0,64},{8,72},{16,80},{24,88},{32,96},{40,104},{48,112},{56,120},{... | collective-permute-start | bytes 2162696 | tf_op jit(solution)/shard_map/ppermute | solution.py:646
  14.0 5.6 %shard_map.147 = (f32[10,128,128]{2,1,0:T(8,128)}, f32[16,128,128]{2,1,0:T(8,128)}) custom-call(s32[8]{0:T(128)} %dynamic-slice_reduce_fusion.2.s_ref, f32[1024,1024]{1,0:T(8,128)} %bitcast.17, f32[384,768]{1,0:T(8,128)} %bitcast.32), custom_call_target="tpu_custom_call" | custom-call | bytes 7077888 | tf_op jit(solution)/shard_map/pallas_call | solution.py:43
  23.2 3.4 %collective-permute-done.refs_1_ = f32[11,128,128]{2,1,0:T(8,128)S(1)} collective-permute-done((f32[11,128,128]{2,1,0:T(8,128)}, f32[11,128,128]{2,1,0:T(8,128)S(1)}, u32[]{:S(2)}, u32[]{:S(2)}) %collective-permute-start) | collective-permute-done | bytes 720928 | tf_op jit(solution)/shard_map/ppermute | solution.py:646
  29.9 10.3 %shard_map.148 = (f32[768,256]{1,0:T(8,128)}, bf16[768,256]{1,0:T(8,128)(2,1)}, bf16[768,256]{1,0:T(8,128)(2,1)}, bf16[256,128]{1,0:T(8,128)(2,1)}, bf16[256,128]{1,0:T(8,128)(2,1)}) custom-call(s32[86]{0:T(128)} %concatenate.3.s_ref, f32[11,128,128]{2,1,0:T(8,128)} %shard_map.146.refs_0_, f32[11,128,128]{2,1,0:T(8,128)} %copy-done.20), custom_call_target="tpu_custom_call" | custom-call | flops 20000000000 | bytes 4063232 | tf_op jit(solution)/shard_map/pallas_call | solution.py:43
  40.1 6.0 %shard_map.150.x_ref = f32[768,768]{1,0:T(8,128)} custom-call(s32[86]{0:T(128)} %concatenate.3.s_ref, f32[768,2304]{1,0:T(8,128)} %bitcast.22, f32[1024,1024]{1,0:T(8,128)} %bitcast.18), custom_call_target="tpu_custom_call" | custom-call | bytes 13631488 | tf_op jit(solution)/shard_map/pallas_call | solution.py:43
  47.3 21.7 %shard_map.149 = (f32[384,768]{1,0:T(8,128)}, bf16[768,768]{1,0:T(8,128)(2,1)}, bf16[768,768]{1,0:T(8,128)(2,1)}, bf16[768,128]{1,0:T(8,128)(2,1)}, bf16[768,128]{1,0:T(8,128)(2,1)}) custom-call(s32[86]{0:T(128)} %concatenate.3.s_ref, f32[10,128,128]{2,1,0:T(8,128)} %get-tuple-element.66.refs_0_, f32[10,128,128]{2,1,0:T(8,128)} %copy-done.21, ...), custom_call_target="tpu_custom_call" | custom-call | flops 20000000000 | bytes 10616832 | tf_op jit(solution)/shard_map/pallas_call | solution.py:43
  72.6 11.2 %shard_map.151 = (f32[768,768]{1,0:T(8,128)}, f32[768,384]{1,0:T(8,128)}) custom-call(s32[86]{0:T(128)} %concatenate.3.s_ref, f32[768,768]{1,0:T(8,128)} %shard_map.150.x_ref, f32[16,128,128]{2,1,0:T(8,128)} %copy-done.19, bf16[768,768]{1,0:T(8,128)(2,1)} %get-tuple-element.83.lh, bf16[768,768]{1,0:T(8,128)(2,1)} %get-tuple-element.84.ll, ...), custom_call_target="tpu_custom_call" | custom-call | flops 3000000000 | bytes 12451840 | tf_op jit(solution)/shard_map/pallas_call | solution.py:43
  84.9 12.0 %shard_map.152 = (f32[768,768]{1,0:T(8,128)}, f32[21,128,128]{2,1,0:T(8,128)}) custom-call(s32[86]{0:T(128)} %concatenate.3.s_ref, f32[768,768]{1,0:T(8,128)} %get-tuple-element.87.p_ref, f32[768,2304]{1,0:T(8,128)} %bitcast.23, f32[768,2304]{1,0:T(8,128)} %bitcast.24, f32[1024,1024]{1,0:T(8,128)} %bitcast.19, f32[192,768]{1,0:T(8,128)} %bitcast.33), custom_call_target="tpu_custom_call" | custom-call | flops 4000000000 | bytes 25034752 | tf_op jit(solution)/shard_map/pallas_call | solution.py:43
  96.9 12.2 %collective-permute-done.3.q_ref = f32[768,384]{1,0:T(8,128)S(1)} collective-permute-done((f32[768,384]{1,0:T(8,128)}, f32[768,384]{1,0:T(8,128)S(1)}, u32[]{:S(2)}, u32[]{:S(2)}) %collective-permute-start.3) | collective-permute-done | bytes 1179680 | tf_op jit(solution)/shard_map/ppermute | solution.py:646
  110.1 5.6 %shard_map.153 = (f32[10,128,128]{2,1,0:T(8,128)}, f32[11,128,128]{2,1,0:T(8,128)}) custom-call(s32[86]{0:T(128)} %concatenate.3.s_ref, f32[768,768]{1,0:T(8,128)} %get-tuple-element.87.p_ref, f32[768,384]{1,0:T(8,128)} %copy-done.2, f32[21,128,128]{2,1,0:T(8,128)} %get-tuple-element.89.piv_ref), custom_call_target="tpu_custom_call" | custom-call | flops 500000000 | bytes 6291456 | tf_op jit(solution)/shard_map/pallas_call | solution.py:43
  115.8 6.5 %shard_map.155.cross_ref = f32[768,768]{1,0:T(8,128)} custom-call(s32[86]{0:T(128)} %concatenate.3.s_ref, f32[768,768]{1,0:T(8,128)} %get-tuple-element.87.p_ref, f32[768,384]{1,0:T(8,128)} %copy-done.2, f32[768,2304]{1,0:T(8,128)} %bitcast.25), custom_call_target="tpu_custom_call" | custom-call | flops 2000000000 | bytes 12976128 | tf_op jit(solution)/shard_map/pallas_call | solution.py:43
  122.3 12.8 %shard_map.156 = (f32[18,128,128]{2,1,0:T(8,128)}, f32[18,128,128]{2,1,0:T(8,128)}, f32[18,128,128]{2,1,0:T(8,128)}, f32[18,128,128]{2,1,0:T(8,128)}) custom-call(s32[86]{0:T(128)} %concatenate.3.s_ref, f32[768,768]{1,0:T(8,128)} %get-tuple-element.95.own_ref, f32[768,768]{1,0:T(8,128)} %shard_map.155.cross_ref, f32[1024,1024]{1,0:T(8,128)} %bitcast.20), custom_call_target="tpu_custom_call" | custom-call | bytes 13631488 | tf_op jit(solution)/shard_map/pallas_call | solution.py:43
  135.1 5.3 %collective-permute-start.8 = (f32[18,128,128]{2,1,0:T(8,128)}, f32[18,128,128]{2,1,0:T(8,128)S(1)}, u32[]{:S(2)}, u32[]{:S(2)}) collective-permute-start(f32[18,128,128]{2,1,0:T(8,128)} %get-tuple-element.98), channel_id=1, source_target_pairs={{0,4},{1,5},{2,6},{3,7},{4,0},{5,1},{6,2},{7,3},{8,12},{9,13},{10,... | collective-permute-start | bytes 3538952 | tf_op jit(solution)/shard_map/ppermute | solution.py:646
  143.9 38.2 %collective-permute-done.6 = f32[11,128,128]{2,1,0:T(8,128)S(1)} collective-permute-done((f32[11,128,128]{2,1,0:T(8,128)S(1)}, f32[11,128,128]{2,1,0:T(8,128)S(1)}, u32[]{:S(2)}, u32[]{:S(2)}) %collective-permute-start.6) | collective-permute-done | bytes 720928 | tf_op jit(solution)/shard_map/ppermute | solution.py:646
  186.4 14.2 %shard_map.158 = (f32[23,128,128]{2,1,0:T(8,128)}, f32[23,128,128]{2,1,0:T(8,128)}, f32[25,128,128]{2,1,0:T(8,128)}, f32[25,128,128]{2,1,0:T(8,128)}) custom-call(s32[86]{0:T(128)} %concatenate.3.s_ref, f32[768,768]{1,0:T(8,128)} %get-tuple-element.95.own_ref, f32[768,768]{1,0:T(8,128)} %shard_map.155.cross_ref, f32[1024,1024]{1,0:T(8,128)} %bitcast.21), custom_call_target="tpu_custom_call" | custom-call | bytes 15204352 | tf_op jit(solution)/shard_map/pallas_call | solution.py:43
  211.9 29.3 %shard_map.154 = (f32[192,768]{1,0:T(8,128)}, bf16[768,768]{1,0:T(8,128)(2,1)}, bf16[768,768]{1,0:T(8,128)(2,1)}, bf16[768,128]{1,0:T(8,128)(2,1)}, bf16[768,128]{1,0:T(8,128)(2,1)}) custom-call(s32[86]{0:T(128)} %concatenate.3.s_ref, f32[10,128,128]{2,1,0:T(8,128)} %add.88.refs_0_, f32[10,128,128]{2,1,0:T(8,128)} %collective-permute-done.5.refs_1_, ...), custom_call_target="tpu_custom_call" | custom-call | flops 20000000000 | bytes 8847360 | tf_op jit(solution)/shard_map/pallas_call | solution.py:43
  241.2 10.2 %collective-permute-done.9.x2 = f32[9,128,128]{2,1,0:T(8,128)S(1)} collective-permute-done((f32[9,128,128]{2,1,0:T(8,128)}, f32[9,128,128]{2,1,0:T(8,128)S(1)}, u32[]{:S(2)}, u32[]{:S(2)}) %collective-permute-start.9) | collective-permute-done | bytes 589856 | tf_op jit(solution)/shard_map/ppermute | solution.py:646
  252.3 9.1 %shard_map.157.p_ref = f32[384,768]{1,0:T(8,128)} custom-call(s32[86]{0:T(128)} %concatenate.3.s_ref, f32[384,2304]{1,0:T(8,128)} %bitcast.28, f32[18,128,128]{2,1,0:T(8,128)} %get-tuple-element.97.xk, f32[18,128,128]{2,1,0:T(8,128)} %copy-done.8, f32[9,128,128]{2,1,0:T(8,128)} %copy-done.17, f32[18,128,128]{2,1,0:T(8,128)} %get-tuple-element.99.zk, ...), custom_call_target="tpu_custom_call" | custom-call | flops 2000000000 | bytes 16121856 | tf_op jit(solution)/shard_map/pallas_call | solution.py:43
  271.0 22.0 %collective-permute-done.17.pz = f32[384,768]{1,0:T(8,128)S(1)} collective-permute-done((f32[384,768]{1,0:T(8,128)}, f32[384,768]{1,0:T(8,128)S(1)}, u32[]{:S(2)}, u32[]{:S(2)}) %collective-permute-start.17) | collective-permute-done | bytes 1179680 | tf_op jit(solution)/shard_map/ppermute | solution.py:646
  299.5 15.3 %collective-permute-done.13.x2 = f32[16,128,128]{2,1,0:T(8,128)S(1)} collective-permute-done((f32[16,128,128]{2,1,0:T(8,128)S(1)}, f32[16,128,128]{2,1,0:T(8,128)S(1)}, u32[]{:S(2)}, u32[]{:S(2)}) %collective-permute-start.13) | collective-permute-done | bytes 1048608 | tf_op jit(solution)/shard_map/ppermute | solution.py:646
  316.8 8.6 %shard_map.159.b_ref = f32[384,1536]{1,0:T(8,128)} custom-call(s32[86]{0:T(128)} %concatenate.3.s_ref, f32[384,2304]{1,0:T(8,128)} %bitcast.29, f32[384,768]{1,0:T(8,128)} %shard_map.157.p_ref, f32[23,128,128]{2,1,0:T(8,128)} %get-tuple-element.105.xk, f32[23,128,128]{2,1,0:T(8,128)} %collective-permute-done.12.x1, f32[16,128,128]{2,1,0:T(8,128)} %copy-done.12, ...), custom_call_target="tpu_custom_call" | custom-call | flops 1000000000 | bytes 15532032 | tf_op jit(solution)/shard_map/pallas_call | solution.py:43
  325.4 6.9 %shard_map.160.b_ref = f32[384,1536]{1,0:T(8,128)} custom-call(s32[86]{0:T(128)} %concatenate.3.s_ref, f32[384,1536]{1,0:T(8,128)} %shard_map.159.b_ref, f32[384,768]{1,0:T(8,128)} %shard_map.157.p_ref, f32[384,768]{1,0:T(8,128)} %copy-done.9, f32[384,768]{1,0:T(8,128)} %copy-done.10), custom_call_target="tpu_custom_call" | custom-call | flops 2000000000 | bytes 8257536 | tf_op jit(solution)/shard_map/pallas_call | solution.py:43
  333.9 4.5 %shard_map.161 = f32[384,1536]{1,0:T(8,128)} custom-call(s32[86]{0:T(128)} %concatenate.3.s_ref, f32[384,1536]{1,0:T(8,128)} %shard_map.160.b_ref, f32[384,768]{1,0:T(8,128)} %shard_map.157.p_ref, f32[192,768]{1,0:T(8,128)} %copy-done.15, f32[192,768]{1,0:T(8,128)} %copy-done.16), custom_call_target="tpu_custom_call", output_to_operand_aliasing={{}: (1, {})} | custom-call | flops 1000000000 | bytes 7077888 | tf_op jit(solution)/shard_map/pallas_call | solution.py:43
  (96 shorter events, 58.7 us)
Async XLA Ops:
  0.6 12.1 %copy-start = (s32[8,8,12,6]{2,1,3,0:T(8,128)S(1)}, s32[8,8,12,6]{2,1,3,0:T(8,128)}, u32[]{:S(2)}) copy-start(s32[8,8,12,6]{2,1,3,0:T(8,128)} %param.18) | copy-start | bytes 55300
  6.2 20.4 %collective-permute-start = (f32[11,128,128]{2,1,0:T(8,128)}, f32[11,128,128]{2,1,0:T(8,128)S(1)}, u32[]{:S(2)}, u32[]{:S(2)}) collective-permute-start(f32[11,128,128]{2,1,0:T(8,128)} %shard_map.146.refs_0_), channel_id=1, source_target_pairs={{0,64},{8,72},{16,80},{24,88},{32,96},{40,104},{48,112},{56,120},{... | collective-permute-start | bytes 2162696 | tf_op jit(solution)/shard_map/ppermute | solution.py:646
  26.6 19.5 %collective-permute-start.1 = (f32[10,128,128]{2,1,0:T(8,128)}, f32[10,128,128]{2,1,0:T(8,128)S(1)}, u32[]{:S(2)}, u32[]{:S(2)}) collective-permute-start(f32[10,128,128]{2,1,0:T(8,128)} %get-tuple-element.66.refs_0_), channel_id=1, source_target_pairs={{0,64},{8,72},{16,80},{24,88},{32,96},{40,104},{48,112},{56,120},{... | collective-permute-start | bytes 1966088 | tf_op jit(solution)/shard_map/ppermute | solution.py:646
  46.2 25.5 %collective-permute-start.2 = (f32[16,128,128]{2,1,0:T(8,128)S(1)}, f32[16,128,128]{2,1,0:T(8,128)S(1)}, u32[]{:S(2)}, u32[]{:S(2)}) collective-permute-start(f32[16,128,128]{2,1,0:T(8,128)S(1)} %copy-done.18), channel_id=1, source_target_pairs={{0,64},{8,72},{16,80},{24,88},{32,96},{40,104},{48,112},{56,120},{... | collective-permute-start | bytes 3145736 | tf_op jit(solution)/shard_map/ppermute | solution.py:646
  83.8 25.3 %collective-permute-start.3 = (f32[768,384]{1,0:T(8,128)}, f32[768,384]{1,0:T(8,128)S(1)}, u32[]{:S(2)}, u32[]{:S(2)}) collective-permute-start(f32[768,384]{1,0:T(8,128)} %get-tuple-element.88), channel_id=1, source_target_pairs={{0,64},{8,72},{16,80},{24,88},{32,96},{40,104},{48,112},{56,120},{... | collective-permute-start | bytes 3538952 | tf_op jit(solution)/shard_map/ppermute | solution.py:646
  122.3 20.0 %copy-start.14 = (f32[11,128,128]{2,1,0:T(8,128)S(1)}, f32[11,128,128]{2,1,0:T(8,128)}, u32[]{:S(2)}) copy-start(f32[11,128,128]{2,1,0:T(8,128)} %get-tuple-element.93) | copy-start | bytes 2162692
  135.1 68.0 %collective-permute-start.8 = (f32[18,128,128]{2,1,0:T(8,128)}, f32[18,128,128]{2,1,0:T(8,128)S(1)}, u32[]{:S(2)}, u32[]{:S(2)}) collective-permute-start(f32[18,128,128]{2,1,0:T(8,128)} %get-tuple-element.98), channel_id=1, source_target_pairs={{0,4},{1,5},{2,6},{3,7},{4,0},{5,1},{6,2},{7,3},{8,12},{9,13},{10,... | collective-permute-start | bytes 3538952 | tf_op jit(solution)/shard_map/ppermute | solution.py:646
  140.4 67.6 %collective-permute-start.10 = (f32[18,128,128]{2,1,0:T(8,128)}, f32[18,128,128]{2,1,0:T(8,128)}, u32[]{:S(2)}, u32[]{:S(2)}) collective-permute-start(f32[18,128,128]{2,1,0:T(8,128)} %get-tuple-element.100), channel_id=1, source_target_pairs={{0,64},{8,72},{16,80},{24,88},{32,96},{40,104},{48,112},{56,120},{... | collective-permute-start | bytes 3538952 | tf_op jit(solution)/shard_map/ppermute | solution.py:646
  142.3 39.9 %collective-permute-start.6 = (f32[11,128,128]{2,1,0:T(8,128)S(1)}, f32[11,128,128]{2,1,0:T(8,128)S(1)}, u32[]{:S(2)}, u32[]{:S(2)}) collective-permute-start(f32[11,128,128]{2,1,0:T(8,128)S(1)} %copy-done.14), channel_id=1, source_target_pairs={{0,64},{8,72},{16,80},{24,88},{32,96},{40,104},{48,112},{56,120},{... | collective-permute-start | bytes 2162696 | tf_op jit(solution)/shard_map/ppermute | solution.py:646
  143.9 38.7 %collective-permute-start.4 = (f32[10,128,128]{2,1,0:T(8,128)}, f32[10,128,128]{2,1,0:T(8,128)S(1)}, u32[]{:S(2)}, u32[]{:S(2)}) collective-permute-start(f32[10,128,128]{2,1,0:T(8,128)} %get-tuple-element.92), channel_id=1, source_target_pairs={{0,4},{1,5},{2,6},{3,7},{4,0},{5,1},{6,2},{7,3},{8,12},{9,13},{10,... | collective-permute-start | bytes 1966088 | tf_op jit(solution)/shard_map/ppermute | solution.py:646
  182.2 18.4 %copy-start.13 = (f32[11,128,128]{2,1,0:T(8,128)}, f32[11,128,128]{2,1,0:T(8,128)S(1)}, u32[]{:S(2)}) copy-start(f32[11,128,128]{2,1,0:T(8,128)S(1)} %add.89.refs_2_) | copy-start | bytes 2162692
  182.3 29.6 %collective-permute-start.7 = (f32[11,128,128]{2,1,0:T(8,128)S(1)}, f32[11,128,128]{2,1,0:T(8,128)}, u32[]{:S(2)}, u32[]{:S(2)}) collective-permute-start(f32[11,128,128]{2,1,0:T(8,128)S(1)} %add.89.refs_2_), channel_id=1, source_target_pairs={{0,4},{1,5},{2,6},{3,7},{4,0},{5,1},{6,2},{7,3},{8,12},{9,13},{10,... | collective-permute-start | bytes 2162696 | tf_op jit(solution)/shard_map/ppermute | solution.py:646
  184.6 21.4 %copy-start.6 = (f32[18,128,128]{2,1,0:T(8,128)S(1)}, f32[18,128,128]{2,1,0:T(8,128)}, u32[]{:S(2)}) copy-start(f32[18,128,128]{2,1,0:T(8,128)} %get-tuple-element.97.xk) | copy-start | bytes 3538948
  184.6 26.1 %collective-permute-start.5 = (f32[10,128,128]{2,1,0:T(8,128)}, f32[10,128,128]{2,1,0:T(8,128)}, u32[]{:S(2)}, u32[]{:S(2)}) collective-permute-start(f32[10,128,128]{2,1,0:T(8,128)} %add.88.refs_0_), channel_id=1, source_target_pairs={{0,64},{8,72},{16,80},{24,88},{32,96},{40,104},{48,112},{56,120},{... | collective-permute-start | bytes 1966088 | tf_op jit(solution)/shard_map/ppermute | solution.py:646
  200.6 67.5 %collective-permute-start.12 = (f32[23,128,128]{2,1,0:T(8,128)}, f32[23,128,128]{2,1,0:T(8,128)}, u32[]{:S(2)}, u32[]{:S(2)}) collective-permute-start(f32[23,128,128]{2,1,0:T(8,128)} %get-tuple-element.106), channel_id=1, source_target_pairs={{0,4},{1,5},{2,6},{3,7},{4,0},{5,1},{6,2},{7,3},{8,12},{9,13},{10,... | collective-permute-start | bytes 4521992 | tf_op jit(solution)/shard_map/ppermute | solution.py:646
  204.1 59.7 %collective-permute-start.14 = (f32[25,128,128]{2,1,0:T(8,128)}, f32[25,128,128]{2,1,0:T(8,128)S(1)}, u32[]{:S(2)}, u32[]{:S(2)}) collective-permute-start(f32[25,128,128]{2,1,0:T(8,128)} %get-tuple-element.108), channel_id=1, source_target_pairs={{0,64},{8,72},{16,80},{24,88},{32,96},{40,104},{48,112},{56,120},{... | collective-permute-start | bytes 4915208 | tf_op jit(solution)/shard_map/ppermute | solution.py:646
  208.0 43.4 %collective-permute-start.9 = (f32[9,128,128]{2,1,0:T(8,128)}, f32[9,128,128]{2,1,0:T(8,128)S(1)}, u32[]{:S(2)}, u32[]{:S(2)}) collective-permute-start(f32[9,128,128]{2,1,0:T(8,128)} %slice_add_fusion.3), channel_id=1, source_target_pairs={{0,64},{8,72},{16,80},{24,88},{32,96},{40,104},{48,112},{56,120},{... | collective-permute-start | bytes 1769480 | tf_op jit(solution)/shard_map/ppermute | solution.py:646
  210.7 40.7 %collective-permute-start.11 = (f32[9,128,128]{2,1,0:T(8,128)S(1)}, f32[9,128,128]{2,1,0:T(8,128)}, u32[]{:S(2)}, u32[]{:S(2)}) collective-permute-start(f32[9,128,128]{2,1,0:T(8,128)S(1)} %slice_add_fusion.2), channel_id=1, source_target_pairs={{0,4},{1,5},{2,6},{3,7},{4,0},{5,1},{6,2},{7,3},{8,12},{9,13},{10,... | collective-permute-start | bytes 1769480 | tf_op jit(solution)/shard_map/ppermute | solution.py:646
  261.3 34.2 %collective-permute-start.16 = (f32[384,768]{1,0:T(8,128)}, f32[384,768]{1,0:T(8,128)S(1)}, u32[]{:S(2)}, u32[]{:S(2)}) collective-permute-start(f32[384,768]{1,0:T(8,128)} %shard_map.157.p_ref), channel_id=1, source_target_pairs={{0,4},{1,5},{2,6},{3,7},{4,0},{5,1},{6,2},{7,3},{8,12},{9,13},{10,... | collective-permute-start | bytes 3538952 | tf_op jit(solution)/shard_map/ppermute | solution.py:646
  262.5 30.6 %collective-permute-start.17 = (f32[384,768]{1,0:T(8,128)}, f32[384,768]{1,0:T(8,128)S(1)}, u32[]{:S(2)}, u32[]{:S(2)}) collective-permute-start(f32[384,768]{1,0:T(8,128)} %shard_map.157.p_ref), channel_id=1, source_target_pairs={{0,64},{8,72},{16,80},{24,88},{32,96},{40,104},{48,112},{56,120},{... | collective-permute-start | bytes 3538952 | tf_op jit(solution)/shard_map/ppermute | solution.py:646
  264.9 50.3 %collective-permute-start.15 = (f32[17,128,128]{2,1,0:T(8,128)S(1)}, f32[17,128,128]{2,1,0:T(8,128)S(1)}, u32[]{:S(2)}, u32[]{:S(2)}) collective-permute-start(f32[17,128,128]{2,1,0:T(8,128)S(1)} %slice_add_fusion), channel_id=1, source_target_pairs={{0,4},{1,5},{2,6},{3,7},{4,0},{5,1},{6,2},{7,3},{8,12},{9,13},{10,... | collective-permute-start | bytes 3342344 | tf_op jit(solution)/shard_map/ppermute | solution.py:646
  269.5 45.3 %collective-permute-start.13 = (f32[16,128,128]{2,1,0:T(8,128)S(1)}, f32[16,128,128]{2,1,0:T(8,128)S(1)}, u32[]{:S(2)}, u32[]{:S(2)}) collective-permute-start(f32[16,128,128]{2,1,0:T(8,128)S(1)} %slice_add_fusion.1), channel_id=1, source_target_pairs={{0,64},{8,72},{16,80},{24,88},{32,96},{40,104},{48,112},{56,120},{... | collective-permute-start | bytes 3145736 | tf_op jit(solution)/shard_map/ppermute | solution.py:646
  293.1 39.1 %collective-permute-start.18 = (f32[192,768]{1,0:T(8,128)S(1)}, f32[192,768]{1,0:T(8,128)S(1)}, u32[]{:S(2)}, u32[]{:S(2)}) collective-permute-start(f32[192,768]{1,0:T(8,128)S(1)} %slice.44), channel_id=1, source_target_pairs={{0,4},{1,5},{2,6},{3,7},{4,0},{5,1},{6,2},{7,3},{8,12},{9,13},{10,... | collective-permute-start | bytes 1769480 | tf_op jit(solution)/shard_map/ppermute | solution.py:646
  297.5 34.8 %collective-permute-start.19 = (f32[192,768]{1,0:T(8,128)}, f32[192,768]{1,0:T(8,128)S(1)}, u32[]{:S(2)}, u32[]{:S(2)}) collective-permute-start(f32[192,768]{1,0:T(8,128)} %slice.45), channel_id=1, source_target_pairs={{0,64},{8,72},{16,80},{24,88},{32,96},{40,104},{48,112},{56,120},{... | collective-permute-start | bytes 1769480 | tf_op jit(solution)/shard_map/ppermute | solution.py:646
  (18 other events, 53.9 us)
